TPU v7x, 256 devices: a whole 4x4x8 slice. The times are simulated.
256 devices in a mesh: samp: 16 (over z_hi, x, core), gene: 4 (over z_lo), snp: 4 (over y).
Axes of the slice: x: 4, y: 4, z: 8 (z_hi: 2, z_lo: 4; z = z_hi * 4 + z_lo), core: 2. Of those that a mesh axis runs over, the one named last changes fastest.
Arguments:
- expression: bfloat16 [4096, 16384], P('samp', ('gene', 'snp')), may hold values from -6 to 6
- loadings: bfloat16 [16384, 128], P(('gene', 'snp')), may hold values from -0.046875 to 0.046875
- dosage: bfloat16 [4096, 16384], P(None, ('gene', 'snp')), may hold values from 0 to 2
Outputs:
- assoc: bfloat16 [16, 16, 64, 16384], P(None, 'samp', None, ('gene', 'snp'))
All inputs are finite; a program needn't handle non-finite values.
Results may differ from a plain program's by a relative error of at most 0.0065.
Values may be sent and summed in bfloat16 or wider, within the bound.
No kernel may reach another device: no remote copies, remote signals or barrier semaphores. Data moves between devices by JAX's collectives and lax.ppermute only.
A program may use at most 64 MiB of HBM per device.

v0:
```python
import functools

import jax
import jax.numpy as jnp
from jax import lax
from jax.experimental import pallas as pl
from jax.experimental.pallas import tpu as pltpu
from jax.sharding import Mesh, PartitionSpec as P

ridge_factor = 1.0
ridge_sample = 1.0
SAMP = ("zh", "x", "core")
COLS = ("zl", "y")
CHUNKS = 2
F32 = jnp.float32
BF16 = jnp.bfloat16
HI = lax.Precision.HIGHEST
NT = (((1,), (1,)), ((), ()))
TN = (((0,), (0,)), ((), ()))


def cycle(array, axis, by):
    size = lax.axis_size(axis)
    return lax.ppermute(array, axis, [(i, (i + by) % size) for i in range(size)])


def invert2(a, b, c):
    r = 1.0 / (a * c - b * b)
    return c * r, -b * r, a * r


def sweep(a_ref):
    n = a_ref.shape[0]
    ci = lax.broadcasted_iota(jnp.int32, (n, n), 1)
    lane = ci[:1]

    def step(t, _):
        k = 4 * t
        a = a_ref[...]
        r = [a_ref[pl.ds(k + i, 1), :] for i in range(4)]
        c = [jnp.sum(jnp.where(ci == k + i, a, 0.0), axis=1, keepdims=True) for i in range(4)]
        b = [[None] * i + [jnp.sum(jnp.where(lane == k + j, r[i], 0.0), axis=1, keepdims=True) for j in range(i, 4)] for i in range(4)]
        s11, s12, s22 = invert2(b[0][0], b[0][1], b[1][1])
        q11, q12, q21, q22 = b[0][2], b[0][3], b[1][2], b[1][3]
        w11, w12 = s11 * q11 + s12 * q21, s11 * q12 + s12 * q22
        w21, w22 = s12 * q11 + s22 * q21, s12 * q12 + s22 * q22
        t11, t12, t22 = invert2(
            b[2][2] - (q11 * w11 + q21 * w21), b[2][3] - (q11 * w12 + q21 * w22), b[3][3] - (q12 * w12 + q22 * w22)
        )
        m11, m12 = -(w11 * t11 + w12 * t12), -(w11 * t12 + w12 * t22)
        m21, m22 = -(w21 * t11 + w22 * t12), -(w21 * t12 + w22 * t22)
        l11, l12 = s11 - (m11 * w11 + m12 * w12), s12 - (m11 * w21 + m12 * w22)
        l22 = s22 - (m21 * w21 + m22 * w22)
        inv = [[l11, l12, m11, m12], [l12, l22, m21, m22], [m11, m21, t11, t12], [m12, m22, t12, t22]]
        p = [(inv[i][0] * r[0] + inv[i][1] * r[1]) + (inv[i][2] * r[2] + inv[i][3] * r[3]) for i in range(4)]
        new = a - ((c[0] * p[0] + c[1] * p[1]) + (c[2] * p[2] + c[3] * p[3]))
        for i in range(4):
            q = (inv[i][0] * c[0] + inv[i][1] * c[1]) + (inv[i][2] * c[2] + inv[i][3] * c[3])
            new = jnp.where(ci == k + i, q, new)
        a_ref[...] = new
        for i in range(4):
            for j in range(4):
                p[i] = jnp.where(lane == k + j, -inv[i][j], p[i])
            a_ref[pl.ds(k + i, 1), :] = p[i]
        return 0

    lax.fori_loop(0, n // 4, step, 0)


def eye(n):
    ri = lax.broadcasted_iota(jnp.int32, (n, n), 0)
    return jnp.where(ri == lax.broadcasted_iota(jnp.int32, (n, n), 1), 1.0, 0.0).astype(F32)


def factor_kernel(sums_ref, out_ref, mat):
    k = sums_ref.shape[0]
    mat[...] = sums_ref[:, -k:] + ridge_factor * eye(k)
    sweep(mat)
    found = jnp.dot(-mat[...], sums_ref[:, :-k], preferred_element_type=F32, precision=HI)
    out_ref[...] = found.astype(BF16)


def hess_kernel(places, near, other, dos_hbm, fac, inverse, proj, mat, dos, sem):
    k = mat.shape[0]
    width = near.shape[2]
    fetch = pltpu.make_async_copy(dos_hbm, dos, sem)
    fetch.start()
    for i in range(8):
        fac[:, pl.ds(pl.multiple_of(places[i] * width, width), width)] = near[i]
        fac[:, pl.ds(pl.multiple_of(places[8 + i] * width, width), width)] = other[i]
    mat[...] = lax.dot_general(fac[...], fac[...], NT, preferred_element_type=F32) + ridge_sample * eye(k)
    sweep(mat)
    inverse[...] = -mat[...]
    fetch.wait()
    total = jnp.dot(fac[...], dos[...], preferred_element_type=F32)
    high = total.astype(BF16)
    proj[:k, :] = high
    proj[k:, :] = (total - high.astype(F32)).astype(BF16)


def finish_kernel(scale, start, genes, count, places, *refs):
    pieces, scores = refs[:count], refs[count : 2 * count]
    fac, inverse, proj = refs[2 * count : 2 * count + 3]
    out, done, sems = refs[-3:]
    cross = [lax.dot_general(piece[...], fac[...], NT, preferred_element_type=F32) for piece in pieces]
    cross = jnp.concatenate(cross)
    half = jnp.dot(cross, inverse[...], preferred_element_type=F32, precision=HI).astype(BF16)
    coef = jnp.concatenate([half, half], axis=1)
    at, copies = 0, []
    for score in scores:
        rows = score.shape[0]
        total = score[...] - jnp.dot(coef[at : at + rows], proj[...], preferred_element_type=F32)
        done[pl.ds(at, rows), :] = (total * scale).astype(BF16)
        for i in range(at // genes, (at + rows) // genes):
            copy = pltpu.make_async_copy(
                done.at[pl.ds(i * genes, genes), :], out.at[places[i], 0, pl.ds(start, genes), :], sems.at[i]
            )
            copy.start()
            copies.append(copy)
        at += rows
    for copy in copies:
        copy.wait()


def finish(places, pieces, scores, fac, inverse, proj, out, start, genes, panel, samples):
    snps = scores[0].shape[1]
    rows = sum(p.shape[0] for p in pieces)
    ins = list(pieces) + list(scores) + [fac, inverse, proj]
    specs = [pl.BlockSpec(a.shape, lambda n, _, nd=a.ndim: (0,) * nd) for a in ins]
    alias = {}
    if out is not None:
        alias = {len(ins) + 1: 0}
        ins.append(out)
        specs.append(pl.BlockSpec(memory_space=pl.ANY))
    return pl.pallas_call(
        functools.partial(finish_kernel, float(samples) ** -0.5, start, genes, len(pieces)),
        out_shape=jax.ShapeDtypeStruct((16, 1, panel, snps), BF16),
        grid_spec=pltpu.PrefetchScalarGridSpec(
            num_scalar_prefetch=1,
            grid=(1,),
            in_specs=specs,
            out_specs=pl.BlockSpec(memory_space=pl.ANY),
            scratch_shapes=[pltpu.VMEM((rows, snps), BF16), pltpu.SemaphoreType.DMA((rows // genes,))],
        ),
        input_output_aliases=alias,
        cost_estimate=pl.CostEstimate(flops=2 * rows * samples * 256, bytes_accessed=rows * 16384, transcendentals=0),
        compiler_params=pltpu.CompilerParams(vmem_limit_bytes=30 << 20),
    )(places, *ins)


def body(expression, loadings, dosage):
    samples, genes = expression.shape
    k = loadings.shape[1]
    n_samp, n_cols = lax.axis_size(SAMP), lax.axis_size(COLS)
    panel = genes // n_samp
    all_samples, snps = dosage.shape
    at = {name: lax.axis_index(name) for name in SAMP + COLS}

    flipped = expression.T
    mine = lax.all_to_all(flipped.reshape(n_samp, panel, samples), SAMP, 0, 0, tiled=True)
    mine = mine.transpose(1, 0, 2).reshape(panel, all_samples)

    both = jnp.concatenate(
        [
            lax.dot_general(loadings, flipped, TN, preferred_element_type=F32),
            lax.dot_general(loadings, loadings, TN, preferred_element_type=F32),
        ],
        axis=1,
    )
    both = lax.all_to_all(both.reshape(n_cols, k // n_cols, samples + k), COLS, 0, 0, tiled=True)
    both = both.sum(axis=0)
    both = lax.all_to_all(jnp.broadcast_to(both[None], (n_cols,) + both.shape), COLS, 0, 0, tiled=True)
    factors = pl.pallas_call(
        factor_kernel,
        out_shape=jax.ShapeDtypeStruct((k, samples), BF16),
        scratch_shapes=[pltpu.VMEM((k, k), F32)],
        cost_estimate=pl.CostEstimate(flops=7_000_000_000, bytes_accessed=400_000, transcendentals=0),
        name="factor",
    )(both.reshape(k, samples + k))

    width = panel // CHUNKS
    groups = []
    for c in range(CHUNKS):
        piece = mine[c * width : c * width + width]
        own = jnp.concatenate([piece] + [cycle(piece, "zl", by) for by in (1, 2, 3)])
        ahead, behind = cycle(own, "y", 1), cycle(own, "y", -1)
        low, high = cycle(ahead[: 2 * width], "y", 1), cycle(behind[2 * width :], "y", -1)
        near_slots, far_slots = [(0, 4), (4, 8), (12, 16)], [(8, 10), (10, 12)]
        if c < CHUNKS - 1:
            groups.append((c * width, near_slots + far_slots, [own, ahead, behind, low, high]))
        else:
            groups.append((c * width, near_slots, [own, ahead, behind]))
            groups.append((c * width, far_slots, [low, high]))
    scores = [[jnp.dot(rows, dosage, preferred_element_type=F32) for rows in pieces] for _, _, pieces in groups]

    two = jnp.stack([factors, cycle(factors, "zh", 1)])
    near = jnp.concatenate([two] + [cycle(two, "x", by) for by in (1, 2, 3)])
    other = cycle(near, "core", 1)
    back = jnp.arange(16)
    from_core = (at["core"] - back // 8) % 2
    from_x = (at["x"] - back // 2 % 4) % 4
    from_zh = (at["zh"] - back % 2) % 2
    order = (from_zh * 8 + from_x * 2 + from_core).astype(jnp.int32)
    fac, inverse, proj = pl.pallas_call(
        hess_kernel,
        out_shape=(
            jax.ShapeDtypeStruct((k, all_samples), BF16),
            jax.ShapeDtypeStruct((k, k), F32),
            jax.ShapeDtypeStruct((2 * k, snps), BF16),
        ),
        in_specs=[
            pl.BlockSpec(memory_space=pltpu.SMEM),
            pl.BlockSpec(memory_space=pltpu.VMEM),
            pl.BlockSpec(memory_space=pltpu.VMEM),
            pl.BlockSpec(memory_space=pl.ANY),
        ],
        scratch_shapes=[
            pltpu.VMEM((k, k), F32),
            pltpu.VMEM(dosage.shape, BF16),
            pltpu.SemaphoreType.DMA,
        ],
        cost_estimate=pl.CostEstimate(flops=9_000_000_000, bytes_accessed=10_000_000, transcendentals=0),
        compiler_params=pltpu.CompilerParams(vmem_limit_bytes=24 << 20),
        name="hess",
    )(order, near, other, dosage)

    back_z = (at["zl"] - jnp.arange(4)) % 4
    back_y = (at["y"] - jnp.arange(4)) % 4
    places = (back_z[None, :] * 4 + back_y[:, None]).astype(jnp.int32).reshape(16)
    out = None
    for (start, slots, pieces), score in zip(groups, scores):
        where = jnp.concatenate([places[a:b] for a, b in slots])
        out = finish(where, pieces, score, fac, inverse, proj, out, start, width, panel, all_samples)
    return out


def solution(mesh):
    fine = Mesh(mesh.devices.reshape(2, 4, 2, 4, 4), SAMP + COLS)
    placed = (P(SAMP, COLS), P(COLS, None), P(None, COLS))
    return jax.shard_map(body, mesh=fine, in_specs=placed, out_specs=P(None, SAMP, None, COLS), check_vma=False)
```

profile of v0, /device:TPU:64, one launch (start us, length us, event | category | flops | bytes accessed | tf_op | source)
XLA Modules:
  0.0 197.0 jit_solution(6699590486274105301)
XLA Ops:
  0.0 0.9 copy-done
  1.0 0.3 fusion.17
  1.2 1.4 fusion.16
  2.6 0.7 maximum_bitcast_fusion
  3.3 8.2 %all-to-all-start.1 = ((f32[16,8,384]{2,1,0:T(8,128)}), f32[16,8,384]{2,1,0:T(8,128)S(1)}, u32[]{:S(2)}, u32[]{:S(2)}) async-start(f32[16,8,384]{2,1,0:T(8,128)} %maximum_bitcast_fusion), calls=%async_computation.1 | async-start | bytes 393216 | tf_op jit(solution)/shard_map/all_to_all | solution.py:170
  11.5 0.1 broadcast_add_fusion
  11.6 7.4 %all-to-all-done.1 = f32[16,8,384]{2,1,0:T(8,128)S(1)} async-done(((f32[16,8,384]{2,1,0:T(8,128)}), f32[16,8,384]{2,1,0:T(8,128)S(1)}, u32[]{:S(2)}, u32[]{:S(2)}) %all-to-all-start.1) | async-done | bytes 196640 | tf_op jit(solution)/shard_map/all_to_all | solution.py:170
  19.0 0.7 broadcast_in_dim.2
  19.7 5.6 %all-to-all-start.2 = ((f32[16,8,384]{2,1,0:T(8,128)}), f32[16,8,384]{2,1,0:T(8,128)S(1)}, u32[]{:S(2)}, u32[]{:S(2)}) async-start(f32[16,8,384]{2,1,0:T(8,128)} %broadcast_in_dim.2), calls=%async_computation.2 | async-start | bytes 393216 | tf_op jit(solution)/shard_map/all_to_all | solution.py:172
  25.3 2.0 %copy.8 = bf16[256,1024]{0,1:T(8,128)(2,1)} copy(bf16[256,1024]{1,0:T(8,128)(2,1)} %param.3) | data formatting | bytes 1048576 | tf_op args[0]
  27.3 0.1 pad_add_fusion.places
  27.4 0.1 pad_add_fusion.1.places
  27.5 5.0 %all-to-all-done.2 = f32[16,8,384]{2,1,0:T(8,128)S(1)} async-done(((f32[16,8,384]{2,1,0:T(8,128)}), f32[16,8,384]{2,1,0:T(8,128)S(1)}, u32[]{:S(2)}, u32[]{:S(2)}) %all-to-all-start.2) | async-done | bytes 196640 | tf_op jit(solution)/shard_map/all_to_all | solution.py:172
  32.5 8.3 %all-to-all-start = ((bf16[16,64,256]{2,1,0:T(8,128)(2,1)}), bf16[16,64,256]{2,1,0:T(8,128)(2,1)S(1)}, u32[]{:S(2)}, u32[]{:S(2)}) async-start(bf16[16,64,256]{2,1,0:T(8,128)(2,1)} %bitcast.2), calls=%async_computation | async-start | bytes 1048576 | tf_op jit(solution)/shard_map/all_to_all | solution.py:160
  40.9 8.9 %factor.1 = bf16[128,256]{1,0:T(8,128)(2,1)} custom-call(f32[128,384]{1,0:T(8,128)} %bitcast.62), custom_call_target="tpu_custom_call" | custom-call | flops 7000000000 | bytes 400000 | tf_op jit(solution)/shard_map/factor/pallas_call | solution.py:173
  49.8 5.8 %collective-permute-start.7 = (bf16[128,256]{1,0:T(8,128)(2,1)}, bf16[128,256]{1,0:T(8,128)(2,1)S(1)}, u32[]{:S(2)}, u32[]{:S(2)}) collective-permute-start(bf16[128,256]{1,0:T(8,128)(2,1)} %factor.1), channel_id=1, source_target_pairs={{0,128},{128,0},{1,129},{129,1},{2,130},{130,2},{3,131},{131,3},{4... | collective-permute-start | bytes 196616 | tf_op jit(solution)/shard_map/ppermute | solution.py:24
  55.7 0.9 constant_dynamic-update-slice_fusion.8
  56.6 5.4 %collective-permute-done.7 = bf16[128,256]{1,0:T(8,128)(2,1)S(1)} collective-permute-done((bf16[128,256]{1,0:T(8,128)(2,1)}, bf16[128,256]{1,0:T(8,128)(2,1)S(1)}, u32[]{:S(2)}, u32[]{:S(2)}) %collective-permute-start.7) | collective-permute-done | bytes 65568 | tf_op jit(solution)/shard_map/ppermute | solution.py:24
  61.9 0.9 pad_maximum_fusion
  62.8 1.5 collective-permute-start.8
  64.3 2.7 %collective-permute-start.9 = (bf16[2,128,256]{2,1,0:T(8,128)(2,1)S(1)}, bf16[2,128,256]{2,1,0:T(8,128)(2,1)S(1)}, u32[]{:S(2)}, u32[]{:S(2)}) collective-permute-start(bf16[2,128,256]{2,1,0:T(8,128)(2,1)S(1)} %pad_maximum_fusion), channel_id=1, source_target_pairs={{0,64},{32,96},{64,0},{96,32},{1,65},{33,97},{65,1},{97,33},{2,66}... | collective-permute-start | bytes 393224 | tf_op jit(solution)/shard_map/ppermute | solution.py:24
  67.0 1.5 collective-permute-start.10
  68.5 1.1 collective-permute-done.8
  69.6 3.1 %collective-permute-done.9 = bf16[2,128,256]{2,1,0:T(8,128)(2,1)S(1)} collective-permute-done((bf16[2,128,256]{2,1,0:T(8,128)(2,1)S(1)}, bf16[2,128,256]{2,1,0:T(8,128)(2,1)S(1)}, u32[]{:S(2)}, u32[]{:S(2)}) %collective-permute-start.9) | collective-permute-done | bytes 131104 | tf_op jit(solution)/shard_map/ppermute | solution.py:24
  72.8 0.1 collective-permute-start.11
  73.0 0.1 collective-permute-start.12
  73.1 2.6 %collective-permute-start.13 = (bf16[32,4096]{1,0:T(8,128)(2,1)S(1)}, bf16[32,4096]{1,0:T(8,128)(2,1)S(1)}, u32[]{:S(2)}, u32[]{:S(2)}) collective-permute-start(bf16[32,4096]{1,0:T(8,128)(2,1)S(1)} %bitcast.58), channel_id=1, source_target_pairs={{0,8},{4,12},{8,0},{12,4},{1,9},{5,13},{9,1},{13,5},{2,10},{6,14},... | collective-permute-start | bytes 786440 | tf_op jit(solution)/shard_map/ppermute | solution.py:24
  75.7 2.1 %collective-permute-start = (bf16[32,4096]{1,0:T(8,128)(2,1)S(1)}, bf16[32,4096]{1,0:T(8,128)(2,1)S(1)}, u32[]{:S(2)}, u32[]{:S(2)}) collective-permute-start(bf16[32,4096]{1,0:T(8,128)(2,1)S(1)} %bitcast.52), channel_id=1, source_target_pairs={{0,4},{4,8},{8,12},{12,0},{1,5},{5,9},{9,13},{13,1},{2,6},{6,10},{... | collective-permute-start | bytes 786440 | tf_op jit(solution)/shard_map/ppermute | solution.py:24
  77.8 4.8 %collective-permute-done.12 = bf16[32,4096]{1,0:T(8,128)(2,1)S(1)} collective-permute-done((bf16[32,4096]{1,0:T(8,128)(2,1)S(1)}, bf16[32,4096]{1,0:T(8,128)(2,1)S(1)}, u32[]{:S(2)}, u32[]{:S(2)}) %collective-permute-start.12) | collective-permute-done | bytes 262176 | tf_op jit(solution)/shard_map/ppermute | solution.py:24
  82.6 0.7 collective-permute-start.1
  83.4 7.5 %collective-permute-done.13 = bf16[32,4096]{1,0:T(8,128)(2,1)S(1)} collective-permute-done((bf16[32,4096]{1,0:T(8,128)(2,1)S(1)}, bf16[32,4096]{1,0:T(8,128)(2,1)S(1)}, u32[]{:S(2)}, u32[]{:S(2)}) %collective-permute-start.13) | collective-permute-done | bytes 262176 | tf_op jit(solution)/shard_map/ppermute | solution.py:24
  90.9 7.6 %collective-permute-start.2 = (bf16[32,4096]{1,0:T(8,128)(2,1)S(1)}, bf16[32,4096]{1,0:T(8,128)(2,1)S(1)}, u32[]{:S(2)}, u32[]{:S(2)}) collective-permute-start(bf16[32,4096]{1,0:T(8,128)(2,1)S(1)} %bitcast.55), channel_id=1, source_target_pairs={{0,12},{4,0},{8,4},{12,8},{1,13},{5,1},{9,5},{13,9},{2,14},{6,2},{... | collective-permute-start | bytes 786440 | tf_op jit(solution)/shard_map/ppermute | solution.py:24
  98.5 9.0 %collective-permute-done.14 = bf16[32,4096]{1,0:T(8,128)(2,1)S(1)} collective-permute-done((bf16[32,4096]{1,0:T(8,128)(2,1)S(1)}, bf16[32,4096]{1,0:T(8,128)(2,1)S(1)}, u32[]{:S(2)}, u32[]{:S(2)}) %collective-permute-start.14) | collective-permute-done | bytes 262176 | tf_op jit(solution)/shard_map/ppermute | solution.py:24
  107.6 0.6 collective-permute-start.15
  108.2 7.8 %collective-permute-done = bf16[32,4096]{1,0:T(8,128)(2,1)S(1)} collective-permute-done((bf16[32,4096]{1,0:T(8,128)(2,1)S(1)}, bf16[32,4096]{1,0:T(8,128)(2,1)S(1)}, u32[]{:S(2)}, u32[]{:S(2)}) %collective-permute-start) | collective-permute-done | bytes 262176 | tf_op jit(solution)/shard_map/ppermute | solution.py:24
  115.9 0.4 collective-permute-start.16
  116.4 2.3 %collective-permute-done.2 = bf16[32,4096]{1,0:T(8,128)(2,1)S(1)} collective-permute-done((bf16[32,4096]{1,0:T(8,128)(2,1)S(1)}, bf16[32,4096]{1,0:T(8,128)(2,1)S(1)}, u32[]{:S(2)}, u32[]{:S(2)}) %collective-permute-start.2) | collective-permute-done | bytes 262176 | tf_op jit(solution)/shard_map/ppermute | solution.py:24
  118.7 0.0 slice-start.1
  118.7 0.6 collective-permute-start.3
  119.4 2.7 %collective-permute-start.5 = (bf16[128,4096]{1,0:T(8,128)(2,1)S(1)}, bf16[128,4096]{1,0:T(8,128)(2,1)S(1)}, u32[]{:S(2)}, u32[]{:S(2)}) collective-permute-start(bf16[128,4096]{1,0:T(8,128)(2,1)S(1)} %constant_dynamic-update-slice_fusion.refs_0_), channel_id=1, source_target_pairs={{0,3},{1,0},{2,1},{3,2},{4,7},{5,4},{6,5},{7,6},{8,11},{9,8},{10,9... | collective-permute-start | bytes 3145736 | tf_op jit(solution)/shard_map/ppermute | solution.py:24
  122.1 4.7 %fusion.21.refs_5_ = f32[128,1024]{1,0:T(8,128)S(1)} fusion(bf16[128,4096]{1,0:T(8,128)(2,1)S(1)} %constant_dynamic-update-slice_fusion.9.refs_0_, bf16[4096,1024]{1,0:T(8,128)(2,1)} %dos_hbm.1), kind=kOutput, calls=%fused_computation.70 | convolution fusion | flops 1073741824 | bytes 9961472 | tf_op jit(solution)/shard_map/dot_general | solution.py:194
  126.8 1.3 fusion.18.refs_3_
  128.1 10.1 %hess.1 = (bf16[128,4096]{1,0:T(8,128)(2,1)S(1)}, f32[128,128]{1,0:T(8,128)S(1)}, bf16[256,1024]{1,0:T(8,128)(2,1)S(1)}) custom-call(s32[16]{0:T(128)S(1)} %fusion.places, bf16[8,128,256]{2,1,0:T(8,128)(2,1)S(1)} %constant_dynamic-update-slice_fusion.4.near, bf16[8,128,256]{2,1,0:T(8,128)(2,1)S(1)} %collective-permute-done.11.other, ...), custom_call_target="tpu_custom_call" | custom-call | flops 8999999488 | bytes 10000000 | tf_op jit(solution)/shard_map/hess/pallas_call | solution.py:204
  138.3 0.1 collective-permute-start.17
  138.4 3.6 %collective-permute-done.16.refs_2_ = bf16[128,4096]{1,0:T(8,128)(2,1)S(1)} collective-permute-done((bf16[128,4096]{1,0:T(8,128)(2,1)S(1)}, bf16[128,4096]{1,0:T(8,128)(2,1)S(1)}, u32[]{:S(2)}, u32[]{:S(2)}) %collective-permute-start.16) | collective-permute-done | bytes 1048608 | tf_op jit(solution)/shard_map/ppermute | solution.py:24
  142.0 1.7 collective-permute-start.18
  143.7 13.7 %collective-permute-done.3.refs_1_ = bf16[128,4096]{1,0:T(8,128)(2,1)S(1)} collective-permute-done((bf16[128,4096]{1,0:T(8,128)(2,1)S(1)}, bf16[128,4096]{1,0:T(8,128)(2,1)S(1)}, u32[]{:S(2)}, u32[]{:S(2)}) %collective-permute-start.3) | collective-permute-done | bytes 1048608 | tf_op jit(solution)/shard_map/ppermute | solution.py:24
  157.4 0.1 collective-permute-start.4
  157.5 7.0 %collective-permute-done.5.refs_2_ = bf16[128,4096]{1,0:T(8,128)(2,1)S(1)} collective-permute-done((bf16[128,4096]{1,0:T(8,128)(2,1)S(1)}, bf16[128,4096]{1,0:T(8,128)(2,1)S(1)}, u32[]{:S(2)}, u32[]{:S(2)}) %collective-permute-start.5) | collective-permute-done | bytes 1048608 | tf_op jit(solution)/shard_map/ppermute | solution.py:24
  164.5 1.9 collective-permute-start.6
  166.4 1.3 fusion.22.refs_6_
  167.7 1.3 fusion.23.refs_7_
  169.0 1.3 fusion.19.refs_4_
  170.3 1.3 fusion.20.refs_5_
  171.6 1.6 fusion.24.refs_8_
  173.2 2.5 %collective-permute-done.18.refs_4_ = bf16[64,4096]{1,0:T(8,128)(2,1)S(1)} collective-permute-done((bf16[64,4096]{1,0:T(8,128)(2,1)S(1)}, bf16[64,4096]{1,0:T(8,128)(2,1)S(1)}, u32[]{:S(2)}, u32[]{:S(2)}) %collective-permute-start.18) | collective-permute-done | bytes 524320 | tf_op jit(solution)/shard_map/ppermute | solution.py:24
  175.7 1.6 fusion.25.refs_9_
  177.3 1.6 collective-permute-done.4.refs_0_
  178.8 1.6 fusion.14.refs_2_
  180.4 4.7 %collective-permute-done.6.refs_1_ = bf16[64,4096]{1,0:T(8,128)(2,1)S(1)} collective-permute-done((bf16[64,4096]{1,0:T(8,128)(2,1)S(1)}, bf16[64,4096]{1,0:T(8,128)(2,1)S(1)}, u32[]{:S(2)}, u32[]{:S(2)}) %collective-permute-start.6) | collective-permute-done | bytes 524320 | tf_op jit(solution)/shard_map/ppermute | solution.py:24
  185.1 1.6 fusion.15.refs_3_
  186.7 4.2 %shard_map.37.refs_9_ = bf16[16,1,64,1024]{3,2,1,0:T(8,128)(2,1)} custom-call(s32[16]{0:T(128)S(1)} %pad_add_fusion.1.places, bf16[128,4096]{1,0:T(8,128)(2,1)S(1)} %constant_dynamic-update-slice_fusion.9.refs_0_, bf16[128,4096]{1,0:T(8,128)(2,1)S(1)} %collective-permute-done.15.refs_1_, bf16[128,4096]{1,0:T(8,128)(2,1)S(1)} %collective-permute-done.16.refs_2_, ...), custom_call_target="tpu_custom_call" | custom-call | flops 1073741824 | bytes 8388608 | tf_op jit(solution)/shard_map/pallas_call | solution.py:135
  190.9 3.4 %shard_map.38.refs_7_ = bf16[16,1,64,1024]{3,2,1,0:T(8,128)(2,1)} custom-call(s32[12]{0:T(128)S(1)} %pad_add_fusion.places, bf16[128,4096]{1,0:T(8,128)(2,1)S(1)} %constant_dynamic-update-slice_fusion.refs_0_, bf16[128,4096]{1,0:T(8,128)(2,1)S(1)} %collective-permute-done.3.refs_1_, ...), custom_call_target="tpu_custom_call", output_to_operand_aliasing={{}: (10, {})} | custom-call | flops 805306368 | bytes 6291456 | tf_op jit(solution)/shard_map/pallas_call | solution.py:135
  194.3 2.6 %shard_map.39 = bf16[16,1,64,1024]{3,2,1,0:T(8,128)(2,1)} custom-call(s32[4]{0:T(128)S(1)} %get-tuple-element.16.places, bf16[64,4096]{1,0:T(8,128)(2,1)S(1)} %collective-permute-done.4.refs_0_, bf16[64,4096]{1,0:T(8,128)(2,1)S(1)} %collective-permute-done.6.refs_1_, f32[64,1024]{1,0:T(8,128)S(1)} %fusion.14.refs_2_, ...), custom_call_target="tpu_custom_call", output_to_operand_aliasing={{}: (8, {})} | custom-call | flops 268435456 | bytes 2097152 | tf_op jit(solution)/shard_map/pallas_call | solution.py:135
  (37 shorter events, 0.5 us)
Async XLA Ops:
  0.0 1.0 copy-start
  3.3 15.7 %all-to-all-start.1 = ((f32[16,8,384]{2,1,0:T(8,128)}), f32[16,8,384]{2,1,0:T(8,128)S(1)}, u32[]{:S(2)}, u32[]{:S(2)}) async-start(f32[16,8,384]{2,1,0:T(8,128)} %maximum_bitcast_fusion), calls=%async_computation.1 | async-start | bytes 393216 | tf_op jit(solution)/shard_map/all_to_all | solution.py:170
  19.7 12.8 %all-to-all-start.2 = ((f32[16,8,384]{2,1,0:T(8,128)}), f32[16,8,384]{2,1,0:T(8,128)S(1)}, u32[]{:S(2)}, u32[]{:S(2)}) async-start(f32[16,8,384]{2,1,0:T(8,128)} %broadcast_in_dim.2), calls=%async_computation.2 | async-start | bytes 393216 | tf_op jit(solution)/shard_map/all_to_all | solution.py:172
  32.5 8.3 %copy-start.1 = (f32[16,8,384]{2,1,0:T(8,128)}, f32[16,8,384]{2,1,0:T(8,128)S(1)}, u32[]{:S(2)}) copy-start(f32[16,8,384]{2,1,0:T(8,128)S(1)} %all-to-all-done.2) | copy-start | bytes 589828
  32.5 40.3 %all-to-all-start = ((bf16[16,64,256]{2,1,0:T(8,128)(2,1)}), bf16[16,64,256]{2,1,0:T(8,128)(2,1)S(1)}, u32[]{:S(2)}, u32[]{:S(2)}) async-start(bf16[16,64,256]{2,1,0:T(8,128)(2,1)} %bitcast.2), calls=%async_computation | async-start | bytes 1048576 | tf_op jit(solution)/shard_map/all_to_all | solution.py:160
  49.8 12.1 %collective-permute-start.7 = (bf16[128,256]{1,0:T(8,128)(2,1)}, bf16[128,256]{1,0:T(8,128)(2,1)S(1)}, u32[]{:S(2)}, u32[]{:S(2)}) collective-permute-start(bf16[128,256]{1,0:T(8,128)(2,1)} %factor.1), channel_id=1, source_target_pairs={{0,128},{128,0},{1,129},{129,1},{2,130},{130,2},{3,131},{131,3},{4... | collective-permute-start | bytes 196616 | tf_op jit(solution)/shard_map/ppermute | solution.py:24
  62.8 6.8 %collective-permute-start.8 = (bf16[2,128,256]{2,1,0:T(8,128)(2,1)S(1)}, bf16[2,128,256]{2,1,0:T(8,128)(2,1)S(1)}, u32[]{:S(2)}, u32[]{:S(2)}) collective-permute-start(bf16[2,128,256]{2,1,0:T(8,128)(2,1)S(1)} %pad_maximum_fusion), channel_id=1, source_target_pairs={{0,32},{32,64},{64,96},{96,0},{1,33},{33,65},{65,97},{97,1},{2,34}... | collective-permute-start | bytes 393224 | tf_op jit(solution)/shard_map/ppermute | solution.py:24
  64.3 8.4 %collective-permute-start.9 = (bf16[2,128,256]{2,1,0:T(8,128)(2,1)S(1)}, bf16[2,128,256]{2,1,0:T(8,128)(2,1)S(1)}, u32[]{:S(2)}, u32[]{:S(2)}) collective-permute-start(bf16[2,128,256]{2,1,0:T(8,128)(2,1)S(1)} %pad_maximum_fusion), channel_id=1, source_target_pairs={{0,64},{32,96},{64,0},{96,32},{1,65},{33,97},{65,1},{97,33},{2,66}... | collective-permute-start | bytes 393224 | tf_op jit(solution)/shard_map/ppermute | solution.py:24
  67.0 5.7 %collective-permute-start.10 = (bf16[2,128,256]{2,1,0:T(8,128)(2,1)S(1)}, bf16[2,128,256]{2,1,0:T(8,128)(2,1)S(1)}, u32[]{:S(2)}, u32[]{:S(2)}) collective-permute-start(bf16[2,128,256]{2,1,0:T(8,128)(2,1)S(1)} %pad_maximum_fusion), channel_id=1, source_target_pairs={{0,96},{32,0},{64,32},{96,64},{1,97},{33,1},{65,33},{97,65},{2,98}... | collective-permute-start | bytes 393224 | tf_op jit(solution)/shard_map/ppermute | solution.py:24
  72.8 55.4 %collective-permute-start.11 = (bf16[8,128,256]{2,1,0:T(8,128)(2,1)S(1)}, bf16[8,128,256]{2,1,0:T(8,128)(2,1)S(1)}, u32[]{:S(2)}, u32[]{:S(2)}) collective-permute-start(bf16[8,128,256]{2,1,0:T(8,128)(2,1)S(1)} %constant_dynamic-update-slice_fusion.4.near), channel_id=1, source_target_pairs={{0,16},{16,0},{1,17},{17,1},{2,18},{18,2},{3,19},{19,3},{4,20},{20... | collective-permute-start | bytes 1572872 | tf_op jit(solution)/shard_map/ppermute | solution.py:24
  73.0 9.6 %collective-permute-start.12 = (bf16[32,4096]{1,0:T(8,128)(2,1)S(1)}, bf16[32,4096]{1,0:T(8,128)(2,1)S(1)}, u32[]{:S(2)}, u32[]{:S(2)}) collective-permute-start(bf16[32,4096]{1,0:T(8,128)(2,1)S(1)} %bitcast.57), channel_id=1, source_target_pairs={{0,4},{4,8},{8,12},{12,0},{1,5},{5,9},{9,13},{13,1},{2,6},{6,10},{... | collective-permute-start | bytes 786440 | tf_op jit(solution)/shard_map/ppermute | solution.py:24
  73.1 17.8 %collective-permute-start.13 = (bf16[32,4096]{1,0:T(8,128)(2,1)S(1)}, bf16[32,4096]{1,0:T(8,128)(2,1)S(1)}, u32[]{:S(2)}, u32[]{:S(2)}) collective-permute-start(bf16[32,4096]{1,0:T(8,128)(2,1)S(1)} %bitcast.58), channel_id=1, source_target_pairs={{0,8},{4,12},{8,0},{12,4},{1,9},{5,13},{9,1},{13,5},{2,10},{6,14},... | collective-permute-start | bytes 786440 | tf_op jit(solution)/shard_map/ppermute | solution.py:24
  75.7 31.9 %collective-permute-start.14 = (bf16[32,4096]{1,0:T(8,128)(2,1)S(1)}, bf16[32,4096]{1,0:T(8,128)(2,1)S(1)}, u32[]{:S(2)}, u32[]{:S(2)}) collective-permute-start(bf16[32,4096]{1,0:T(8,128)(2,1)S(1)} %bitcast.59), channel_id=1, source_target_pairs={{0,12},{4,0},{8,4},{12,8},{1,13},{5,1},{9,5},{13,9},{2,14},{6,2},{... | collective-permute-start | bytes 786440 | tf_op jit(solution)/shard_map/ppermute | solution.py:24
  75.7 40.2 %collective-permute-start = (bf16[32,4096]{1,0:T(8,128)(2,1)S(1)}, bf16[32,4096]{1,0:T(8,128)(2,1)S(1)}, u32[]{:S(2)}, u32[]{:S(2)}) collective-permute-start(bf16[32,4096]{1,0:T(8,128)(2,1)S(1)} %bitcast.52), channel_id=1, source_target_pairs={{0,4},{4,8},{8,12},{12,0},{1,5},{5,9},{9,13},{13,1},{2,6},{6,10},{... | collective-permute-start | bytes 786440 | tf_op jit(solution)/shard_map/ppermute | solution.py:24
  82.6 33.7 %collective-permute-start.1 = (bf16[32,4096]{1,0:T(8,128)(2,1)S(1)}, bf16[32,4096]{1,0:T(8,128)(2,1)S(1)}, u32[]{:S(2)}, u32[]{:S(2)}) collective-permute-start(bf16[32,4096]{1,0:T(8,128)(2,1)S(1)} %bitcast.54), channel_id=1, source_target_pairs={{0,8},{4,12},{8,0},{12,4},{1,9},{5,13},{9,1},{13,5},{2,10},{6,14},... | collective-permute-start | bytes 786440 | tf_op jit(solution)/shard_map/ppermute | solution.py:24
  90.9 27.8 %collective-permute-start.2 = (bf16[32,4096]{1,0:T(8,128)(2,1)S(1)}, bf16[32,4096]{1,0:T(8,128)(2,1)S(1)}, u32[]{:S(2)}, u32[]{:S(2)}) collective-permute-start(bf16[32,4096]{1,0:T(8,128)(2,1)S(1)} %bitcast.55), channel_id=1, source_target_pairs={{0,12},{4,0},{8,4},{12,8},{1,13},{5,1},{9,5},{13,9},{2,14},{6,2},{... | collective-permute-start | bytes 786440 | tf_op jit(solution)/shard_map/ppermute | solution.py:24
  107.6 30.7 %collective-permute-start.15 = (bf16[128,4096]{1,0:T(8,128)(2,1)S(1)}, bf16[128,4096]{1,0:T(8,128)(2,1)S(1)}, u32[]{:S(2)}, u32[]{:S(2)}) collective-permute-start(bf16[128,4096]{1,0:T(8,128)(2,1)S(1)} %constant_dynamic-update-slice_fusion.9.refs_0_), channel_id=1, source_target_pairs={{0,1},{1,2},{2,3},{3,0},{4,5},{5,6},{6,7},{7,4},{8,9},{9,10},{10,1... | collective-permute-start | bytes 3145736 | tf_op jit(solution)/shard_map/ppermute | solution.py:24
  115.9 26.0 %collective-permute-start.16 = (bf16[128,4096]{1,0:T(8,128)(2,1)S(1)}, bf16[128,4096]{1,0:T(8,128)(2,1)S(1)}, u32[]{:S(2)}, u32[]{:S(2)}) collective-permute-start(bf16[128,4096]{1,0:T(8,128)(2,1)S(1)} %constant_dynamic-update-slice_fusion.9.refs_0_), channel_id=1, source_target_pairs={{0,3},{1,0},{2,1},{3,2},{4,7},{5,4},{6,5},{7,6},{8,11},{9,8},{10,9... | collective-permute-start | bytes 3145736 | tf_op jit(solution)/shard_map/ppermute | solution.py:24
  116.4 10.4 %slice-start = ((s8[8388608]{0:T(1024)(128)(4,1)}), s8[4194304]{0:T(1024)(128)(4,1)S(1)}, s32[]{:S(2)}) async-start(s8[8388608]{0:T(1024)(128)(4,1)} %bitcast.49), calls=%async_computation.3 | async-start | bytes 8388608
  118.7 8.1 %slice-start.1 = ((s8[8388608]{0:T(1024)(128)(4,1)}), s8[4194304]{0:T(1024)(128)(4,1)S(1)}, s32[]{:S(2)}) async-start(s8[8388608]{0:T(1024)(128)(4,1)} %bitcast.49), calls=%async_computation.4 | async-start | bytes 8388608
  118.7 38.6 %collective-permute-start.3 = (bf16[128,4096]{1,0:T(8,128)(2,1)S(1)}, bf16[128,4096]{1,0:T(8,128)(2,1)S(1)}, u32[]{:S(2)}, u32[]{:S(2)}) collective-permute-start(bf16[128,4096]{1,0:T(8,128)(2,1)S(1)} %constant_dynamic-update-slice_fusion.refs_0_), channel_id=1, source_target_pairs={{0,1},{1,2},{2,3},{3,0},{4,5},{5,6},{6,7},{7,4},{8,9},{9,10},{10,1... | collective-permute-start | bytes 3145736 | tf_op jit(solution)/shard_map/ppermute | solution.py:24
  119.4 45.1 %collective-permute-start.5 = (bf16[128,4096]{1,0:T(8,128)(2,1)S(1)}, bf16[128,4096]{1,0:T(8,128)(2,1)S(1)}, u32[]{:S(2)}, u32[]{:S(2)}) collective-permute-start(bf16[128,4096]{1,0:T(8,128)(2,1)S(1)} %constant_dynamic-update-slice_fusion.refs_0_), channel_id=1, source_target_pairs={{0,3},{1,0},{2,1},{3,2},{4,7},{5,4},{6,5},{7,6},{8,11},{9,8},{10,9... | collective-permute-start | bytes 3145736 | tf_op jit(solution)/shard_map/ppermute | solution.py:24
  138.3 33.3 %collective-permute-start.17 = (bf16[64,4096]{1,0:T(8,128)(2,1)S(1)}, bf16[64,4096]{1,0:T(8,128)(2,1)S(1)}, u32[]{:S(2)}, u32[]{:S(2)}) collective-permute-start(bf16[64,4096]{1,0:T(8,128)(2,1)S(1)} %slice.70), channel_id=1, source_target_pairs={{0,1},{1,2},{2,3},{3,0},{4,5},{5,6},{6,7},{7,4},{8,9},{9,10},{10,1... | collective-permute-start | bytes 1572872 | tf_op jit(solution)/shard_map/ppermute | solution.py:24
  142.0 33.7 %collective-permute-start.18 = (bf16[64,4096]{1,0:T(8,128)(2,1)S(1)}, bf16[64,4096]{1,0:T(8,128)(2,1)S(1)}, u32[]{:S(2)}, u32[]{:S(2)}) collective-permute-start(bf16[64,4096]{1,0:T(8,128)(2,1)S(1)} %slice.71), channel_id=1, source_target_pairs={{0,3},{1,0},{2,1},{3,2},{4,7},{5,4},{6,5},{7,6},{8,11},{9,8},{10,9... | collective-permute-start | bytes 1572872 | tf_op jit(solution)/shard_map/ppermute | solution.py:24
  157.4 21.4 %collective-permute-start.4 = (bf16[64,4096]{1,0:T(8,128)(2,1)S(1)}, bf16[64,4096]{1,0:T(8,128)(2,1)S(1)}, u32[]{:S(2)}, u32[]{:S(2)}) collective-permute-start(bf16[64,4096]{1,0:T(8,128)(2,1)S(1)} %slice.67), channel_id=1, source_target_pairs={{0,1},{1,2},{2,3},{3,0},{4,5},{5,6},{6,7},{7,4},{8,9},{9,10},{10,1... | collective-permute-start | bytes 1572872 | tf_op jit(solution)/shard_map/ppermute | solution.py:24
  164.5 20.6 %collective-permute-start.6 = (bf16[64,4096]{1,0:T(8,128)(2,1)S(1)}, bf16[64,4096]{1,0:T(8,128)(2,1)S(1)}, u32[]{:S(2)}, u32[]{:S(2)}) collective-permute-start(bf16[64,4096]{1,0:T(8,128)(2,1)S(1)} %slice.68), channel_id=1, source_target_pairs={{0,3},{1,0},{2,1},{3,2},{4,7},{5,4},{6,5},{7,6},{8,11},{9,8},{10,9... | collective-permute-start | bytes 1572872 | tf_op jit(solution)/shard_map/ppermute | solution.py:24
where the time goes:
time: 198 us; the launch traced here: 197 us
  waiting for transfers between devices  86.4 us (44%)
  starting transfers between devices  54.9 us (28%)
  Pallas kernels  29.1 us (15%)
  matrix products  19.1 us (10%)
  local copies, waits for them, and re-layouts  4.98 us (3%)
    ppermute x19, waiting for transfers between devices, cycle(): lax.ppermute(array, axis, [(i, (i + by) % size) for i in range(size)])  74 us
    ppermute x19, starting transfers between devices, cycle(): lax.ppermute(array, axis, [(i, (i + by) % size) for i in range(size)])  32.8 us
    dot_general x10, matrix products, body(): jnp.dot(rows, dosage, preferred_element_type=F32)  17.5 us
    pallas_call x3, Pallas kernels, finish(): pl.pallas_call(functools.partial(finish_kernel, float(samples) ** (-0.5),...  10.1 us
    pallas_call x1, Pallas kernels, body(): pl.pallas_call(hess_kernel, out_shape=(jax.ShapeDtypeStruct((k, all_sampl...  10.1 us
    pallas_call x1, Pallas kernels, body(): pl.pallas_call(factor_kernel, out_shape=jax.ShapeDtypeStruct((k, samples)...  8.94 us
    all_to_all x1, starting transfers between devices, body(): lax.all_to_all(flipped.reshape(n_samp, panel, samples), SAMP, 0, 0, tiled...  8.33 us
    all_to_all x1, starting transfers between devices, body(): lax.all_to_all(both.reshape(n_cols, k // n_cols, samples + k), COLS, 0, 0...  8.2 us
  transfers between devices with their start and end apart: 22, of which 16 were waited for; matrix products, arithmetic and copies ran while one was open for 10% of the time, Pallas kernels for 10%

commit v1 on v0

--- a/solution.py
+++ b/solution.py
@@ -184,14 +184,19 @@
         piece = mine[c * width : c * width + width]
         own = jnp.concatenate([piece] + [cycle(piece, "zl", by) for by in (1, 2, 3)])
         ahead, behind = cycle(own, "y", 1), cycle(own, "y", -1)
-        low, high = cycle(ahead[: 2 * width], "y", 1), cycle(behind[2 * width :], "y", -1)
+        low, high = ahead[: 2 * width], behind[2 * width :]
+        low, high = cycle(low, "y", 1), cycle(high, "y", -1)
         near_slots, far_slots = [(0, 4), (4, 8), (12, 16)], [(8, 10), (10, 12)]
         if c < CHUNKS - 1:
             groups.append((c * width, near_slots + far_slots, [own, ahead, behind, low, high]))
         else:
             groups.append((c * width, near_slots, [own, ahead, behind]))
             groups.append((c * width, far_slots, [low, high]))
-    scores = [[jnp.dot(rows, dosage, preferred_element_type=F32) for rows in pieces] for _, _, pieces in groups]
+    scores = []
+    for _, _, pieces in groups:
+        scores.append([])
+        for rows in pieces:
+            scores[-1].append(jnp.dot(rows, dosage, preferred_element_type=F32))
 
     two = jnp.stack([factors, cycle(factors, "zh", 1)])
     near = jnp.concatenate([two] + [cycle(two, "x", by) for by in (1, 2, 3)])

time: 198 us -> 198 us (level)
  no operation moved by 1% of the time
where the time goes in v1:
time: 198 us; the launch traced here: 197 us
  waiting for transfers between devices  86.4 us (44%)
  starting transfers between devices  54.9 us (28%)
  Pallas kernels  29.1 us (15%)
  matrix products  19.1 us (10%)
  local copies, waits for them, and re-layouts  4.98 us (3%)
    ppermute x19, waiting for transfers between devices, cycle(): lax.ppermute(array, axis, [(i, (i + by) % size) for i in range(size)])  74 us
    ppermute x19, starting transfers between devices, cycle(): lax.ppermute(array, axis, [(i, (i + by) % size) for i in range(size)])  32.8 us
    dot_general x10, matrix products, body(): scores[-1].append(jnp.dot(rows, dosage, preferred_element_type=F32))  17.5 us
    pallas_call x3, Pallas kernels, finish(): pl.pallas_call(functools.partial(finish_kernel, float(samples) ** (-0.5),...  10.1 us
    pallas_call x1, Pallas kernels, body(): pl.pallas_call(hess_kernel, out_shape=(jax.ShapeDtypeStruct((k, all_sampl...  10.1 us
    pallas_call x1, Pallas kernels, body(): pl.pallas_call(factor_kernel, out_shape=jax.ShapeDtypeStruct((k, samples)...  8.94 us
    all_to_all x1, starting transfers between devices, body(): lax.all_to_all(flipped.reshape(n_samp, panel, samples), SAMP, 0, 0, tiled...  8.33 us
    all_to_all x1, starting transfers between devices, body(): lax.all_to_all(both.reshape(n_cols, k // n_cols, samples + k), COLS, 0, 0...  8.2 us
  transfers between devices with their start and end apart: 22, of which 16 were waited for; matrix products, arithmetic and copies ran while one was open for 10% of the time, Pallas kernels for 10%

profile of v1, /device:TPU:64, one launch (start us, length us, event | category | flops | bytes accessed | tf_op | source)
XLA Modules:
  0.0 197.0 jit_solution(6699590486274105301)
XLA Ops:
  0.0 0.9 copy-done
  1.0 0.3 fusion.17
  1.2 1.4 fusion.16
  2.6 0.7 maximum_bitcast_fusion
  3.3 8.2 %all-to-all-start.1 = ((f32[16,8,384]{2,1,0:T(8,128)}), f32[16,8,384]{2,1,0:T(8,128)S(1)}, u32[]{:S(2)}, u32[]{:S(2)}) async-start(f32[16,8,384]{2,1,0:T(8,128)} %maximum_bitcast_fusion), calls=%async_computation.1 | async-start | bytes 393216 | tf_op jit(solution)/shard_map/all_to_all | solution.py:170
  11.5 0.1 broadcast_add_fusion
  11.6 7.4 %all-to-all-done.1 = f32[16,8,384]{2,1,0:T(8,128)S(1)} async-done(((f32[16,8,384]{2,1,0:T(8,128)}), f32[16,8,384]{2,1,0:T(8,128)S(1)}, u32[]{:S(2)}, u32[]{:S(2)}) %all-to-all-start.1) | async-done | bytes 196640 | tf_op jit(solution)/shard_map/all_to_all | solution.py:170
  19.0 0.7 broadcast_in_dim.2
  19.7 5.6 %all-to-all-start.2 = ((f32[16,8,384]{2,1,0:T(8,128)}), f32[16,8,384]{2,1,0:T(8,128)S(1)}, u32[]{:S(2)}, u32[]{:S(2)}) async-start(f32[16,8,384]{2,1,0:T(8,128)} %broadcast_in_dim.2), calls=%async_computation.2 | async-start | bytes 393216 | tf_op jit(solution)/shard_map/all_to_all | solution.py:172
  25.3 2.0 %copy.8 = bf16[256,1024]{0,1:T(8,128)(2,1)} copy(bf16[256,1024]{1,0:T(8,128)(2,1)} %param.3) | data formatting | bytes 1048576 | tf_op args[0]
  27.3 0.1 pad_add_fusion.places
  27.4 0.1 pad_add_fusion.1.places
  27.5 5.0 %all-to-all-done.2 = f32[16,8,384]{2,1,0:T(8,128)S(1)} async-done(((f32[16,8,384]{2,1,0:T(8,128)}), f32[16,8,384]{2,1,0:T(8,128)S(1)}, u32[]{:S(2)}, u32[]{:S(2)}) %all-to-all-start.2) | async-done | bytes 196640 | tf_op jit(solution)/shard_map/all_to_all | solution.py:172
  32.5 8.3 %all-to-all-start = ((bf16[16,64,256]{2,1,0:T(8,128)(2,1)}), bf16[16,64,256]{2,1,0:T(8,128)(2,1)S(1)}, u32[]{:S(2)}, u32[]{:S(2)}) async-start(bf16[16,64,256]{2,1,0:T(8,128)(2,1)} %bitcast.2), calls=%async_computation | async-start | bytes 1048576 | tf_op jit(solution)/shard_map/all_to_all | solution.py:160
  40.9 8.9 %factor.1 = bf16[128,256]{1,0:T(8,128)(2,1)} custom-call(f32[128,384]{1,0:T(8,128)} %bitcast.62), custom_call_target="tpu_custom_call" | custom-call | flops 7000000000 | bytes 400000 | tf_op jit(solution)/shard_map/factor/pallas_call | solution.py:173
  49.8 5.8 %collective-permute-start.7 = (bf16[128,256]{1,0:T(8,128)(2,1)}, bf16[128,256]{1,0:T(8,128)(2,1)S(1)}, u32[]{:S(2)}, u32[]{:S(2)}) collective-permute-start(bf16[128,256]{1,0:T(8,128)(2,1)} %factor.1), channel_id=1, source_target_pairs={{0,128},{128,0},{1,129},{129,1},{2,130},{130,2},{3,131},{131,3},{4... | collective-permute-start | bytes 196616 | tf_op jit(solution)/shard_map/ppermute | solution.py:24
  55.7 0.9 constant_dynamic-update-slice_fusion.8
  56.6 5.4 %collective-permute-done.7 = bf16[128,256]{1,0:T(8,128)(2,1)S(1)} collective-permute-done((bf16[128,256]{1,0:T(8,128)(2,1)}, bf16[128,256]{1,0:T(8,128)(2,1)S(1)}, u32[]{:S(2)}, u32[]{:S(2)}) %collective-permute-start.7) | collective-permute-done | bytes 65568 | tf_op jit(solution)/shard_map/ppermute | solution.py:24
  61.9 0.9 pad_maximum_fusion
  62.8 1.5 collective-permute-start.8
  64.3 2.7 %collective-permute-start.9 = (bf16[2,128,256]{2,1,0:T(8,128)(2,1)S(1)}, bf16[2,128,256]{2,1,0:T(8,128)(2,1)S(1)}, u32[]{:S(2)}, u32[]{:S(2)}) collective-permute-start(bf16[2,128,256]{2,1,0:T(8,128)(2,1)S(1)} %pad_maximum_fusion), channel_id=1, source_target_pairs={{0,64},{32,96},{64,0},{96,32},{1,65},{33,97},{65,1},{97,33},{2,66}... | collective-permute-start | bytes 393224 | tf_op jit(solution)/shard_map/ppermute | solution.py:24
  67.0 1.5 collective-permute-start.10
  68.5 1.1 collective-permute-done.8
  69.6 3.1 %collective-permute-done.9 = bf16[2,128,256]{2,1,0:T(8,128)(2,1)S(1)} collective-permute-done((bf16[2,128,256]{2,1,0:T(8,128)(2,1)S(1)}, bf16[2,128,256]{2,1,0:T(8,128)(2,1)S(1)}, u32[]{:S(2)}, u32[]{:S(2)}) %collective-permute-start.9) | collective-permute-done | bytes 131104 | tf_op jit(solution)/shard_map/ppermute | solution.py:24
  72.8 0.1 collective-permute-start.11
  73.0 0.1 collective-permute-start.12
  73.1 2.6 %collective-permute-start.13 = (bf16[32,4096]{1,0:T(8,128)(2,1)S(1)}, bf16[32,4096]{1,0:T(8,128)(2,1)S(1)}, u32[]{:S(2)}, u32[]{:S(2)}) collective-permute-start(bf16[32,4096]{1,0:T(8,128)(2,1)S(1)} %bitcast.58), channel_id=1, source_target_pairs={{0,8},{4,12},{8,0},{12,4},{1,9},{5,13},{9,1},{13,5},{2,10},{6,14},... | collective-permute-start | bytes 786440 | tf_op jit(solution)/shard_map/ppermute | solution.py:24
  75.7 2.1 %collective-permute-start = (bf16[32,4096]{1,0:T(8,128)(2,1)S(1)}, bf16[32,4096]{1,0:T(8,128)(2,1)S(1)}, u32[]{:S(2)}, u32[]{:S(2)}) collective-permute-start(bf16[32,4096]{1,0:T(8,128)(2,1)S(1)} %bitcast.52), channel_id=1, source_target_pairs={{0,4},{4,8},{8,12},{12,0},{1,5},{5,9},{9,13},{13,1},{2,6},{6,10},{... | collective-permute-start | bytes 786440 | tf_op jit(solution)/shard_map/ppermute | solution.py:24
  77.8 4.8 %collective-permute-done.12 = bf16[32,4096]{1,0:T(8,128)(2,1)S(1)} collective-permute-done((bf16[32,4096]{1,0:T(8,128)(2,1)S(1)}, bf16[32,4096]{1,0:T(8,128)(2,1)S(1)}, u32[]{:S(2)}, u32[]{:S(2)}) %collective-permute-start.12) | collective-permute-done | bytes 262176 | tf_op jit(solution)/shard_map/ppermute | solution.py:24
  82.6 0.7 collective-permute-start.1
  83.4 7.5 %collective-permute-done.13 = bf16[32,4096]{1,0:T(8,128)(2,1)S(1)} collective-permute-done((bf16[32,4096]{1,0:T(8,128)(2,1)S(1)}, bf16[32,4096]{1,0:T(8,128)(2,1)S(1)}, u32[]{:S(2)}, u32[]{:S(2)}) %collective-permute-start.13) | collective-permute-done | bytes 262176 | tf_op jit(solution)/shard_map/ppermute | solution.py:24
  90.9 7.6 %collective-permute-start.2 = (bf16[32,4096]{1,0:T(8,128)(2,1)S(1)}, bf16[32,4096]{1,0:T(8,128)(2,1)S(1)}, u32[]{:S(2)}, u32[]{:S(2)}) collective-permute-start(bf16[32,4096]{1,0:T(8,128)(2,1)S(1)} %bitcast.55), channel_id=1, source_target_pairs={{0,12},{4,0},{8,4},{12,8},{1,13},{5,1},{9,5},{13,9},{2,14},{6,2},{... | collective-permute-start | bytes 786440 | tf_op jit(solution)/shard_map/ppermute | solution.py:24
  98.5 9.0 %collective-permute-done.14 = bf16[32,4096]{1,0:T(8,128)(2,1)S(1)} collective-permute-done((bf16[32,4096]{1,0:T(8,128)(2,1)S(1)}, bf16[32,4096]{1,0:T(8,128)(2,1)S(1)}, u32[]{:S(2)}, u32[]{:S(2)}) %collective-permute-start.14) | collective-permute-done | bytes 262176 | tf_op jit(solution)/shard_map/ppermute | solution.py:24
  107.6 0.6 collective-permute-start.15
  108.2 7.8 %collective-permute-done = bf16[32,4096]{1,0:T(8,128)(2,1)S(1)} collective-permute-done((bf16[32,4096]{1,0:T(8,128)(2,1)S(1)}, bf16[32,4096]{1,0:T(8,128)(2,1)S(1)}, u32[]{:S(2)}, u32[]{:S(2)}) %collective-permute-start) | collective-permute-done | bytes 262176 | tf_op jit(solution)/shard_map/ppermute | solution.py:24
  115.9 0.4 collective-permute-start.16
  116.4 2.3 %collective-permute-done.2 = bf16[32,4096]{1,0:T(8,128)(2,1)S(1)} collective-permute-done((bf16[32,4096]{1,0:T(8,128)(2,1)S(1)}, bf16[32,4096]{1,0:T(8,128)(2,1)S(1)}, u32[]{:S(2)}, u32[]{:S(2)}) %collective-permute-start.2) | collective-permute-done | bytes 262176 | tf_op jit(solution)/shard_map/ppermute | solution.py:24
  118.7 0.0 slice-start.1
  118.7 0.6 collective-permute-start.3
  119.4 2.7 %collective-permute-start.5 = (bf16[128,4096]{1,0:T(8,128)(2,1)S(1)}, bf16[128,4096]{1,0:T(8,128)(2,1)S(1)}, u32[]{:S(2)}, u32[]{:S(2)}) collective-permute-start(bf16[128,4096]{1,0:T(8,128)(2,1)S(1)} %constant_dynamic-update-slice_fusion.refs_0_), channel_id=1, source_target_pairs={{0,3},{1,0},{2,1},{3,2},{4,7},{5,4},{6,5},{7,6},{8,11},{9,8},{10,9... | collective-permute-start | bytes 3145736 | tf_op jit(solution)/shard_map/ppermute | solution.py:24
  122.1 4.7 %fusion.21.refs_5_ = f32[128,1024]{1,0:T(8,128)S(1)} fusion(bf16[128,4096]{1,0:T(8,128)(2,1)S(1)} %constant_dynamic-update-slice_fusion.9.refs_0_, bf16[4096,1024]{1,0:T(8,128)(2,1)} %dos_hbm.1), kind=kOutput, calls=%fused_computation.70 | convolution fusion | flops 1073741824 | bytes 9961472 | tf_op jit(solution)/shard_map/dot_general | solution.py:199
  126.8 1.3 fusion.18.refs_3_
  128.1 10.1 %hess.1 = (bf16[128,4096]{1,0:T(8,128)(2,1)S(1)}, f32[128,128]{1,0:T(8,128)S(1)}, bf16[256,1024]{1,0:T(8,128)(2,1)S(1)}) custom-call(s32[16]{0:T(128)S(1)} %fusion.places, bf16[8,128,256]{2,1,0:T(8,128)(2,1)S(1)} %constant_dynamic-update-slice_fusion.4.near, bf16[8,128,256]{2,1,0:T(8,128)(2,1)S(1)} %collective-permute-done.11.other, ...), custom_call_target="tpu_custom_call" | custom-call | flops 8999999488 | bytes 10000000 | tf_op jit(solution)/shard_map/hess/pallas_call | solution.py:209
  138.3 0.1 collective-permute-start.17
  138.4 3.6 %collective-permute-done.16.refs_2_ = bf16[128,4096]{1,0:T(8,128)(2,1)S(1)} collective-permute-done((bf16[128,4096]{1,0:T(8,128)(2,1)S(1)}, bf16[128,4096]{1,0:T(8,128)(2,1)S(1)}, u32[]{:S(2)}, u32[]{:S(2)}) %collective-permute-start.16) | collective-permute-done | bytes 1048608 | tf_op jit(solution)/shard_map/ppermute | solution.py:24
  142.0 1.7 collective-permute-start.18
  143.7 13.7 %collective-permute-done.3.refs_1_ = bf16[128,4096]{1,0:T(8,128)(2,1)S(1)} collective-permute-done((bf16[128,4096]{1,0:T(8,128)(2,1)S(1)}, bf16[128,4096]{1,0:T(8,128)(2,1)S(1)}, u32[]{:S(2)}, u32[]{:S(2)}) %collective-permute-start.3) | collective-permute-done | bytes 1048608 | tf_op jit(solution)/shard_map/ppermute | solution.py:24
  157.4 0.1 collective-permute-start.4
  157.5 7.0 %collective-permute-done.5.refs_2_ = bf16[128,4096]{1,0:T(8,128)(2,1)S(1)} collective-permute-done((bf16[128,4096]{1,0:T(8,128)(2,1)S(1)}, bf16[128,4096]{1,0:T(8,128)(2,1)S(1)}, u32[]{:S(2)}, u32[]{:S(2)}) %collective-permute-start.5) | collective-permute-done | bytes 1048608 | tf_op jit(solution)/shard_map/ppermute | solution.py:24
  164.5 1.9 collective-permute-start.6
  166.4 1.3 fusion.22.refs_6_
  167.7 1.3 fusion.23.refs_7_
  169.0 1.3 fusion.19.refs_4_
  170.3 1.3 fusion.20.refs_5_
  171.6 1.6 fusion.24.refs_8_
  173.2 2.5 %collective-permute-done.18.refs_4_ = bf16[64,4096]{1,0:T(8,128)(2,1)S(1)} collective-permute-done((bf16[64,4096]{1,0:T(8,128)(2,1)S(1)}, bf16[64,4096]{1,0:T(8,128)(2,1)S(1)}, u32[]{:S(2)}, u32[]{:S(2)}) %collective-permute-start.18) | collective-permute-done | bytes 524320 | tf_op jit(solution)/shard_map/ppermute | solution.py:24
  175.7 1.6 fusion.25.refs_9_
  177.3 1.6 collective-permute-done.4.refs_0_
  178.8 1.6 fusion.14.refs_2_
  180.4 4.7 %collective-permute-done.6.refs_1_ = bf16[64,4096]{1,0:T(8,128)(2,1)S(1)} collective-permute-done((bf16[64,4096]{1,0:T(8,128)(2,1)S(1)}, bf16[64,4096]{1,0:T(8,128)(2,1)S(1)}, u32[]{:S(2)}, u32[]{:S(2)}) %collective-permute-start.6) | collective-permute-done | bytes 524320 | tf_op jit(solution)/shard_map/ppermute | solution.py:24
  185.1 1.6 fusion.15.refs_3_
  186.7 4.2 %shard_map.37.refs_9_ = bf16[16,1,64,1024]{3,2,1,0:T(8,128)(2,1)} custom-call(s32[16]{0:T(128)S(1)} %pad_add_fusion.1.places, bf16[128,4096]{1,0:T(8,128)(2,1)S(1)} %constant_dynamic-update-slice_fusion.9.refs_0_, bf16[128,4096]{1,0:T(8,128)(2,1)S(1)} %collective-permute-done.15.refs_1_, bf16[128,4096]{1,0:T(8,128)(2,1)S(1)} %collective-permute-done.16.refs_2_, ...), custom_call_target="tpu_custom_call" | custom-call | flops 1073741824 | bytes 8388608 | tf_op jit(solution)/shard_map/pallas_call | solution.py:135
  190.9 3.4 %shard_map.38.refs_7_ = bf16[16,1,64,1024]{3,2,1,0:T(8,128)(2,1)} custom-call(s32[12]{0:T(128)S(1)} %pad_add_fusion.places, bf16[128,4096]{1,0:T(8,128)(2,1)S(1)} %constant_dynamic-update-slice_fusion.refs_0_, bf16[128,4096]{1,0:T(8,128)(2,1)S(1)} %collective-permute-done.3.refs_1_, ...), custom_call_target="tpu_custom_call", output_to_operand_aliasing={{}: (10, {})} | custom-call | flops 805306368 | bytes 6291456 | tf_op jit(solution)/shard_map/pallas_call | solution.py:135
  194.3 2.6 %shard_map.39 = bf16[16,1,64,1024]{3,2,1,0:T(8,128)(2,1)} custom-call(s32[4]{0:T(128)S(1)} %get-tuple-element.16.places, bf16[64,4096]{1,0:T(8,128)(2,1)S(1)} %collective-permute-done.4.refs_0_, bf16[64,4096]{1,0:T(8,128)(2,1)S(1)} %collective-permute-done.6.refs_1_, f32[64,1024]{1,0:T(8,128)S(1)} %fusion.14.refs_2_, ...), custom_call_target="tpu_custom_call", output_to_operand_aliasing={{}: (8, {})} | custom-call | flops 268435456 | bytes 2097152 | tf_op jit(solution)/shard_map/pallas_call | solution.py:135
  (37 shorter events, 0.5 us)
Async XLA Ops:
  0.0 1.0 copy-start
  3.3 15.7 %all-to-all-start.1 = ((f32[16,8,384]{2,1,0:T(8,128)}), f32[16,8,384]{2,1,0:T(8,128)S(1)}, u32[]{:S(2)}, u32[]{:S(2)}) async-start(f32[16,8,384]{2,1,0:T(8,128)} %maximum_bitcast_fusion), calls=%async_computation.1 | async-start | bytes 393216 | tf_op jit(solution)/shard_map/all_to_all | solution.py:170
  19.7 12.8 %all-to-all-start.2 = ((f32[16,8,384]{2,1,0:T(8,128)}), f32[16,8,384]{2,1,0:T(8,128)S(1)}, u32[]{:S(2)}, u32[]{:S(2)}) async-start(f32[16,8,384]{2,1,0:T(8,128)} %broadcast_in_dim.2), calls=%async_computation.2 | async-start | bytes 393216 | tf_op jit(solution)/shard_map/all_to_all | solution.py:172
  32.5 8.3 %copy-start.1 = (f32[16,8,384]{2,1,0:T(8,128)}, f32[16,8,384]{2,1,0:T(8,128)S(1)}, u32[]{:S(2)}) copy-start(f32[16,8,384]{2,1,0:T(8,128)S(1)} %all-to-all-done.2) | copy-start | bytes 589828
  32.5 40.3 %all-to-all-start = ((bf16[16,64,256]{2,1,0:T(8,128)(2,1)}), bf16[16,64,256]{2,1,0:T(8,128)(2,1)S(1)}, u32[]{:S(2)}, u32[]{:S(2)}) async-start(bf16[16,64,256]{2,1,0:T(8,128)(2,1)} %bitcast.2), calls=%async_computation | async-start | bytes 1048576 | tf_op jit(solution)/shard_map/all_to_all | solution.py:160
  49.8 12.1 %collective-permute-start.7 = (bf16[128,256]{1,0:T(8,128)(2,1)}, bf16[128,256]{1,0:T(8,128)(2,1)S(1)}, u32[]{:S(2)}, u32[]{:S(2)}) collective-permute-start(bf16[128,256]{1,0:T(8,128)(2,1)} %factor.1), channel_id=1, source_target_pairs={{0,128},{128,0},{1,129},{129,1},{2,130},{130,2},{3,131},{131,3},{4... | collective-permute-start | bytes 196616 | tf_op jit(solution)/shard_map/ppermute | solution.py:24
  62.8 6.8 %collective-permute-start.8 = (bf16[2,128,256]{2,1,0:T(8,128)(2,1)S(1)}, bf16[2,128,256]{2,1,0:T(8,128)(2,1)S(1)}, u32[]{:S(2)}, u32[]{:S(2)}) collective-permute-start(bf16[2,128,256]{2,1,0:T(8,128)(2,1)S(1)} %pad_maximum_fusion), channel_id=1, source_target_pairs={{0,32},{32,64},{64,96},{96,0},{1,33},{33,65},{65,97},{97,1},{2,34}... | collective-permute-start | bytes 393224 | tf_op jit(solution)/shard_map/ppermute | solution.py:24
  64.3 8.4 %collective-permute-start.9 = (bf16[2,128,256]{2,1,0:T(8,128)(2,1)S(1)}, bf16[2,128,256]{2,1,0:T(8,128)(2,1)S(1)}, u32[]{:S(2)}, u32[]{:S(2)}) collective-permute-start(bf16[2,128,256]{2,1,0:T(8,128)(2,1)S(1)} %pad_maximum_fusion), channel_id=1, source_target_pairs={{0,64},{32,96},{64,0},{96,32},{1,65},{33,97},{65,1},{97,33},{2,66}... | collective-permute-start | bytes 393224 | tf_op jit(solution)/shard_map/ppermute | solution.py:24
  67.0 5.7 %collective-permute-start.10 = (bf16[2,128,256]{2,1,0:T(8,128)(2,1)S(1)}, bf16[2,128,256]{2,1,0:T(8,128)(2,1)S(1)}, u32[]{:S(2)}, u32[]{:S(2)}) collective-permute-start(bf16[2,128,256]{2,1,0:T(8,128)(2,1)S(1)} %pad_maximum_fusion), channel_id=1, source_target_pairs={{0,96},{32,0},{64,32},{96,64},{1,97},{33,1},{65,33},{97,65},{2,98}... | collective-permute-start | bytes 393224 | tf_op jit(solution)/shard_map/ppermute | solution.py:24
  72.8 55.4 %collective-permute-start.11 = (bf16[8,128,256]{2,1,0:T(8,128)(2,1)S(1)}, bf16[8,128,256]{2,1,0:T(8,128)(2,1)S(1)}, u32[]{:S(2)}, u32[]{:S(2)}) collective-permute-start(bf16[8,128,256]{2,1,0:T(8,128)(2,1)S(1)} %constant_dynamic-update-slice_fusion.4.near), channel_id=1, source_target_pairs={{0,16},{16,0},{1,17},{17,1},{2,18},{18,2},{3,19},{19,3},{4,20},{20... | collective-permute-start | bytes 1572872 | tf_op jit(solution)/shard_map/ppermute | solution.py:24
  73.0 9.6 %collective-permute-start.12 = (bf16[32,4096]{1,0:T(8,128)(2,1)S(1)}, bf16[32,4096]{1,0:T(8,128)(2,1)S(1)}, u32[]{:S(2)}, u32[]{:S(2)}) collective-permute-start(bf16[32,4096]{1,0:T(8,128)(2,1)S(1)} %bitcast.57), channel_id=1, source_target_pairs={{0,4},{4,8},{8,12},{12,0},{1,5},{5,9},{9,13},{13,1},{2,6},{6,10},{... | collective-permute-start | bytes 786440 | tf_op jit(solution)/shard_map/ppermute | solution.py:24
  73.1 17.8 %collective-permute-start.13 = (bf16[32,4096]{1,0:T(8,128)(2,1)S(1)}, bf16[32,4096]{1,0:T(8,128)(2,1)S(1)}, u32[]{:S(2)}, u32[]{:S(2)}) collective-permute-start(bf16[32,4096]{1,0:T(8,128)(2,1)S(1)} %bitcast.58), channel_id=1, source_target_pairs={{0,8},{4,12},{8,0},{12,4},{1,9},{5,13},{9,1},{13,5},{2,10},{6,14},... | collective-permute-start | bytes 786440 | tf_op jit(solution)/shard_map/ppermute | solution.py:24
  75.7 31.9 %collective-permute-start.14 = (bf16[32,4096]{1,0:T(8,128)(2,1)S(1)}, bf16[32,4096]{1,0:T(8,128)(2,1)S(1)}, u32[]{:S(2)}, u32[]{:S(2)}) collective-permute-start(bf16[32,4096]{1,0:T(8,128)(2,1)S(1)} %bitcast.59), channel_id=1, source_target_pairs={{0,12},{4,0},{8,4},{12,8},{1,13},{5,1},{9,5},{13,9},{2,14},{6,2},{... | collective-permute-start | bytes 786440 | tf_op jit(solution)/shard_map/ppermute | solution.py:24
  75.7 40.2 %collective-permute-start = (bf16[32,4096]{1,0:T(8,128)(2,1)S(1)}, bf16[32,4096]{1,0:T(8,128)(2,1)S(1)}, u32[]{:S(2)}, u32[]{:S(2)}) collective-permute-start(bf16[32,4096]{1,0:T(8,128)(2,1)S(1)} %bitcast.52), channel_id=1, source_target_pairs={{0,4},{4,8},{8,12},{12,0},{1,5},{5,9},{9,13},{13,1},{2,6},{6,10},{... | collective-permute-start | bytes 786440 | tf_op jit(solution)/shard_map/ppermute | solution.py:24
  82.6 33.7 %collective-permute-start.1 = (bf16[32,4096]{1,0:T(8,128)(2,1)S(1)}, bf16[32,4096]{1,0:T(8,128)(2,1)S(1)}, u32[]{:S(2)}, u32[]{:S(2)}) collective-permute-start(bf16[32,4096]{1,0:T(8,128)(2,1)S(1)} %bitcast.54), channel_id=1, source_target_pairs={{0,8},{4,12},{8,0},{12,4},{1,9},{5,13},{9,1},{13,5},{2,10},{6,14},... | collective-permute-start | bytes 786440 | tf_op jit(solution)/shard_map/ppermute | solution.py:24
  90.9 27.8 %collective-permute-start.2 = (bf16[32,4096]{1,0:T(8,128)(2,1)S(1)}, bf16[32,4096]{1,0:T(8,128)(2,1)S(1)}, u32[]{:S(2)}, u32[]{:S(2)}) collective-permute-start(bf16[32,4096]{1,0:T(8,128)(2,1)S(1)} %bitcast.55), channel_id=1, source_target_pairs={{0,12},{4,0},{8,4},{12,8},{1,13},{5,1},{9,5},{13,9},{2,14},{6,2},{... | collective-permute-start | bytes 786440 | tf_op jit(solution)/shard_map/ppermute | solution.py:24
  107.6 30.7 %collective-permute-start.15 = (bf16[128,4096]{1,0:T(8,128)(2,1)S(1)}, bf16[128,4096]{1,0:T(8,128)(2,1)S(1)}, u32[]{:S(2)}, u32[]{:S(2)}) collective-permute-start(bf16[128,4096]{1,0:T(8,128)(2,1)S(1)} %constant_dynamic-update-slice_fusion.9.refs_0_), channel_id=1, source_target_pairs={{0,1},{1,2},{2,3},{3,0},{4,5},{5,6},{6,7},{7,4},{8,9},{9,10},{10,1... | collective-permute-start | bytes 3145736 | tf_op jit(solution)/shard_map/ppermute | solution.py:24
  115.9 26.0 %collective-permute-start.16 = (bf16[128,4096]{1,0:T(8,128)(2,1)S(1)}, bf16[128,4096]{1,0:T(8,128)(2,1)S(1)}, u32[]{:S(2)}, u32[]{:S(2)}) collective-permute-start(bf16[128,4096]{1,0:T(8,128)(2,1)S(1)} %constant_dynamic-update-slice_fusion.9.refs_0_), channel_id=1, source_target_pairs={{0,3},{1,0},{2,1},{3,2},{4,7},{5,4},{6,5},{7,6},{8,11},{9,8},{10,9... | collective-permute-start | bytes 3145736 | tf_op jit(solution)/shard_map/ppermute | solution.py:24
  116.4 10.4 %slice-start = ((s8[8388608]{0:T(1024)(128)(4,1)}), s8[4194304]{0:T(1024)(128)(4,1)S(1)}, s32[]{:S(2)}) async-start(s8[8388608]{0:T(1024)(128)(4,1)} %bitcast.49), calls=%async_computation.3 | async-start | bytes 8388608
  118.7 8.1 %slice-start.1 = ((s8[8388608]{0:T(1024)(128)(4,1)}), s8[4194304]{0:T(1024)(128)(4,1)S(1)}, s32[]{:S(2)}) async-start(s8[8388608]{0:T(1024)(128)(4,1)} %bitcast.49), calls=%async_computation.4 | async-start | bytes 8388608
  118.7 38.6 %collective-permute-start.3 = (bf16[128,4096]{1,0:T(8,128)(2,1)S(1)}, bf16[128,4096]{1,0:T(8,128)(2,1)S(1)}, u32[]{:S(2)}, u32[]{:S(2)}) collective-permute-start(bf16[128,4096]{1,0:T(8,128)(2,1)S(1)} %constant_dynamic-update-slice_fusion.refs_0_), channel_id=1, source_target_pairs={{0,1},{1,2},{2,3},{3,0},{4,5},{5,6},{6,7},{7,4},{8,9},{9,10},{10,1... | collective-permute-start | bytes 3145736 | tf_op jit(solution)/shard_map/ppermute | solution.py:24
  119.4 45.1 %collective-permute-start.5 = (bf16[128,4096]{1,0:T(8,128)(2,1)S(1)}, bf16[128,4096]{1,0:T(8,128)(2,1)S(1)}, u32[]{:S(2)}, u32[]{:S(2)}) collective-permute-start(bf16[128,4096]{1,0:T(8,128)(2,1)S(1)} %constant_dynamic-update-slice_fusion.refs_0_), channel_id=1, source_target_pairs={{0,3},{1,0},{2,1},{3,2},{4,7},{5,4},{6,5},{7,6},{8,11},{9,8},{10,9... | collective-permute-start | bytes 3145736 | tf_op jit(solution)/shard_map/ppermute | solution.py:24
  138.3 33.3 %collective-permute-start.17 = (bf16[64,4096]{1,0:T(8,128)(2,1)S(1)}, bf16[64,4096]{1,0:T(8,128)(2,1)S(1)}, u32[]{:S(2)}, u32[]{:S(2)}) collective-permute-start(bf16[64,4096]{1,0:T(8,128)(2,1)S(1)} %slice.70), channel_id=1, source_target_pairs={{0,1},{1,2},{2,3},{3,0},{4,5},{5,6},{6,7},{7,4},{8,9},{9,10},{10,1... | collective-permute-start | bytes 1572872 | tf_op jit(solution)/shard_map/ppermute | solution.py:24
  142.0 33.7 %collective-permute-start.18 = (bf16[64,4096]{1,0:T(8,128)(2,1)S(1)}, bf16[64,4096]{1,0:T(8,128)(2,1)S(1)}, u32[]{:S(2)}, u32[]{:S(2)}) collective-permute-start(bf16[64,4096]{1,0:T(8,128)(2,1)S(1)} %slice.71), channel_id=1, source_target_pairs={{0,3},{1,0},{2,1},{3,2},{4,7},{5,4},{6,5},{7,6},{8,11},{9,8},{10,9... | collective-permute-start | bytes 1572872 | tf_op jit(solution)/shard_map/ppermute | solution.py:24
  157.4 21.4 %collective-permute-start.4 = (bf16[64,4096]{1,0:T(8,128)(2,1)S(1)}, bf16[64,4096]{1,0:T(8,128)(2,1)S(1)}, u32[]{:S(2)}, u32[]{:S(2)}) collective-permute-start(bf16[64,4096]{1,0:T(8,128)(2,1)S(1)} %slice.67), channel_id=1, source_target_pairs={{0,1},{1,2},{2,3},{3,0},{4,5},{5,6},{6,7},{7,4},{8,9},{9,10},{10,1... | collective-permute-start | bytes 1572872 | tf_op jit(solution)/shard_map/ppermute | solution.py:24
  164.5 20.6 %collective-permute-start.6 = (bf16[64,4096]{1,0:T(8,128)(2,1)S(1)}, bf16[64,4096]{1,0:T(8,128)(2,1)S(1)}, u32[]{:S(2)}, u32[]{:S(2)}) collective-permute-start(bf16[64,4096]{1,0:T(8,128)(2,1)S(1)} %slice.68), channel_id=1, source_target_pairs={{0,3},{1,0},{2,1},{3,2},{4,7},{5,4},{6,5},{7,6},{8,11},{9,8},{10,9... | collective-permute-start | bytes 1572872 | tf_op jit(solution)/shard_map/ppermute | solution.py:24

commit v2 on v0

v2 whole, which is shorter than its diff:
```python
import functools

import jax
import jax.numpy as jnp
from jax import lax
from jax.experimental import pallas as pl
from jax.experimental.pallas import tpu as pltpu
from jax.sharding import Mesh, PartitionSpec as P

ridge_factor = 1.0
ridge_sample = 1.0
SAMP = ("zh", "x", "core")
COLS = ("zl", "y")
CHUNKS = 2
F32 = jnp.float32
BF16 = jnp.bfloat16
HI = lax.Precision.HIGHEST
NT = (((1,), (1,)), ((), ()))
TN = (((0,), (0,)), ((), ()))


def cycle(array, axis, by):
    size = lax.axis_size(axis)
    return lax.ppermute(array, axis, [(i, (i + by) % size) for i in range(size)])


def invert2(a, b, c):
    r = 1.0 / (a * c - b * b)
    return c * r, -b * r, a * r


def sweep(a_ref, beside):
    n = a_ref.shape[0]
    ci = lax.broadcasted_iota(jnp.int32, (n, n), 1)
    lane = ci[:1]

    def step(t, _):
        k = 4 * t
        beside(t, True)
        a = a_ref[...]
        r = [a_ref[pl.ds(k + i, 1), :] for i in range(4)]
        c = [jnp.sum(jnp.where(ci == k + i, a, 0.0), axis=1, keepdims=True) for i in range(4)]
        b = [[None] * i + [jnp.sum(jnp.where(lane == k + j, r[i], 0.0), axis=1, keepdims=True) for j in range(i, 4)] for i in range(4)]
        s11, s12, s22 = invert2(b[0][0], b[0][1], b[1][1])
        q11, q12, q21, q22 = b[0][2], b[0][3], b[1][2], b[1][3]
        w11, w12 = s11 * q11 + s12 * q21, s11 * q12 + s12 * q22
        w21, w22 = s12 * q11 + s22 * q21, s12 * q12 + s22 * q22
        t11, t12, t22 = invert2(
            b[2][2] - (q11 * w11 + q21 * w21), b[2][3] - (q11 * w12 + q21 * w22), b[3][3] - (q12 * w12 + q22 * w22)
        )
        m11, m12 = -(w11 * t11 + w12 * t12), -(w11 * t12 + w12 * t22)
        m21, m22 = -(w21 * t11 + w22 * t12), -(w21 * t12 + w22 * t22)
        l11, l12 = s11 - (m11 * w11 + m12 * w12), s12 - (m11 * w21 + m12 * w22)
        l22 = s22 - (m21 * w21 + m22 * w22)
        inv = [[l11, l12, m11, m12], [l12, l22, m21, m22], [m11, m21, t11, t12], [m12, m22, t12, t22]]
        p = [(inv[i][0] * r[0] + inv[i][1] * r[1]) + (inv[i][2] * r[2] + inv[i][3] * r[3]) for i in range(4)]
        new = a - ((c[0] * p[0] + c[1] * p[1]) + (c[2] * p[2] + c[3] * p[3]))
        for i in range(4):
            q = (inv[i][0] * c[0] + inv[i][1] * c[1]) + (inv[i][2] * c[2] + inv[i][3] * c[3])
            new = jnp.where(ci == k + i, q, new)
        a_ref[...] = new
        for i in range(4):
            for j in range(4):
                p[i] = jnp.where(lane == k + j, -inv[i][j], p[i])
            a_ref[pl.ds(k + i, 1), :] = p[i]
        beside(t)
        return 0

    lax.fori_loop(0, n // 4, step, 0)


def eye(n):
    ri = lax.broadcasted_iota(jnp.int32, (n, n), 0)
    return jnp.where(ri == lax.broadcasted_iota(jnp.int32, (n, n), 1), 1.0, 0.0).astype(F32)


STEPS = 32
TILE = 256


class Products:
    def __init__(self, dos_hbm, dos, sems):
        self.dos = dos
        self.copies = [
            pltpu.make_async_copy(
                dos_hbm.at[:, pl.ds(n * TILE, TILE)], dos.at[:, pl.ds(n * TILE, TILE)], sems.at[n]
            )
            for n in range(dos.shape[1] // TILE)
        ]
        self.shares = STEPS // len(self.copies)
        self.pairs = []
        for copy in self.copies:
            copy.start()

    def __call__(self, t, before=False):
        if before:
            for n, copy in enumerate(self.copies):
                pl.when(t == n * self.shares)(copy.wait)
            return
        depth = self.dos.shape[0] // self.shares
        part = lax.rem(t, self.shares)
        inner = pl.ds(pl.multiple_of(part * depth, depth), depth)
        column = pl.ds(pl.multiple_of(lax.div(t, self.shares) * TILE, TILE), TILE)
        tile = self.dos[inner, column]
        for rows, out in self.pairs:
            found = jnp.dot(rows[:, inner], tile, preferred_element_type=F32)
            out[:, column] = jnp.where(part == 0, found, out[:, column] + found)


def factor_kernel(sums_ref, rows, dos_hbm, out_ref, score, mat, dos, sems):
    k = sums_ref.shape[0]
    products = Products(dos_hbm, dos, sems)
    products.pairs = [(rows, score)]
    mat[...] = sums_ref[:, -k:] + ridge_factor * eye(k)
    sweep(mat, products)
    found = jnp.dot(-mat[...], sums_ref[:, :-k], preferred_element_type=F32, precision=HI)
    out_ref[...] = found.astype(BF16)


def hess_kernel(places, near, other, ahead, behind, dos_hbm, fac, inverse, proj, score1, score2, mat, total, dos, sems):
    k = mat.shape[0]
    width = near.shape[2]
    products = Products(dos_hbm, dos, sems)
    products.pairs = [(fac, total), (ahead, score1), (behind, score2)]
    for i in range(8):
        fac[:, pl.ds(pl.multiple_of(places[i] * width, width), width)] = near[i]
        fac[:, pl.ds(pl.multiple_of(places[8 + i] * width, width), width)] = other[i]
    mat[...] = lax.dot_general(fac[...], fac[...], NT, preferred_element_type=F32) + ridge_sample * eye(k)
    sweep(mat, products)
    inverse[...] = -mat[...]
    found = total[...]
    high = found.astype(BF16)
    proj[:k, :] = high
    proj[k:, :] = (found - high.astype(F32)).astype(BF16)


def finish_kernel(scale, genes, spots, given, places, *refs):
    count = len(spots)
    pieces, scores = refs[:count], refs[count : count + given]
    dos, fac, inverse, proj = refs[count + given : count + given + 4]
    out, done, coef, sems = refs[-4:]
    n = pl.program_id(0)

    @pl.when(n == 0)
    def _():
        at = 0
        for piece in pieces:
            cross = lax.dot_general(piece[...], fac[...], NT, preferred_element_type=F32)
            half = jnp.dot(cross, inverse[...], preferred_element_type=F32, precision=HI).astype(BF16)
            coef[pl.ds(at, piece.shape[0]), :] = jnp.concatenate([half, half], axis=1)
            at += piece.shape[0]

    at = 0
    for i, piece in enumerate(pieces):
        rows = pl.ds(at, piece.shape[0])
        total = scores[i][...] if i < given else jnp.dot(piece[...], dos[...], preferred_element_type=F32)
        total -= jnp.dot(coef[rows, :], proj[...], preferred_element_type=F32)
        done[rows, pl.ds(pl.multiple_of(n * TILE, TILE), TILE)] = (total * scale).astype(BF16)
        at += piece.shape[0]

    @pl.when(n == pl.num_programs(0) - 1)
    def _():
        copies, at = [], 0
        for (start, slot), piece in zip(spots, pieces):
            for i in range(piece.shape[0] // genes):
                copies.append(
                    pltpu.make_async_copy(
                        done.at[pl.ds(at, genes), :],
                        out.at[places[slot + i], 0, pl.ds(start, genes), :],
                        sems.at[at // genes],
                    )
                )
                at += genes
        for copy in copies:
            copy.start()
        for copy in copies:
            copy.wait()


def finish(places, spots, pieces, scores, dosage, fac, inverse, proj, out, genes, panel):
    samples, snps = dosage.shape
    rows = sum(p.shape[0] for p in pieces)
    fixed = lambda a: pl.BlockSpec(a.shape, lambda n, _: (0, 0), pipeline_mode=pl.Buffered(1))
    across = lambda a: pl.BlockSpec((a.shape[0], TILE), lambda n, _: (0, n))
    ins = list(pieces) + list(scores) + [dosage, fac, inverse, proj]
    specs = [fixed(a) for a in pieces] + [across(a) for a in scores]
    specs += [across(dosage), fixed(fac), fixed(inverse), across(proj)]
    alias = {}
    if out is not None:
        alias = {len(ins) + 1: 0}
        ins.append(out)
        specs.append(pl.BlockSpec(memory_space=pl.ANY))
    return pl.pallas_call(
        functools.partial(finish_kernel, float(samples) ** -0.5, genes, spots, len(scores)),
        out_shape=jax.ShapeDtypeStruct((16, 1, panel, snps), BF16),
        grid_spec=pltpu.PrefetchScalarGridSpec(
            num_scalar_prefetch=1,
            grid=(snps // TILE,),
            in_specs=specs,
            out_specs=pl.BlockSpec(memory_space=pl.ANY),
            scratch_shapes=[
                pltpu.VMEM((rows, snps), BF16),
                pltpu.VMEM((rows, proj.shape[0]), BF16),
                pltpu.SemaphoreType.DMA((rows // genes,)),
            ],
        ),
        input_output_aliases=alias,
        cost_estimate=pl.CostEstimate(flops=2 * rows * samples * 1024, bytes_accessed=rows * 16384, transcendentals=0),
        compiler_params=pltpu.CompilerParams(vmem_limit_bytes=36 << 20),
    )(places, *ins)


def body(expression, loadings, dosage):
    samples, genes = expression.shape
    k = loadings.shape[1]
    n_samp, n_cols = lax.axis_size(SAMP), lax.axis_size(COLS)
    panel = genes // n_samp
    all_samples, snps = dosage.shape
    at = {name: lax.axis_index(name) for name in SAMP + COLS}

    flipped = expression.T
    mine = lax.all_to_all(flipped.reshape(n_samp, panel, samples), SAMP, 0, 0, tiled=True)
    mine = mine.transpose(1, 0, 2).reshape(panel, all_samples)

    both = jnp.concatenate(
        [
            lax.dot_general(loadings, flipped, TN, preferred_element_type=F32),
            lax.dot_general(loadings, loadings, TN, preferred_element_type=F32),
        ],
        axis=1,
    )
    both = lax.all_to_all(both.reshape(n_cols, k // n_cols, samples + k), COLS, 0, 0, tiled=True)
    both = both.sum(axis=0)
    both = lax.all_to_all(jnp.broadcast_to(both[None], (n_cols,) + both.shape), COLS, 0, 0, tiled=True)
    width = panel // CHUNKS
    groups = []
    for c in range(CHUNKS):
        piece = mine[c * width : c * width + width]
        own = jnp.concatenate([piece] + [cycle(piece, "zl", by) for by in (1, 2, 3)])
        ahead, behind = cycle(own, "y", 1), cycle(own, "y", -1)
        low, high = ahead[: 2 * width], behind[2 * width :]
        low, high = cycle(low, "y", 1), cycle(high, "y", -1)
        groups.append((own, ahead, behind, low, high))

    vmem, hbm = pl.BlockSpec(memory_space=pltpu.VMEM), pl.BlockSpec(memory_space=pltpu.HBM)
    table = jax.ShapeDtypeStruct((4 * width, snps), F32)
    tiles = [pltpu.VMEM(dosage.shape, BF16), pltpu.SemaphoreType.DMA((snps // TILE,))]
    roomy = pltpu.CompilerParams(vmem_limit_bytes=30 << 20)
    factors, score0 = pl.pallas_call(
        factor_kernel,
        out_shape=(jax.ShapeDtypeStruct((k, samples), BF16), table),
        in_specs=[vmem, vmem, hbm],
        scratch_shapes=[pltpu.VMEM((k, k), F32)] + tiles,
        cost_estimate=pl.CostEstimate(flops=7_000_000_000, bytes_accessed=400_000, transcendentals=0),
        compiler_params=roomy,
        name="factor",
    )(both.reshape(k, samples + k), groups[0][0], dosage)

    two = jnp.stack([factors, cycle(factors, "zh", 1)])
    near = jnp.concatenate([two] + [cycle(two, "x", by) for by in (1, 2, 3)])
    other = cycle(near, "core", 1)
    back = jnp.arange(16)
    from_core = (at["core"] - back // 8) % 2
    from_x = (at["x"] - back // 2 % 4) % 4
    from_zh = (at["zh"] - back % 2) % 2
    order = (from_zh * 8 + from_x * 2 + from_core).astype(jnp.int32)
    fac, inverse, proj, score1, score2 = pl.pallas_call(
        hess_kernel,
        out_shape=(
            jax.ShapeDtypeStruct((k, all_samples), BF16),
            jax.ShapeDtypeStruct((k, k), F32),
            jax.ShapeDtypeStruct((2 * k, snps), BF16),
            table,
            table,
        ),
        in_specs=[pl.BlockSpec(memory_space=pltpu.SMEM), vmem, vmem, vmem, vmem, hbm],
        scratch_shapes=[pltpu.VMEM((k, k), F32), pltpu.VMEM((k, snps), F32)] + tiles,
        cost_estimate=pl.CostEstimate(flops=9_000_000_000, bytes_accessed=10_000_000, transcendentals=0),
        compiler_params=roomy,
        name="hess",
    )(order, near, other, groups[0][1], groups[0][2], dosage)

    back_z = (at["zl"] - jnp.arange(4)) % 4
    back_y = (at["y"] - jnp.arange(4)) % 4
    places = (back_z[None, :] * 4 + back_y[:, None]).astype(jnp.int32).reshape(16)
    slots = (0, 4, 12, 8, 10)
    spots = [(c * width, slot) for c in range(CHUNKS) for slot in slots]
    pieces = [piece for group in groups for piece in group]
    rest = (dosage, fac, inverse, proj)
    out = finish(places, spots[:8], pieces[:8], (score0, score1, score2), *rest, None, width, panel)
    return finish(places, spots[8:], pieces[8:], (), *rest, out, width, panel)


def solution(mesh):
    fine = Mesh(mesh.devices.reshape(2, 4, 2, 4, 4), SAMP + COLS)
    placed = (P(SAMP, COLS), P(COLS, None), P(None, COLS))
    return jax.shard_map(body, mesh=fine, in_specs=placed, out_specs=P(None, SAMP, None, COLS), check_vma=False)
```

time: 198 us -> 191 us (0.965)
  the two profiles are of different devices: /device:TPU:64 before, /device:TPU:32 now
where the time goes in v2:
time: 191 us
  waiting for transfers between devices  71.6 us (37%)
  Pallas kernels  50.1 us (26%)
  starting transfers between devices  45.1 us (24%)
  local copies, waits for them, and re-layouts  20.8 us (11%)
    ppermute x19, waiting for transfers between devices, cycle(): lax.ppermute(array, axis, [(i, (i + by) % size) for i in range(size)])  44.4 us
    pallas_call x2, Pallas kernels, finish(): pl.pallas_call(functools.partial(finish_kernel, float(samples) ** (-0.5),...  26.1 us
    ppermute x19, starting transfers between devices, cycle(): lax.ppermute(array, axis, [(i, (i + by) % size) for i in range(size)])  23.7 us
    all_to_all x1, waiting for transfers between devices, body(): lax.all_to_all(flipped.reshape(n_samp, panel, samples), SAMP, 0, 0, tiled...  20.3 us
    unnamed x28, local copies, waits for them, and re-layouts  16.6 us
    pallas_call x1, Pallas kernels, body(): pl.pallas_call(hess_kernel, out_shape=(jax.ShapeDtypeStruct((k, all_sampl...  13 us
    pallas_call x1, Pallas kernels, body(): pl.pallas_call(factor_kernel, out_shape=(jax.ShapeDtypeStruct((k, samples...  11 us
    all_to_all x1, starting transfers between devices, body(): lax.all_to_all(both.reshape(n_cols, k // n_cols, samples + k), COLS, 0, 0...  8.65 us
  transfers between devices with their start and end apart: 22, of which 9 were waited for; matrix products, arithmetic and copies ran while one was open for 7% of the time, Pallas kernels for 22%

profile of v2, /device:TPU:32, one launch (start us, length us, event | category | flops | bytes accessed | tf_op | source)
XLA Modules:
  0.0 190.5 jit_solution(12260347120057985483)
XLA Ops:
  0.0 0.9 copy-done
  1.0 0.3 fusion.15
  1.2 1.4 fusion.14
  2.6 0.7 maximum_bitcast_fusion
  3.3 8.7 %all-to-all-start.1 = ((f32[16,8,384]{2,1,0:T(8,128)}), f32[16,8,384]{2,1,0:T(8,128)S(1)}, u32[]{:S(2)}, u32[]{:S(2)}) async-start(f32[16,8,384]{2,1,0:T(8,128)} %maximum_bitcast_fusion), calls=%async_computation.1 | async-start | bytes 393216 | tf_op jit(solution)/shard_map/all_to_all | solution.py:232
  11.9 1.0 copy.7
  12.9 7.0 %all-to-all-done.1 = f32[16,8,384]{2,1,0:T(8,128)S(1)} async-done(((f32[16,8,384]{2,1,0:T(8,128)}), f32[16,8,384]{2,1,0:T(8,128)S(1)}, u32[]{:S(2)}, u32[]{:S(2)}) %all-to-all-start.1) | async-done | bytes 196640 | tf_op jit(solution)/shard_map/all_to_all | solution.py:232
  19.9 8.3 %all-to-all-start = ((bf16[16,64,256]{2,1,0:T(8,128)(2,1)}), bf16[16,64,256]{2,1,0:T(8,128)(2,1)S(1)}, u32[]{:S(2)}, u32[]{:S(2)}) async-start(bf16[16,64,256]{2,1,0:T(8,128)(2,1)} %bitcast.1), calls=%async_computation | async-start | bytes 1048576 | tf_op jit(solution)/shard_map/all_to_all | solution.py:222
  28.3 20.3 %all-to-all-done = bf16[16,64,256]{2,1,0:T(8,128)(2,1)S(1)} async-done(((bf16[16,64,256]{2,1,0:T(8,128)(2,1)}), bf16[16,64,256]{2,1,0:T(8,128)(2,1)S(1)}, u32[]{:S(2)}, u32[]{:S(2)}) %all-to-all-start) | async-done | bytes 524320 | tf_op jit(solution)/shard_map/all_to_all | solution.py:222
  48.6 0.7 broadcast_in_dim.2
  49.3 4.3 %all-to-all-start.2 = ((f32[16,8,384]{2,1,0:T(8,128)}), f32[16,8,384]{2,1,0:T(8,128)S(1)}, u32[]{:S(2)}, u32[]{:S(2)}) async-start(f32[16,8,384]{2,1,0:T(8,128)} %broadcast_in_dim.2), calls=%async_computation.2 | async-start | bytes 393216 | tf_op jit(solution)/shard_map/all_to_all | solution.py:234
  53.7 0.7 constant_dynamic-update-slice_fusion.7
  54.4 1.5 collective-permute-start.7
  55.9 1.0 collective-permute-start.8
  56.9 1.9 %collective-permute-start.9 = (bf16[32,4096]{1,0:T(8,128)(2,1)S(1)}, bf16[32,4096]{1,0:T(8,128)(2,1)S(1)}, u32[]{:S(2)}, u32[]{:S(2)}) collective-permute-start(bf16[32,4096]{1,0:T(8,128)(2,1)S(1)} %bitcast.33), channel_id=1, source_target_pairs={{0,12},{4,0},{8,4},{12,8},{1,13},{5,1},{9,5},{13,9},{2,14},{6,2},{... | collective-permute-start | bytes 786440 | tf_op jit(solution)/shard_map/ppermute | solution.py:24
  58.8 0.2 collective-permute-start
  59.0 3.7 %collective-permute-start.1 = (bf16[32,4096]{1,0:T(8,128)(2,1)S(1)}, bf16[32,4096]{1,0:T(8,128)(2,1)S(1)}, u32[]{:S(2)}, u32[]{:S(2)}) collective-permute-start(bf16[32,4096]{1,0:T(8,128)(2,1)S(1)} %bitcast.27), channel_id=1, source_target_pairs={{0,8},{4,12},{8,0},{12,4},{1,9},{5,13},{9,1},{13,5},{2,10},{6,14},... | collective-permute-start | bytes 786440 | tf_op jit(solution)/shard_map/ppermute | solution.py:24
  62.7 0.7 constant_dynamic-update-slice_fusion.3
  63.4 11.2 %collective-permute-done.7 = bf16[32,4096]{1,0:T(8,128)(2,1)S(1)} collective-permute-done((bf16[32,4096]{1,0:T(8,128)(2,1)S(1)}, bf16[32,4096]{1,0:T(8,128)(2,1)S(1)}, u32[]{:S(2)}, u32[]{:S(2)}) %collective-permute-start.7) | collective-permute-done | bytes 262176 | tf_op jit(solution)/shard_map/ppermute | solution.py:24
  74.6 0.7 constant_dynamic-update-slice_fusion.6
  75.4 16.3 %collective-permute-done.8 = bf16[32,4096]{1,0:T(8,128)(2,1)S(1)} collective-permute-done((bf16[32,4096]{1,0:T(8,128)(2,1)S(1)}, bf16[32,4096]{1,0:T(8,128)(2,1)S(1)}, u32[]{:S(2)}, u32[]{:S(2)}) %collective-permute-start.8) | collective-permute-done | bytes 262176 | tf_op jit(solution)/shard_map/ppermute | solution.py:24
  91.6 0.7 constant_dynamic-update-slice_fusion.5
  92.3 1.6 collective-permute-done.9
  94.0 0.7 constant_dynamic-update-slice_fusion.4.rows.refs_0_
  94.7 1.5 collective-permute-start.15
  96.1 1.8 collective-permute-start.16
  97.9 0.0 all-to-all-done.2
  97.9 3.4 %copy-done.1 = bf16[4096,1024]{1,0:T(8,128)(2,1)S(1)} copy-done((bf16[4096,1024]{1,0:T(8,128)(2,1)S(1)}, bf16[4096,1024]{1,0:T(8,128)(2,1)}, u32[]{:S(2)}) %copy-start.1) | copy-done | bytes 8388632
  101.3 11.0 %factor.1 = (bf16[128,256]{1,0:T(8,128)(2,1)S(1)}, f32[128,1024]{1,0:T(8,128)S(1)}) custom-call(f32[128,384]{1,0:T(8,128)S(1)} %bitcast.24, bf16[128,4096]{1,0:T(8,128)(2,1)} %constant_dynamic-update-slice_fusion.4.rows.refs_0_, bf16[4096,1024]{1,0:T(8,128)(2,1)S(1)} %copy-done.1), custom_call_target="tpu_custom_call" | custom-call | flops 7000000000 | bytes 400000 | tf_op jit(solution)/shard_map/factor/pallas_call | solution.py:249
  112.4 0.7 collective-permute-start.10
  113.1 1.7 constant_dynamic-update-slice_fusion.2
  114.7 0.0 collective-permute-done.1
  114.7 0.7 constant_dynamic-update-slice_fusion.1
  115.4 0.0 collective-permute-done.2
  115.4 0.7 constant_dynamic-update-slice_fusion.refs_5_
  116.2 0.3 collective-permute-start.3
  116.4 3.0 %collective-permute-start.5 = (bf16[128,4096]{1,0:T(8,128)(2,1)}, bf16[128,4096]{1,0:T(8,128)(2,1)}, u32[]{:S(2)}, u32[]{:S(2)}) collective-permute-start(bf16[128,4096]{1,0:T(8,128)(2,1)} %constant_dynamic-update-slice_fusion.refs_5_), channel_id=1, source_target_pairs={{0,3},{1,0},{2,1},{3,2},{4,7},{5,4},{6,5},{7,6},{8,11},{9,8},{10,9... | collective-permute-start | bytes 3145736 | tf_op jit(solution)/shard_map/ppermute | solution.py:24
  119.4 1.2 collective-permute-done.10
  120.6 0.1 collective-permute-start.11
  120.7 0.6 constant_dynamic-update-slice_fusion.12
  121.4 5.8 %collective-permute-done.11 = bf16[2,128,256]{2,1,0:T(8,128)(2,1)S(1)} collective-permute-done((bf16[2,128,256]{2,1,0:T(8,128)(2,1)S(1)}, bf16[2,128,256]{2,1,0:T(8,128)(2,1)S(1)}, u32[]{:S(2)}, u32[]{:S(2)}) %collective-permute-start.11) | collective-permute-done | bytes 131104 | tf_op jit(solution)/shard_map/ppermute | solution.py:24
  127.2 0.0 collective-permute-start.12
  127.2 0.6 constant_dynamic-update-slice_fusion.11
  127.8 5.8 %collective-permute-done.12 = bf16[2,128,256]{2,1,0:T(8,128)(2,1)S(1)} collective-permute-done((bf16[2,128,256]{2,1,0:T(8,128)(2,1)S(1)}, bf16[2,128,256]{2,1,0:T(8,128)(2,1)S(1)}, u32[]{:S(2)}, u32[]{:S(2)}) %collective-permute-start.12) | collective-permute-done | bytes 131104 | tf_op jit(solution)/shard_map/ppermute | solution.py:24
  133.7 1.2 collective-permute-start.13
  134.9 0.7 constant_dynamic-update-slice_fusion.10
  135.5 0.7 constant_dynamic-update-slice_fusion.9
  136.2 2.4 %collective-permute-done.13 = bf16[2,128,256]{2,1,0:T(8,128)(2,1)S(1)} collective-permute-done((bf16[2,128,256]{2,1,0:T(8,128)(2,1)S(1)}, bf16[2,128,256]{2,1,0:T(8,128)(2,1)S(1)}, u32[]{:S(2)}, u32[]{:S(2)}) %collective-permute-start.13) | collective-permute-done | bytes 131104 | tf_op jit(solution)/shard_map/ppermute | solution.py:24
  138.6 0.7 constant_dynamic-update-slice_fusion.8.near
  139.3 0.0 collective-permute-start.14
  139.3 0.1 broadcast_add_fusion
  139.4 0.1 add.70.places
  139.5 0.0 collective-permute-done.15.ahead.refs_1_
  139.5 0.1 collective-permute-start.17
  139.6 0.0 collective-permute-done.16.behind.refs_2_
  139.7 3.3 %collective-permute-start.18 = (bf16[64,4096]{1,0:T(8,128)(2,1)S(1)}, bf16[64,4096]{1,0:T(8,128)(2,1)S(1)}, u32[]{:S(2)}, u32[]{:S(2)}) collective-permute-start(bf16[64,4096]{1,0:T(8,128)(2,1)S(1)} %slice.37), channel_id=1, source_target_pairs={{0,3},{1,0},{2,1},{3,2},{4,7},{5,4},{6,5},{7,6},{8,11},{9,8},{10,9... | collective-permute-start | bytes 1572872 | tf_op jit(solution)/shard_map/ppermute | solution.py:24
  143.0 0.1 collective-permute-start.4
  143.1 1.1 slice.34
  144.3 3.5 %collective-permute-start.6 = (bf16[64,4096]{1,0:T(8,128)(2,1)S(1)}, bf16[64,4096]{1,0:T(8,128)(2,1)S(1)}, u32[]{:S(2)}, u32[]{:S(2)}) collective-permute-start(bf16[64,4096]{1,0:T(8,128)(2,1)S(1)} %slice.34), channel_id=1, source_target_pairs={{0,3},{1,0},{2,1},{3,2},{4,7},{5,4},{6,5},{7,6},{8,11},{9,8},{10,9... | collective-permute-start | bytes 1572872 | tf_op jit(solution)/shard_map/ppermute | solution.py:24
  147.8 3.4 %copy-done.2 = bf16[4096,1024]{1,0:T(8,128)(2,1)S(1)} copy-done((bf16[4096,1024]{1,0:T(8,128)(2,1)S(1)}, bf16[4096,1024]{1,0:T(8,128)(2,1)}, u32[]{:S(2)}) %copy-start.2) | copy-done | bytes 8388632
  151.2 13.0 %hess.1 = (bf16[128,4096]{1,0:T(8,128)(2,1)S(1)}, f32[128,128]{1,0:T(8,128)S(1)}, bf16[256,1024]{1,0:T(8,128)(2,1)S(1)}, f32[128,1024]{1,0:T(8,128)S(1)}, f32[128,1024]{1,0:T(8,128)S(1)}) custom-call(s32[16]{0:T(128)S(1)} %fusion.places, bf16[8,128,256]{2,1,0:T(8,128)(2,1)} %constant_dynamic-update-slice_fusion.8.near, ...), custom_call_target="tpu_custom_call" | custom-call | flops 8999999488 | bytes 10000000 | tf_op jit(solution)/shard_map/hess/pallas_call | solution.py:267
  164.2 0.0 slice-start
  164.2 18.4 %shard_map.37.refs_6_ = bf16[16,1,64,1024]{3,2,1,0:T(8,128)(2,1)} custom-call(s32[16]{0:T(128)S(1)} %add.70.places, bf16[128,4096]{1,0:T(8,128)(2,1)} %constant_dynamic-update-slice_fusion.4.rows.refs_0_, bf16[128,4096]{1,0:T(8,128)(2,1)S(1)} %collective-permute-done.15.ahead.refs_1_, bf16[128,4096]{1,0:T(8,128)(2,1)S(1)} %collective-permute-done.16.behind.refs_2_, ...), custom_call_target="tpu_custom_call" | custom-call | flops 7516192768 | bytes 14680064 | tf_op jit(solution)/shard_map/pallas_call | solution.py:193
  182.6 7.7 %shard_map.38 = bf16[16,1,64,1024]{3,2,1,0:T(8,128)(2,1)} custom-call(s32[16]{0:T(128)S(1)} %add.70.places, bf16[64,4096]{1,0:T(8,128)(2,1)S(1)} %collective-permute-done.4.refs_0_, bf16[64,4096]{1,0:T(8,128)(2,1)S(1)} %collective-permute-done.6.refs_1_, bf16[4096,1024]{1,0:T(8,128)(2,1)S(1)} %bitcast.22, ...), custom_call_target="tpu_custom_call", output_to_operand_aliasing={{}: (7, {})} | custom-call | flops 1073741824 | bytes 2097152 | tf_op jit(solution)/shard_map/pallas_call | solution.py:193
  (32 shorter events, 0.3 us)
Async XLA Ops:
  0.0 1.0 copy-start
  0.0 11.9 %copy-start.5 = (bf16[256,1024]{1,0:T(8,128)(2,1)S(1)}, bf16[256,1024]{1,0:T(8,128)(2,1)}, u32[]{:S(2)}) copy-start(bf16[256,1024]{1,0:T(8,128)(2,1)} %param.3) | copy-start | bytes 1572868
  3.3 16.6 %all-to-all-start.1 = ((f32[16,8,384]{2,1,0:T(8,128)}), f32[16,8,384]{2,1,0:T(8,128)S(1)}, u32[]{:S(2)}, u32[]{:S(2)}) async-start(f32[16,8,384]{2,1,0:T(8,128)} %maximum_bitcast_fusion), calls=%async_computation.1 | async-start | bytes 393216 | tf_op jit(solution)/shard_map/all_to_all | solution.py:232
  19.9 28.7 %all-to-all-start = ((bf16[16,64,256]{2,1,0:T(8,128)(2,1)}), bf16[16,64,256]{2,1,0:T(8,128)(2,1)S(1)}, u32[]{:S(2)}, u32[]{:S(2)}) async-start(bf16[16,64,256]{2,1,0:T(8,128)(2,1)} %bitcast.1), calls=%async_computation | async-start | bytes 1048576 | tf_op jit(solution)/shard_map/all_to_all | solution.py:222
  49.3 48.6 %all-to-all-start.2 = ((f32[16,8,384]{2,1,0:T(8,128)}), f32[16,8,384]{2,1,0:T(8,128)S(1)}, u32[]{:S(2)}, u32[]{:S(2)}) async-start(f32[16,8,384]{2,1,0:T(8,128)} %broadcast_in_dim.2), calls=%async_computation.2 | async-start | bytes 393216 | tf_op jit(solution)/shard_map/all_to_all | solution.py:234
  54.4 20.2 %collective-permute-start.7 = (bf16[32,4096]{1,0:T(8,128)(2,1)S(1)}, bf16[32,4096]{1,0:T(8,128)(2,1)S(1)}, u32[]{:S(2)}, u32[]{:S(2)}) collective-permute-start(bf16[32,4096]{1,0:T(8,128)(2,1)S(1)} %bitcast.31), channel_id=1, source_target_pairs={{0,4},{4,8},{8,12},{12,0},{1,5},{5,9},{9,13},{13,1},{2,6},{6,10},{... | collective-permute-start | bytes 786440 | tf_op jit(solution)/shard_map/ppermute | solution.py:24
  55.9 35.7 %collective-permute-start.8 = (bf16[32,4096]{1,0:T(8,128)(2,1)S(1)}, bf16[32,4096]{1,0:T(8,128)(2,1)S(1)}, u32[]{:S(2)}, u32[]{:S(2)}) collective-permute-start(bf16[32,4096]{1,0:T(8,128)(2,1)S(1)} %bitcast.32), channel_id=1, source_target_pairs={{0,8},{4,12},{8,0},{12,4},{1,9},{5,13},{9,1},{13,5},{2,10},{6,14},... | collective-permute-start | bytes 786440 | tf_op jit(solution)/shard_map/ppermute | solution.py:24
  56.9 37.1 %collective-permute-start.9 = (bf16[32,4096]{1,0:T(8,128)(2,1)S(1)}, bf16[32,4096]{1,0:T(8,128)(2,1)S(1)}, u32[]{:S(2)}, u32[]{:S(2)}) collective-permute-start(bf16[32,4096]{1,0:T(8,128)(2,1)S(1)} %bitcast.33), channel_id=1, source_target_pairs={{0,12},{4,0},{8,4},{12,8},{1,13},{5,1},{9,5},{13,9},{2,14},{6,2},{... | collective-permute-start | bytes 786440 | tf_op jit(solution)/shard_map/ppermute | solution.py:24
  58.8 53.5 %collective-permute-start = (bf16[32,4096]{1,0:T(8,128)(2,1)S(1)}, bf16[32,4096]{1,0:T(8,128)(2,1)}, u32[]{:S(2)}, u32[]{:S(2)}) collective-permute-start(bf16[32,4096]{1,0:T(8,128)(2,1)S(1)} %bitcast.26), channel_id=1, source_target_pairs={{0,4},{4,8},{8,12},{12,0},{1,5},{5,9},{9,13},{13,1},{2,6},{6,10},{... | collective-permute-start | bytes 786440 | tf_op jit(solution)/shard_map/ppermute | solution.py:24
  59.0 55.7 %collective-permute-start.1 = (bf16[32,4096]{1,0:T(8,128)(2,1)S(1)}, bf16[32,4096]{1,0:T(8,128)(2,1)S(1)}, u32[]{:S(2)}, u32[]{:S(2)}) collective-permute-start(bf16[32,4096]{1,0:T(8,128)(2,1)S(1)} %bitcast.27), channel_id=1, source_target_pairs={{0,8},{4,12},{8,0},{12,4},{1,9},{5,13},{9,1},{13,5},{2,10},{6,14},... | collective-permute-start | bytes 786440 | tf_op jit(solution)/shard_map/ppermute | solution.py:24
  74.6 40.8 %collective-permute-start.2 = (bf16[32,4096]{1,0:T(8,128)(2,1)S(1)}, bf16[32,4096]{1,0:T(8,128)(2,1)S(1)}, u32[]{:S(2)}, u32[]{:S(2)}) collective-permute-start(bf16[32,4096]{1,0:T(8,128)(2,1)S(1)} %bitcast.29), channel_id=1, source_target_pairs={{0,12},{4,0},{8,4},{12,8},{1,13},{5,1},{9,5},{13,9},{2,14},{6,2},{... | collective-permute-start | bytes 786440 | tf_op jit(solution)/shard_map/ppermute | solution.py:24
  94.7 44.8 %collective-permute-start.15 = (bf16[128,4096]{1,0:T(8,128)(2,1)}, bf16[128,4096]{1,0:T(8,128)(2,1)S(1)}, u32[]{:S(2)}, u32[]{:S(2)}) collective-permute-start(bf16[128,4096]{1,0:T(8,128)(2,1)} %constant_dynamic-update-slice_fusion.4.rows.refs_0_), channel_id=1, source_target_pairs={{0,1},{1,2},{2,3},{3,0},{4,5},{5,6},{6,7},{7,4},{8,9},{9,10},{10,1... | collective-permute-start | bytes 3145736 | tf_op jit(solution)/shard_map/ppermute | solution.py:24
  96.1 43.5 %collective-permute-start.16 = (bf16[128,4096]{1,0:T(8,128)(2,1)}, bf16[128,4096]{1,0:T(8,128)(2,1)S(1)}, u32[]{:S(2)}, u32[]{:S(2)}) collective-permute-start(bf16[128,4096]{1,0:T(8,128)(2,1)} %constant_dynamic-update-slice_fusion.4.rows.refs_0_), channel_id=1, source_target_pairs={{0,3},{1,0},{2,1},{3,2},{4,7},{5,4},{6,5},{7,6},{8,11},{9,8},{10,9... | collective-permute-start | bytes 3145736 | tf_op jit(solution)/shard_map/ppermute | solution.py:24
  97.9 3.4 %copy-start.1 = (bf16[4096,1024]{1,0:T(8,128)(2,1)S(1)}, bf16[4096,1024]{1,0:T(8,128)(2,1)}, u32[]{:S(2)}) copy-start(bf16[4096,1024]{1,0:T(8,128)(2,1)} %refs_2_.1) | copy-start | bytes 25165828
  112.3 9.0 %copy-start.3 = (f32[128,1024]{1,0:T(8,128)}, f32[128,1024]{1,0:T(8,128)S(1)}, u32[]{:S(2)}) copy-start(f32[128,1024]{1,0:T(8,128)S(1)} %get-tuple-element.16.refs_8_) | copy-start | bytes 1572868
  112.4 8.3 %collective-permute-start.10 = (bf16[128,256]{1,0:T(8,128)(2,1)S(1)}, bf16[128,256]{1,0:T(8,128)(2,1)S(1)}, u32[]{:S(2)}, u32[]{:S(2)}) collective-permute-start(bf16[128,256]{1,0:T(8,128)(2,1)S(1)} %get-tuple-element.12), channel_id=1, source_target_pairs={{0,128},{128,0},{1,129},{129,1},{2,130},{130,2},{3,131},{131,3},{4... | collective-permute-start | bytes 196616 | tf_op jit(solution)/shard_map/ppermute | solution.py:24
  116.2 26.8 %collective-permute-start.3 = (bf16[128,4096]{1,0:T(8,128)(2,1)}, bf16[128,4096]{1,0:T(8,128)(2,1)S(1)}, u32[]{:S(2)}, u32[]{:S(2)}) collective-permute-start(bf16[128,4096]{1,0:T(8,128)(2,1)} %constant_dynamic-update-slice_fusion.refs_5_), channel_id=1, source_target_pairs={{0,1},{1,2},{2,3},{3,0},{4,5},{5,6},{6,7},{7,4},{8,9},{9,10},{10,1... | collective-permute-start | bytes 3145736 | tf_op jit(solution)/shard_map/ppermute | solution.py:24
  116.4 26.7 %collective-permute-start.5 = (bf16[128,4096]{1,0:T(8,128)(2,1)}, bf16[128,4096]{1,0:T(8,128)(2,1)}, u32[]{:S(2)}, u32[]{:S(2)}) collective-permute-start(bf16[128,4096]{1,0:T(8,128)(2,1)} %constant_dynamic-update-slice_fusion.refs_5_), channel_id=1, source_target_pairs={{0,3},{1,0},{2,1},{3,2},{4,7},{5,4},{6,5},{7,6},{8,11},{9,8},{10,9... | collective-permute-start | bytes 3145736 | tf_op jit(solution)/shard_map/ppermute | solution.py:24
  120.6 6.5 %collective-permute-start.11 = (bf16[2,128,256]{2,1,0:T(8,128)(2,1)S(1)}, bf16[2,128,256]{2,1,0:T(8,128)(2,1)S(1)}, u32[]{:S(2)}, u32[]{:S(2)}) collective-permute-start(bf16[2,128,256]{2,1,0:T(8,128)(2,1)S(1)} %pad_maximum_fusion), channel_id=1, source_target_pairs={{0,32},{32,64},{64,96},{96,0},{1,33},{33,65},{65,97},{97,1},{2,34}... | collective-permute-start | bytes 393224 | tf_op jit(solution)/shard_map/ppermute | solution.py:24
  127.2 6.5 %collective-permute-start.12 = (bf16[2,128,256]{2,1,0:T(8,128)(2,1)S(1)}, bf16[2,128,256]{2,1,0:T(8,128)(2,1)S(1)}, u32[]{:S(2)}, u32[]{:S(2)}) collective-permute-start(bf16[2,128,256]{2,1,0:T(8,128)(2,1)S(1)} %pad_maximum_fusion), channel_id=1, source_target_pairs={{0,64},{32,96},{64,0},{96,32},{1,65},{33,97},{65,1},{97,33},{2,66}... | collective-permute-start | bytes 393224 | tf_op jit(solution)/shard_map/ppermute | solution.py:24
  133.7 5.0 %collective-permute-start.13 = (bf16[2,128,256]{2,1,0:T(8,128)(2,1)S(1)}, bf16[2,128,256]{2,1,0:T(8,128)(2,1)S(1)}, u32[]{:S(2)}, u32[]{:S(2)}) collective-permute-start(bf16[2,128,256]{2,1,0:T(8,128)(2,1)S(1)} %pad_maximum_fusion), channel_id=1, source_target_pairs={{0,96},{32,0},{64,32},{96,64},{1,97},{33,1},{65,33},{97,65},{2,98}... | collective-permute-start | bytes 393224 | tf_op jit(solution)/shard_map/ppermute | solution.py:24
  139.3 8.5 %collective-permute-start.14 = (bf16[8,128,256]{2,1,0:T(8,128)(2,1)}, bf16[8,128,256]{2,1,0:T(8,128)(2,1)}, u32[]{:S(2)}, u32[]{:S(2)}) collective-permute-start(bf16[8,128,256]{2,1,0:T(8,128)(2,1)} %constant_dynamic-update-slice_fusion.8.near), channel_id=1, source_target_pairs={{0,16},{16,0},{1,17},{17,1},{2,18},{18,2},{3,19},{19,3},{4,20},{20... | collective-permute-start | bytes 1572872 | tf_op jit(solution)/shard_map/ppermute | solution.py:24
  139.5 24.6 %collective-permute-start.17 = (bf16[64,4096]{1,0:T(8,128)(2,1)S(1)}, bf16[64,4096]{1,0:T(8,128)(2,1)S(1)}, u32[]{:S(2)}, u32[]{:S(2)}) collective-permute-start(bf16[64,4096]{1,0:T(8,128)(2,1)S(1)} %slice.36), channel_id=1, source_target_pairs={{0,1},{1,2},{2,3},{3,0},{4,5},{5,6},{6,7},{7,4},{8,9},{9,10},{10,1... | collective-permute-start | bytes 1572872 | tf_op jit(solution)/shard_map/ppermute | solution.py:24
  139.7 24.5 %collective-permute-start.18 = (bf16[64,4096]{1,0:T(8,128)(2,1)S(1)}, bf16[64,4096]{1,0:T(8,128)(2,1)S(1)}, u32[]{:S(2)}, u32[]{:S(2)}) collective-permute-start(bf16[64,4096]{1,0:T(8,128)(2,1)S(1)} %slice.37), channel_id=1, source_target_pairs={{0,3},{1,0},{2,1},{3,2},{4,7},{5,4},{6,5},{7,6},{8,11},{9,8},{10,9... | collective-permute-start | bytes 1572872 | tf_op jit(solution)/shard_map/ppermute | solution.py:24
  143.0 39.6 %collective-permute-start.4 = (bf16[64,4096]{1,0:T(8,128)(2,1)S(1)}, bf16[64,4096]{1,0:T(8,128)(2,1)S(1)}, u32[]{:S(2)}, u32[]{:S(2)}) collective-permute-start(bf16[64,4096]{1,0:T(8,128)(2,1)S(1)} %slice.33), channel_id=1, source_target_pairs={{0,1},{1,2},{2,3},{3,0},{4,5},{5,6},{6,7},{7,4},{8,9},{9,10},{10,1... | collective-permute-start | bytes 1572872 | tf_op jit(solution)/shard_map/ppermute | solution.py:24
  143.1 21.1 %copy-start.4 = (f32[128,1024]{1,0:T(8,128)S(1)}, f32[128,1024]{1,0:T(8,128)}, u32[]{:S(2)}) copy-start(f32[128,1024]{1,0:T(8,128)} %copy-done.3) | copy-start | bytes 1572868
  144.3 38.3 %collective-permute-start.6 = (bf16[64,4096]{1,0:T(8,128)(2,1)S(1)}, bf16[64,4096]{1,0:T(8,128)(2,1)S(1)}, u32[]{:S(2)}, u32[]{:S(2)}) collective-permute-start(bf16[64,4096]{1,0:T(8,128)(2,1)S(1)} %slice.34), channel_id=1, source_target_pairs={{0,3},{1,0},{2,1},{3,2},{4,7},{5,4},{6,5},{7,6},{8,11},{9,8},{10,9... | collective-permute-start | bytes 1572872 | tf_op jit(solution)/shard_map/ppermute | solution.py:24
  147.8 3.4 %copy-start.2 = (bf16[4096,1024]{1,0:T(8,128)(2,1)S(1)}, bf16[4096,1024]{1,0:T(8,128)(2,1)}, u32[]{:S(2)}) copy-start(bf16[4096,1024]{1,0:T(8,128)(2,1)} %refs_2_.1) | copy-start | bytes 25165828
  164.2 18.4 %slice-start = ((s8[8388608]{0:T(1024)(128)(4,1)}), s8[4194304]{0:T(1024)(128)(4,1)S(1)}, s32[]{:S(2)}) async-start(s8[8388608]{0:T(1024)(128)(4,1)} %bitcast.21), calls=%async_computation.3 | async-start | bytes 8388608
  164.2 18.4 %slice-start.1 = ((s8[8388608]{0:T(1024)(128)(4,1)}), s8[4194304]{0:T(1024)(128)(4,1)S(1)}, s32[]{:S(2)}) async-start(s8[8388608]{0:T(1024)(128)(4,1)} %bitcast.21), calls=%async_computation.4 | async-start | bytes 8388608

commit v3 on v2

--- a/solution.py
+++ b/solution.py
@@ -134,43 +134,50 @@
     proj[k:, :] = (found - high.astype(F32)).astype(BF16)
 
 
-def finish_kernel(scale, genes, spots, given, places, *refs):
+def finish_kernel(scale, genes, spots, sizes, given, places, *refs):
     count = len(spots)
     pieces, scores = refs[:count], refs[count : count + given]
     dos, fac, inverse, proj = refs[count + given : count + given + 4]
-    out, done, coef, sems = refs[-4:]
+    out, held, done, coef, loads, sems = refs[-6:]
     n = pl.program_id(0)
+    spans = [(sum(sizes[:i]), size) for i, size in enumerate(sizes)]
+    known = sum(sizes[:given])
 
     @pl.when(n == 0)
     def _():
-        at = 0
-        for piece in pieces:
-            cross = lax.dot_general(piece[...], fac[...], NT, preferred_element_type=F32)
+        copies = [
+            pltpu.make_async_copy(piece, held.at[pl.ds(at, size), :], loads.at[i])
+            for i, (piece, (at, size)) in enumerate(zip(pieces, spans))
+        ]
+        for copy in copies:
+            copy.start()
+        for copy, (at, size) in zip(copies, spans):
+            copy.wait()
+            cross = lax.dot_general(held[pl.ds(at, size), :], fac[...], NT, preferred_element_type=F32)
             half = jnp.dot(cross, inverse[...], preferred_element_type=F32, precision=HI).astype(BF16)
-            coef[pl.ds(at, piece.shape[0]), :] = jnp.concatenate([half, half], axis=1)
-            at += piece.shape[0]
-
-    at = 0
-    for i, piece in enumerate(pieces):
-        rows = pl.ds(at, piece.shape[0])
-        total = scores[i][...] if i < given else jnp.dot(piece[...], dos[...], preferred_element_type=F32)
-        total -= jnp.dot(coef[rows, :], proj[...], preferred_element_type=F32)
-        done[rows, pl.ds(pl.multiple_of(n * TILE, TILE), TILE)] = (total * scale).astype(BF16)
-        at += piece.shape[0]
+            coef[pl.ds(at, size), :] = jnp.concatenate([half, half], axis=1)
+
+    column = pl.ds(pl.multiple_of(n * TILE, TILE), TILE)
+    for score, (at, size) in zip(scores, spans):
+        rows = pl.ds(at, size)
+        total = score[...] - jnp.dot(coef[rows, :], proj[...], preferred_element_type=F32)
+        done[rows, column] = (total * scale).astype(BF16)
+    total = jnp.dot(held[known:, :], dos[...], preferred_element_type=F32)
+    total -= jnp.dot(coef[known:, :], proj[...], preferred_element_type=F32)
+    done[known:, column] = (total * scale).astype(BF16)
 
     @pl.when(n == pl.num_programs(0) - 1)
     def _():
-        copies, at = [], 0
-        for (start, slot), piece in zip(spots, pieces):
-            for i in range(piece.shape[0] // genes):
+        copies = []
+        for (start, slot), (at, size) in zip(spots, spans):
+            for i in range(size // genes):
                 copies.append(
                     pltpu.make_async_copy(
-                        done.at[pl.ds(at, genes), :],
+                        done.at[pl.ds(at + i * genes, genes), :],
                         out.at[places[slot + i], 0, pl.ds(start, genes), :],
-                        sems.at[at // genes],
+                        sems.at[at // genes + i],
                     )
                 )
-                at += genes
         for copy in copies:
             copy.start()
         for copy in copies:
@@ -179,34 +186,37 @@
 
 def finish(places, spots, pieces, scores, dosage, fac, inverse, proj, out, genes, panel):
     samples, snps = dosage.shape
-    rows = sum(p.shape[0] for p in pieces)
+    sizes = tuple(p.shape[0] for p in pieces)
+    rows = sum(sizes)
     fixed = lambda a: pl.BlockSpec(a.shape, lambda n, _: (0, 0), pipeline_mode=pl.Buffered(1))
     across = lambda a: pl.BlockSpec((a.shape[0], TILE), lambda n, _: (0, n))
+    left = pl.BlockSpec(memory_space=pl.ANY)
     ins = list(pieces) + list(scores) + [dosage, fac, inverse, proj]
-    specs = [fixed(a) for a in pieces] + [across(a) for a in scores]
+    specs = [left for _ in pieces] + [across(a) for a in scores]
     specs += [across(dosage), fixed(fac), fixed(inverse), across(proj)]
     alias = {}
     if out is not None:
         alias = {len(ins) + 1: 0}
         ins.append(out)
-        specs.append(pl.BlockSpec(memory_space=pl.ANY))
+        specs.append(left)
     return pl.pallas_call(
-        functools.partial(finish_kernel, float(samples) ** -0.5, genes, spots, len(scores)),
+        functools.partial(finish_kernel, float(samples) ** -0.5, genes, spots, sizes, len(scores)),
         out_shape=jax.ShapeDtypeStruct((16, 1, panel, snps), BF16),
         grid_spec=pltpu.PrefetchScalarGridSpec(
             num_scalar_prefetch=1,
             grid=(snps // TILE,),
             in_specs=specs,
-            out_specs=pl.BlockSpec(memory_space=pl.ANY),
+            out_specs=left,
             scratch_shapes=[
+                pltpu.VMEM((rows, samples), BF16),
                 pltpu.VMEM((rows, snps), BF16),
                 pltpu.VMEM((rows, proj.shape[0]), BF16),
+                pltpu.SemaphoreType.DMA((len(pieces),)),
                 pltpu.SemaphoreType.DMA((rows // genes,)),
             ],
         ),
         input_output_aliases=alias,
         cost_estimate=pl.CostEstimate(flops=2 * rows * samples * 1024, bytes_accessed=rows * 16384, transcendentals=0),
-        compiler_params=pltpu.CompilerParams(vmem_limit_bytes=36 << 20),
     )(places, *ins)
 
 
@@ -236,7 +246,8 @@
     groups = []
     for c in range(CHUNKS):
         piece = mine[c * width : c * width + width]
-        own = jnp.concatenate([piece] + [cycle(piece, "zl", by) for by in (1, 2, 3)])
+        along = [piece] + [cycle(piece, "zl", by) for by in (1, 2, 3)]
+        own = jnp.concatenate(along)
         ahead, behind = cycle(own, "y", 1), cycle(own, "y", -1)
         low, high = ahead[: 2 * width], behind[2 * width :]
         low, high = cycle(low, "y", 1), cycle(high, "y", -1)
@@ -245,14 +256,12 @@
     vmem, hbm = pl.BlockSpec(memory_space=pltpu.VMEM), pl.BlockSpec(memory_space=pltpu.HBM)
     table = jax.ShapeDtypeStruct((4 * width, snps), F32)
     tiles = [pltpu.VMEM(dosage.shape, BF16), pltpu.SemaphoreType.DMA((snps // TILE,))]
-    roomy = pltpu.CompilerParams(vmem_limit_bytes=30 << 20)
     factors, score0 = pl.pallas_call(
         factor_kernel,
         out_shape=(jax.ShapeDtypeStruct((k, samples), BF16), table),
         in_specs=[vmem, vmem, hbm],
         scratch_shapes=[pltpu.VMEM((k, k), F32)] + tiles,
         cost_estimate=pl.CostEstimate(flops=7_000_000_000, bytes_accessed=400_000, transcendentals=0),
-        compiler_params=roomy,
         name="factor",
     )(both.reshape(k, samples + k), groups[0][0], dosage)
 
@@ -276,7 +285,6 @@
         in_specs=[pl.BlockSpec(memory_space=pltpu.SMEM), vmem, vmem, vmem, vmem, hbm],
         scratch_shapes=[pltpu.VMEM((k, k), F32), pltpu.VMEM((k, snps), F32)] + tiles,
         cost_estimate=pl.CostEstimate(flops=9_000_000_000, bytes_accessed=10_000_000, transcendentals=0),
-        compiler_params=roomy,
         name="hess",
     )(order, near, other, groups[0][1], groups[0][2], dosage)
 

time: 191 us -> 197 us (1.031)
  Pallas kernels: 50.1 us -> 56.5 us
    unnamed x28 -> x24, local copies, waits for them, and re-layouts: 16.6 us -> 12.1 us
    pallas_call x2, Pallas kernels: 26.1 us -> 28.9 us  [finish(): pl.pallas_call(functools.partial(finish_kernel, float(samples) ** (-0.5),...]
    pallas_call x1, Pallas kernels: 13 us -> 15.3 us  [body(): pl.pallas_call(hess_kernel, out_shape=(jax.ShapeDtypeStruct((k, all_sampl...]
    slice x4, local copies, waits for them, and re-layouts: 1.24 us -> 3.51 us  [body(): low, high = (ahead[:2 * width], behind[2 * width:])]
  transfers between devices with their start and end apart: 22 -> 22, of which waited for: 9 -> 9; matrix products, arithmetic and copies ran while one was open for 7% -> 8% of each run, Pallas kernels for 22% -> 24%
where the time goes in v3:
time: 197 us; the launch traced here: 196 us
  waiting for transfers between devices  71.9 us (36%)
  Pallas kernels  56.5 us (29%)
  starting transfers between devices  44.6 us (23%)
  local copies, waits for them, and re-layouts  19 us (10%)
  other arithmetic  2.15 us (1%)
    ppermute x19, waiting for transfers between devices, cycle(): lax.ppermute(array, axis, [(i, (i + by) % size) for i in range(size)])  44.6 us
    pallas_call x2, Pallas kernels, finish(): pl.pallas_call(functools.partial(finish_kernel, float(samples) ** (-0.5),...  28.9 us
    ppermute x19, starting transfers between devices, cycle(): lax.ppermute(array, axis, [(i, (i + by) % size) for i in range(size)])  23.3 us
    all_to_all x1, waiting for transfers between devices, body(): lax.all_to_all(flipped.reshape(n_samp, panel, samples), SAMP, 0, 0, tiled...  20.3 us
    pallas_call x1, Pallas kernels, body(): pl.pallas_call(hess_kernel, out_shape=(jax.ShapeDtypeStruct((k, all_sampl...  15.3 us
    pallas_call x1, Pallas kernels, body(): pl.pallas_call(factor_kernel, out_shape=(jax.ShapeDtypeStruct((k, samples...  12.3 us
    unnamed x24, local copies, waits for them, and re-layouts  12.1 us
    all_to_all x1, starting transfers between devices, body(): lax.all_to_all(both.reshape(n_cols, k // n_cols, samples + k), COLS, 0, 0...  8.65 us
  transfers between devices with their start and end apart: 22, of which 9 were waited for; matrix products, arithmetic and copies ran while one was open for 8% of the time, Pallas kernels for 24%

profile of v3, /device:TPU:32, one launch (start us, length us, event | category | flops | bytes accessed | tf_op | source)
XLA Modules:
  0.0 196.1 jit_solution(9654341555132765917)
XLA Ops:
  0.0 0.9 copy-done
  1.0 0.3 fusion.15
  1.2 1.4 fusion.14
  2.6 0.7 maximum_bitcast_fusion
  3.3 8.7 %all-to-all-start.1 = ((f32[16,8,384]{2,1,0:T(8,128)}), f32[16,8,384]{2,1,0:T(8,128)S(1)}, u32[]{:S(2)}, u32[]{:S(2)}) async-start(f32[16,8,384]{2,1,0:T(8,128)} %maximum_bitcast_fusion), calls=%async_computation.1 | async-start | bytes 393216 | tf_op jit(solution)/shard_map/all_to_all | solution.py:242
  11.9 1.0 copy.7
  12.9 7.0 %all-to-all-done.1 = f32[16,8,384]{2,1,0:T(8,128)S(1)} async-done(((f32[16,8,384]{2,1,0:T(8,128)}), f32[16,8,384]{2,1,0:T(8,128)S(1)}, u32[]{:S(2)}, u32[]{:S(2)}) %all-to-all-start.1) | async-done | bytes 196640 | tf_op jit(solution)/shard_map/all_to_all | solution.py:242
  19.9 8.3 %all-to-all-start = ((bf16[16,64,256]{2,1,0:T(8,128)(2,1)}), bf16[16,64,256]{2,1,0:T(8,128)(2,1)S(1)}, u32[]{:S(2)}, u32[]{:S(2)}) async-start(bf16[16,64,256]{2,1,0:T(8,128)(2,1)} %bitcast.1), calls=%async_computation | async-start | bytes 1048576 | tf_op jit(solution)/shard_map/all_to_all | solution.py:232
  28.3 20.3 %all-to-all-done = bf16[16,64,256]{2,1,0:T(8,128)(2,1)S(1)} async-done(((bf16[16,64,256]{2,1,0:T(8,128)(2,1)}), bf16[16,64,256]{2,1,0:T(8,128)(2,1)S(1)}, u32[]{:S(2)}, u32[]{:S(2)}) %all-to-all-start) | async-done | bytes 524320 | tf_op jit(solution)/shard_map/all_to_all | solution.py:232
  48.6 0.7 broadcast_in_dim.2
  49.3 4.3 %all-to-all-start.2 = ((f32[16,8,384]{2,1,0:T(8,128)}), f32[16,8,384]{2,1,0:T(8,128)S(1)}, u32[]{:S(2)}, u32[]{:S(2)}) async-start(f32[16,8,384]{2,1,0:T(8,128)} %broadcast_in_dim.2), calls=%async_computation.2 | async-start | bytes 393216 | tf_op jit(solution)/shard_map/all_to_all | solution.py:244
  53.7 0.7 constant_dynamic-update-slice_fusion.7
  54.5 1.5 collective-permute-start.7
  55.9 1.0 collective-permute-start.8
  56.9 1.9 collective-permute-start.9
  58.9 0.2 collective-permute-start
  59.0 3.7 %collective-permute-start.1 = (bf16[32,4096]{1,0:T(8,128)(2,1)S(1)}, bf16[32,4096]{1,0:T(8,128)(2,1)S(1)}, u32[]{:S(2)}, u32[]{:S(2)}) collective-permute-start(bf16[32,4096]{1,0:T(8,128)(2,1)S(1)} %bitcast.23), channel_id=1, source_target_pairs={{0,8},{4,12},{8,0},{12,4},{1,9},{5,13},{9,1},{13,5},{2,10},{6,14},... | collective-permute-start | bytes 786440 | tf_op jit(solution)/shard_map/ppermute | solution.py:24
  62.8 0.7 constant_dynamic-update-slice_fusion.3
  63.5 11.1 %collective-permute-done.7 = bf16[32,4096]{1,0:T(8,128)(2,1)S(1)} collective-permute-done((bf16[32,4096]{1,0:T(8,128)(2,1)S(1)}, bf16[32,4096]{1,0:T(8,128)(2,1)S(1)}, u32[]{:S(2)}, u32[]{:S(2)}) %collective-permute-start.7) | collective-permute-done | bytes 262176 | tf_op jit(solution)/shard_map/ppermute | solution.py:24
  74.6 0.0 collective-permute-start.2
  74.6 0.7 constant_dynamic-update-slice_fusion.6
  75.3 16.3 %collective-permute-done.8 = bf16[32,4096]{1,0:T(8,128)(2,1)S(1)} collective-permute-done((bf16[32,4096]{1,0:T(8,128)(2,1)S(1)}, bf16[32,4096]{1,0:T(8,128)(2,1)S(1)}, u32[]{:S(2)}, u32[]{:S(2)}) %collective-permute-start.8) | collective-permute-done | bytes 262176 | tf_op jit(solution)/shard_map/ppermute | solution.py:24
  91.6 0.7 constant_dynamic-update-slice_fusion.5
  92.3 1.6 collective-permute-done.9
  94.0 0.7 constant_dynamic-update-slice_fusion.4.rows.refs_0_
  94.7 1.5 collective-permute-start.15
  96.1 1.8 collective-permute-start.16
  97.9 0.7 copy-done.5
  98.6 12.3 %factor.1 = (bf16[128,256]{1,0:T(8,128)(2,1)}, f32[128,1024]{1,0:T(8,128)}) custom-call(f32[128,384]{1,0:T(8,128)} %bitcast.32, bf16[128,4096]{1,0:T(8,128)(2,1)} %constant_dynamic-update-slice_fusion.4.rows.refs_0_, bf16[4096,1024]{1,0:T(8,128)(2,1)} %refs_2_.1), custom_call_target="tpu_custom_call" | custom-call | flops 7000000000 | bytes 400000 | tf_op jit(solution)/shard_map/factor/pallas_call | solution.py:259
  110.9 0.7 collective-permute-start.10
  111.6 0.7 constant_dynamic-update-slice_fusion.2
  112.3 0.7 constant_dynamic-update-slice_fusion.1
  113.0 0.0 collective-permute-done.2
  113.0 0.7 constant_dynamic-update-slice_fusion.refs_5_
  113.8 0.3 collective-permute-start.3
  114.0 3.0 %collective-permute-start.5 = (bf16[128,4096]{1,0:T(8,128)(2,1)}, bf16[128,4096]{1,0:T(8,128)(2,1)}, u32[]{:S(2)}, u32[]{:S(2)}) collective-permute-start(bf16[128,4096]{1,0:T(8,128)(2,1)} %constant_dynamic-update-slice_fusion.refs_5_), channel_id=1, source_target_pairs={{0,3},{1,0},{2,1},{3,2},{4,7},{5,4},{6,5},{7,6},{8,11},{9,8},{10,9... | collective-permute-start | bytes 3145736 | tf_op jit(solution)/shard_map/ppermute | solution.py:24
  117.0 2.3 %collective-permute-done.10 = bf16[128,256]{1,0:T(8,128)(2,1)S(1)} collective-permute-done((bf16[128,256]{1,0:T(8,128)(2,1)}, bf16[128,256]{1,0:T(8,128)(2,1)S(1)}, u32[]{:S(2)}, u32[]{:S(2)}) %collective-permute-start.10) | collective-permute-done | bytes 65568 | tf_op jit(solution)/shard_map/ppermute | solution.py:24
  119.3 0.9 pad_maximum_fusion
  120.2 0.1 collective-permute-start.11
  120.3 1.5 constant_dynamic-update-slice_fusion.12
  121.8 5.0 %collective-permute-done.11 = bf16[2,128,256]{2,1,0:T(8,128)(2,1)S(1)} collective-permute-done((bf16[2,128,256]{2,1,0:T(8,128)(2,1)S(1)}, bf16[2,128,256]{2,1,0:T(8,128)(2,1)S(1)}, u32[]{:S(2)}, u32[]{:S(2)}) %collective-permute-start.11) | collective-permute-done | bytes 131104 | tf_op jit(solution)/shard_map/ppermute | solution.py:24
  126.7 0.6 constant_dynamic-update-slice_fusion.11
  127.4 5.8 %collective-permute-done.12 = bf16[2,128,256]{2,1,0:T(8,128)(2,1)S(1)} collective-permute-done((bf16[2,128,256]{2,1,0:T(8,128)(2,1)S(1)}, bf16[2,128,256]{2,1,0:T(8,128)(2,1)S(1)}, u32[]{:S(2)}, u32[]{:S(2)}) %collective-permute-start.12) | collective-permute-done | bytes 131104 | tf_op jit(solution)/shard_map/ppermute | solution.py:24
  133.2 1.2 collective-permute-start.13
  134.5 0.7 constant_dynamic-update-slice_fusion.10
  135.1 0.7 constant_dynamic-update-slice_fusion.9
  135.8 2.4 %collective-permute-done.13 = bf16[2,128,256]{2,1,0:T(8,128)(2,1)S(1)} collective-permute-done((bf16[2,128,256]{2,1,0:T(8,128)(2,1)S(1)}, bf16[2,128,256]{2,1,0:T(8,128)(2,1)S(1)}, u32[]{:S(2)}, u32[]{:S(2)}) %collective-permute-start.13) | collective-permute-done | bytes 131104 | tf_op jit(solution)/shard_map/ppermute | solution.py:24
  138.2 0.7 constant_dynamic-update-slice_fusion.8.near
  138.8 0.0 collective-permute-start.14
  138.9 0.1 broadcast_add_fusion
  138.9 0.6 add.70.places
  139.5 0.5 fusion.places
  140.0 0.1 collective-permute-start.17
  140.1 1.3 slice.37
  141.5 3.0 %collective-permute-start.18 = (bf16[64,4096]{1,0:T(8,128)(2,1)S(1)}, bf16[64,4096]{1,0:T(8,128)(2,1)}, u32[]{:S(2)}, u32[]{:S(2)}) collective-permute-start(bf16[64,4096]{1,0:T(8,128)(2,1)S(1)} %slice.37), channel_id=1, source_target_pairs={{0,3},{1,0},{2,1},{3,2},{4,7},{5,4},{6,5},{7,6},{8,11},{9,8},{10,9... | collective-permute-start | bytes 1572872 | tf_op jit(solution)/shard_map/ppermute | solution.py:24
  144.5 1.1 slice.33
  145.6 0.1 collective-permute-start.4
  145.7 1.1 slice.34
  146.8 3.3 %collective-permute-start.6 = (bf16[64,4096]{1,0:T(8,128)(2,1)S(1)}, bf16[64,4096]{1,0:T(8,128)(2,1)S(1)}, u32[]{:S(2)}, u32[]{:S(2)}) collective-permute-start(bf16[64,4096]{1,0:T(8,128)(2,1)S(1)} %slice.34), channel_id=1, source_target_pairs={{0,3},{1,0},{2,1},{3,2},{4,7},{5,4},{6,5},{7,6},{8,11},{9,8},{10,9... | collective-permute-start | bytes 1572872 | tf_op jit(solution)/shard_map/ppermute | solution.py:24
  150.1 15.3 %hess.1 = (bf16[128,4096]{1,0:T(8,128)(2,1)}, f32[128,128]{1,0:T(8,128)}, bf16[256,1024]{1,0:T(8,128)(2,1)}, f32[128,1024]{1,0:T(8,128)}, f32[128,1024]{1,0:T(8,128)}) custom-call(s32[16]{0:T(128)} %fusion.places, bf16[8,128,256]{2,1,0:T(8,128)(2,1)} %constant_dynamic-update-slice_fusion.8.near, bf16[8,128,256]{2,1,0:T(8,128)(2,1)} %collective-permute-done.14.other, ...), custom_call_target="tpu_custom_call" | custom-call | flops 8999999488 | bytes 10000000 | tf_op jit(solution)/shard_map/hess/pallas_call | solution.py:276
  165.4 19.3 %shard_map.37.refs_6_ = bf16[16,1,64,1024]{3,2,1,0:T(8,128)(2,1)} custom-call(s32[16]{0:T(128)} %add.70.places, bf16[128,4096]{1,0:T(8,128)(2,1)} %constant_dynamic-update-slice_fusion.4.rows.refs_0_, bf16[128,4096]{1,0:T(8,128)(2,1)} %copy-done.4, bf16[128,4096]{1,0:T(8,128)(2,1)} %collective-permute-done.16.behind.refs_2_, ...), custom_call_target="tpu_custom_call" | custom-call | flops 7516192768 | bytes 14680064 | tf_op jit(solution)/shard_map/pallas_call | solution.py:202
  184.7 0.8 copy-done.2
  185.5 0.8 copy-done.3
  186.3 9.7 %shard_map.38 = bf16[16,1,64,1024]{3,2,1,0:T(8,128)(2,1)} custom-call(s32[16]{0:T(128)} %add.70.places, bf16[64,4096]{1,0:T(8,128)(2,1)} %copy-done.2, bf16[64,4096]{1,0:T(8,128)(2,1)} %copy-done.3, bf16[4096,1024]{1,0:T(8,128)(2,1)} %refs_2_.1, bf16[128,4096]{1,0:T(8,128)(2,1)} %get-tuple-element.13.refs_12_.refs_3_, ...), custom_call_target="tpu_custom_call", output_to_operand_aliasing={{}: (7, {})} | custom-call | flops 1073741824 | bytes 2097152 | tf_op jit(solution)/shard_map/pallas_call | solution.py:202
  (27 shorter events, 0.2 us)
Async XLA Ops:
  0.0 1.0 copy-start
  0.0 11.9 %copy-start.1 = (bf16[256,1024]{1,0:T(8,128)(2,1)S(1)}, bf16[256,1024]{1,0:T(8,128)(2,1)}, u32[]{:S(2)}) copy-start(bf16[256,1024]{1,0:T(8,128)(2,1)} %param.3) | copy-start | bytes 1572868
  3.3 16.6 %all-to-all-start.1 = ((f32[16,8,384]{2,1,0:T(8,128)}), f32[16,8,384]{2,1,0:T(8,128)S(1)}, u32[]{:S(2)}, u32[]{:S(2)}) async-start(f32[16,8,384]{2,1,0:T(8,128)} %maximum_bitcast_fusion), calls=%async_computation.1 | async-start | bytes 393216 | tf_op jit(solution)/shard_map/all_to_all | solution.py:242
  19.9 28.7 %all-to-all-start = ((bf16[16,64,256]{2,1,0:T(8,128)(2,1)}), bf16[16,64,256]{2,1,0:T(8,128)(2,1)S(1)}, u32[]{:S(2)}, u32[]{:S(2)}) async-start(bf16[16,64,256]{2,1,0:T(8,128)(2,1)} %bitcast.1), calls=%async_computation | async-start | bytes 1048576 | tf_op jit(solution)/shard_map/all_to_all | solution.py:232
  49.3 48.6 %all-to-all-start.2 = ((f32[16,8,384]{2,1,0:T(8,128)}), f32[16,8,384]{2,1,0:T(8,128)S(1)}, u32[]{:S(2)}, u32[]{:S(2)}) async-start(f32[16,8,384]{2,1,0:T(8,128)} %broadcast_in_dim.2), calls=%async_computation.2 | async-start | bytes 393216 | tf_op jit(solution)/shard_map/all_to_all | solution.py:244
  54.5 20.1 %collective-permute-start.7 = (bf16[32,4096]{1,0:T(8,128)(2,1)S(1)}, bf16[32,4096]{1,0:T(8,128)(2,1)S(1)}, u32[]{:S(2)}, u32[]{:S(2)}) collective-permute-start(bf16[32,4096]{1,0:T(8,128)(2,1)S(1)} %bitcast.27), channel_id=1, source_target_pairs={{0,4},{4,8},{8,12},{12,0},{1,5},{5,9},{9,13},{13,1},{2,6},{6,10},{... | collective-permute-start | bytes 786440 | tf_op jit(solution)/shard_map/ppermute | solution.py:24
  55.9 35.7 %collective-permute-start.8 = (bf16[32,4096]{1,0:T(8,128)(2,1)S(1)}, bf16[32,4096]{1,0:T(8,128)(2,1)S(1)}, u32[]{:S(2)}, u32[]{:S(2)}) collective-permute-start(bf16[32,4096]{1,0:T(8,128)(2,1)S(1)} %bitcast.28), channel_id=1, source_target_pairs={{0,8},{4,12},{8,0},{12,4},{1,9},{5,13},{9,1},{13,5},{2,10},{6,14},... | collective-permute-start | bytes 786440 | tf_op jit(solution)/shard_map/ppermute | solution.py:24
  56.9 37.0 %collective-permute-start.9 = (bf16[32,4096]{1,0:T(8,128)(2,1)S(1)}, bf16[32,4096]{1,0:T(8,128)(2,1)S(1)}, u32[]{:S(2)}, u32[]{:S(2)}) collective-permute-start(bf16[32,4096]{1,0:T(8,128)(2,1)S(1)} %bitcast.29), channel_id=1, source_target_pairs={{0,12},{4,0},{8,4},{12,8},{1,13},{5,1},{9,5},{13,9},{2,14},{6,2},{... | collective-permute-start | bytes 786440 | tf_op jit(solution)/shard_map/ppermute | solution.py:24
  58.9 52.0 %collective-permute-start = (bf16[32,4096]{1,0:T(8,128)(2,1)S(1)}, bf16[32,4096]{1,0:T(8,128)(2,1)S(1)}, u32[]{:S(2)}, u32[]{:S(2)}) collective-permute-start(bf16[32,4096]{1,0:T(8,128)(2,1)S(1)} %bitcast.22), channel_id=1, source_target_pairs={{0,4},{4,8},{8,12},{12,0},{1,5},{5,9},{9,13},{13,1},{2,6},{6,10},{... | collective-permute-start | bytes 786440 | tf_op jit(solution)/shard_map/ppermute | solution.py:24
  59.0 53.3 %collective-permute-start.1 = (bf16[32,4096]{1,0:T(8,128)(2,1)S(1)}, bf16[32,4096]{1,0:T(8,128)(2,1)S(1)}, u32[]{:S(2)}, u32[]{:S(2)}) collective-permute-start(bf16[32,4096]{1,0:T(8,128)(2,1)S(1)} %bitcast.23), channel_id=1, source_target_pairs={{0,8},{4,12},{8,0},{12,4},{1,9},{5,13},{9,1},{13,5},{2,10},{6,14},... | collective-permute-start | bytes 786440 | tf_op jit(solution)/shard_map/ppermute | solution.py:24
  74.6 38.4 %collective-permute-start.2 = (bf16[32,4096]{1,0:T(8,128)(2,1)S(1)}, bf16[32,4096]{1,0:T(8,128)(2,1)S(1)}, u32[]{:S(2)}, u32[]{:S(2)}) collective-permute-start(bf16[32,4096]{1,0:T(8,128)(2,1)S(1)} %bitcast.25), channel_id=1, source_target_pairs={{0,12},{4,0},{8,4},{12,8},{1,13},{5,1},{9,5},{13,9},{2,14},{6,2},{... | collective-permute-start | bytes 786440 | tf_op jit(solution)/shard_map/ppermute | solution.py:24
  94.7 45.3 %collective-permute-start.15 = (bf16[128,4096]{1,0:T(8,128)(2,1)}, bf16[128,4096]{1,0:T(8,128)(2,1)S(1)}, u32[]{:S(2)}, u32[]{:S(2)}) collective-permute-start(bf16[128,4096]{1,0:T(8,128)(2,1)} %constant_dynamic-update-slice_fusion.4.rows.refs_0_), channel_id=1, source_target_pairs={{0,1},{1,2},{2,3},{3,0},{4,5},{5,6},{6,7},{7,4},{8,9},{9,10},{10,1... | collective-permute-start | bytes 3145736 | tf_op jit(solution)/shard_map/ppermute | solution.py:24
  96.1 44.0 %collective-permute-start.16 = (bf16[128,4096]{1,0:T(8,128)(2,1)}, bf16[128,4096]{1,0:T(8,128)(2,1)}, u32[]{:S(2)}, u32[]{:S(2)}) collective-permute-start(bf16[128,4096]{1,0:T(8,128)(2,1)} %constant_dynamic-update-slice_fusion.4.rows.refs_0_), channel_id=1, source_target_pairs={{0,3},{1,0},{2,1},{3,2},{4,7},{5,4},{6,5},{7,6},{8,11},{9,8},{10,9... | collective-permute-start | bytes 3145736 | tf_op jit(solution)/shard_map/ppermute | solution.py:24
  97.9 0.7 copy-start.5
  110.9 8.5 %collective-permute-start.10 = (bf16[128,256]{1,0:T(8,128)(2,1)}, bf16[128,256]{1,0:T(8,128)(2,1)S(1)}, u32[]{:S(2)}, u32[]{:S(2)}) collective-permute-start(bf16[128,256]{1,0:T(8,128)(2,1)} %get-tuple-element.12), channel_id=1, source_target_pairs={{0,128},{128,0},{1,129},{129,1},{2,130},{130,2},{3,131},{131,3},{4... | collective-permute-start | bytes 196616 | tf_op jit(solution)/shard_map/ppermute | solution.py:24
  113.8 30.8 %collective-permute-start.3 = (bf16[128,4096]{1,0:T(8,128)(2,1)}, bf16[128,4096]{1,0:T(8,128)(2,1)}, u32[]{:S(2)}, u32[]{:S(2)}) collective-permute-start(bf16[128,4096]{1,0:T(8,128)(2,1)} %constant_dynamic-update-slice_fusion.refs_5_), channel_id=1, source_target_pairs={{0,1},{1,2},{2,3},{3,0},{4,5},{5,6},{6,7},{7,4},{8,9},{9,10},{10,1... | collective-permute-start | bytes 3145736 | tf_op jit(solution)/shard_map/ppermute | solution.py:24
  114.0 31.7 %collective-permute-start.5 = (bf16[128,4096]{1,0:T(8,128)(2,1)}, bf16[128,4096]{1,0:T(8,128)(2,1)}, u32[]{:S(2)}, u32[]{:S(2)}) collective-permute-start(bf16[128,4096]{1,0:T(8,128)(2,1)} %constant_dynamic-update-slice_fusion.refs_5_), channel_id=1, source_target_pairs={{0,3},{1,0},{2,1},{3,2},{4,7},{5,4},{6,5},{7,6},{8,11},{9,8},{10,9... | collective-permute-start | bytes 3145736 | tf_op jit(solution)/shard_map/ppermute | solution.py:24
  120.2 6.5 %collective-permute-start.11 = (bf16[2,128,256]{2,1,0:T(8,128)(2,1)S(1)}, bf16[2,128,256]{2,1,0:T(8,128)(2,1)S(1)}, u32[]{:S(2)}, u32[]{:S(2)}) collective-permute-start(bf16[2,128,256]{2,1,0:T(8,128)(2,1)S(1)} %pad_maximum_fusion), channel_id=1, source_target_pairs={{0,32},{32,64},{64,96},{96,0},{1,33},{33,65},{65,97},{97,1},{2,34}... | collective-permute-start | bytes 393224 | tf_op jit(solution)/shard_map/ppermute | solution.py:24
  126.7 6.5 %collective-permute-start.12 = (bf16[2,128,256]{2,1,0:T(8,128)(2,1)S(1)}, bf16[2,128,256]{2,1,0:T(8,128)(2,1)S(1)}, u32[]{:S(2)}, u32[]{:S(2)}) collective-permute-start(bf16[2,128,256]{2,1,0:T(8,128)(2,1)S(1)} %pad_maximum_fusion), channel_id=1, source_target_pairs={{0,64},{32,96},{64,0},{96,32},{1,65},{33,97},{65,1},{97,33},{2,66}... | collective-permute-start | bytes 393224 | tf_op jit(solution)/shard_map/ppermute | solution.py:24
  133.2 5.0 %collective-permute-start.13 = (bf16[2,128,256]{2,1,0:T(8,128)(2,1)S(1)}, bf16[2,128,256]{2,1,0:T(8,128)(2,1)S(1)}, u32[]{:S(2)}, u32[]{:S(2)}) collective-permute-start(bf16[2,128,256]{2,1,0:T(8,128)(2,1)S(1)} %pad_maximum_fusion), channel_id=1, source_target_pairs={{0,96},{32,0},{64,32},{96,64},{1,97},{33,1},{65,33},{97,65},{2,98}... | collective-permute-start | bytes 393224 | tf_op jit(solution)/shard_map/ppermute | solution.py:24
  138.8 11.2 %collective-permute-start.14 = (bf16[8,128,256]{2,1,0:T(8,128)(2,1)}, bf16[8,128,256]{2,1,0:T(8,128)(2,1)}, u32[]{:S(2)}, u32[]{:S(2)}) collective-permute-start(bf16[8,128,256]{2,1,0:T(8,128)(2,1)} %constant_dynamic-update-slice_fusion.8.near), channel_id=1, source_target_pairs={{0,16},{16,0},{1,17},{17,1},{2,18},{18,2},{3,19},{19,3},{4,20},{20... | collective-permute-start | bytes 1572872 | tf_op jit(solution)/shard_map/ppermute | solution.py:24
  140.0 4.5 %copy-start.4 = (bf16[128,4096]{1,0:T(8,128)(2,1)}, bf16[128,4096]{1,0:T(8,128)(2,1)S(1)}, u32[]{:S(2)}) copy-start(bf16[128,4096]{1,0:T(8,128)(2,1)S(1)} %collective-permute-done.15.ahead.refs_1_) | copy-start | bytes 3145732
  140.0 25.3 %collective-permute-start.17 = (bf16[64,4096]{1,0:T(8,128)(2,1)S(1)}, bf16[64,4096]{1,0:T(8,128)(2,1)}, u32[]{:S(2)}, u32[]{:S(2)}) collective-permute-start(bf16[64,4096]{1,0:T(8,128)(2,1)S(1)} %slice.36), channel_id=1, source_target_pairs={{0,1},{1,2},{2,3},{3,0},{4,5},{5,6},{6,7},{7,4},{8,9},{9,10},{10,1... | collective-permute-start | bytes 1572872 | tf_op jit(solution)/shard_map/ppermute | solution.py:24
  141.5 23.9 %collective-permute-start.18 = (bf16[64,4096]{1,0:T(8,128)(2,1)S(1)}, bf16[64,4096]{1,0:T(8,128)(2,1)}, u32[]{:S(2)}, u32[]{:S(2)}) collective-permute-start(bf16[64,4096]{1,0:T(8,128)(2,1)S(1)} %slice.37), channel_id=1, source_target_pairs={{0,3},{1,0},{2,1},{3,2},{4,7},{5,4},{6,5},{7,6},{8,11},{9,8},{10,9... | collective-permute-start | bytes 1572872 | tf_op jit(solution)/shard_map/ppermute | solution.py:24
  145.6 39.1 %collective-permute-start.4 = (bf16[64,4096]{1,0:T(8,128)(2,1)S(1)}, bf16[64,4096]{1,0:T(8,128)(2,1)S(1)}, u32[]{:S(2)}, u32[]{:S(2)}) collective-permute-start(bf16[64,4096]{1,0:T(8,128)(2,1)S(1)} %slice.33), channel_id=1, source_target_pairs={{0,1},{1,2},{2,3},{3,0},{4,5},{5,6},{6,7},{7,4},{8,9},{9,10},{10,1... | collective-permute-start | bytes 1572872 | tf_op jit(solution)/shard_map/ppermute | solution.py:24
  146.8 37.9 %collective-permute-start.6 = (bf16[64,4096]{1,0:T(8,128)(2,1)S(1)}, bf16[64,4096]{1,0:T(8,128)(2,1)S(1)}, u32[]{:S(2)}, u32[]{:S(2)}) collective-permute-start(bf16[64,4096]{1,0:T(8,128)(2,1)S(1)} %slice.34), channel_id=1, source_target_pairs={{0,3},{1,0},{2,1},{3,2},{4,7},{5,4},{6,5},{7,6},{8,11},{9,8},{10,9... | collective-permute-start | bytes 1572872 | tf_op jit(solution)/shard_map/ppermute | solution.py:24
  184.7 0.8 copy-start.2
  185.5 0.8 copy-start.3

commit v4 on v1

--- a/solution.py
+++ b/solution.py
@@ -80,14 +80,15 @@
     out_ref[...] = found.astype(BF16)
 
 
-def hess_kernel(places, near, other, dos_hbm, fac, inverse, proj, mat, dos, sem):
+def hess_kernel(places, *refs):
+    parts, (dos_hbm, fac, inverse, proj, mat, dos, sem) = refs[:-7], refs[-7:]
     k = mat.shape[0]
-    width = near.shape[2]
+    each, width = parts[0].shape[0], parts[0].shape[2]
     fetch = pltpu.make_async_copy(dos_hbm, dos, sem)
     fetch.start()
-    for i in range(8):
-        fac[:, pl.ds(pl.multiple_of(places[i] * width, width), width)] = near[i]
-        fac[:, pl.ds(pl.multiple_of(places[8 + i] * width, width), width)] = other[i]
+    for i, part in enumerate(parts):
+        for j in range(each):
+            fac[:, pl.ds(pl.multiple_of(places[each * i + j] * width, width), width)] = part[j]
     mat[...] = lax.dot_general(fac[...], fac[...], NT, preferred_element_type=F32) + ridge_sample * eye(k)
     sweep(mat)
     inverse[...] = -mat[...]
@@ -101,19 +102,26 @@
 def finish_kernel(scale, start, genes, count, places, *refs):
     pieces, scores = refs[:count], refs[count : 2 * count]
     fac, inverse, proj = refs[2 * count : 2 * count + 3]
-    out, done, sems = refs[-3:]
-    cross = [lax.dot_general(piece[...], fac[...], NT, preferred_element_type=F32) for piece in pieces]
-    cross = jnp.concatenate(cross)
-    half = jnp.dot(cross, inverse[...], preferred_element_type=F32, precision=HI).astype(BF16)
-    coef = jnp.concatenate([half, half], axis=1)
+    out, done, loads, sems = refs[-2 * count - 4], refs[-2 * count - 3], refs[-2 * count - 2], refs[-2 * count - 1]
+    held, base = refs[-2 * count : -count], refs[-count:]
+    fetches = [pltpu.make_async_copy(a, b, loads.at[i]) for i, (a, b) in enumerate(zip(pieces, held))]
+    fetches += [pltpu.make_async_copy(a, b, loads.at[count + i]) for i, (a, b) in enumerate(zip(scores, base))]
+    for i in range(count):
+        fetches[i].start()
+        fetches[count + i].start()
     at, copies = 0, []
-    for score in scores:
-        rows = score.shape[0]
-        total = score[...] - jnp.dot(coef[at : at + rows], proj[...], preferred_element_type=F32)
+    for i in range(count):
+        rows = held[i].shape[0]
+        fetches[i].wait()
+        cross = lax.dot_general(held[i][...], fac[...], NT, preferred_element_type=F32)
+        half = jnp.dot(cross, inverse[...], preferred_element_type=F32, precision=HI).astype(BF16)
+        coef = jnp.concatenate([half, half], axis=1)
+        fetches[count + i].wait()
+        total = base[i][...] - jnp.dot(coef, proj[...], preferred_element_type=F32)
         done[pl.ds(at, rows), :] = (total * scale).astype(BF16)
-        for i in range(at // genes, (at + rows) // genes):
+        for j in range(at // genes, (at + rows) // genes):
             copy = pltpu.make_async_copy(
-                done.at[pl.ds(i * genes, genes), :], out.at[places[i], 0, pl.ds(start, genes), :], sems.at[i]
+                done.at[pl.ds(j * genes, genes), :], out.at[places[j], 0, pl.ds(start, genes), :], sems.at[j]
             )
             copy.start()
             copies.append(copy)
@@ -126,7 +134,8 @@
     snps = scores[0].shape[1]
     rows = sum(p.shape[0] for p in pieces)
     ins = list(pieces) + list(scores) + [fac, inverse, proj]
-    specs = [pl.BlockSpec(a.shape, lambda n, _, nd=a.ndim: (0,) * nd) for a in ins]
+    specs = [pl.BlockSpec(memory_space=pl.ANY)] * (2 * len(pieces))
+    specs += [pl.BlockSpec(a.shape, lambda n, _, nd=a.ndim: (0,) * nd) for a in ins[-3:]]
     alias = {}
     if out is not None:
         alias = {len(ins) + 1: 0}
@@ -140,7 +149,13 @@
             grid=(1,),
             in_specs=specs,
             out_specs=pl.BlockSpec(memory_space=pl.ANY),
-            scratch_shapes=[pltpu.VMEM((rows, snps), BF16), pltpu.SemaphoreType.DMA((rows // genes,))],
+            scratch_shapes=[
+                pltpu.VMEM((rows, snps), BF16),
+                pltpu.SemaphoreType.DMA((2 * len(pieces),)),
+                pltpu.SemaphoreType.DMA((rows // genes,)),
+            ]
+            + [pltpu.VMEM(p.shape, BF16) for p in pieces]
+            + [pltpu.VMEM(p.shape, F32) for p in scores],
         ),
         input_output_aliases=alias,
         cost_estimate=pl.CostEstimate(flops=2 * rows * samples * 256, bytes_accessed=rows * 16384, transcendentals=0),
@@ -162,7 +177,7 @@
 
     both = jnp.concatenate(
         [
-            lax.dot_general(loadings, flipped, TN, preferred_element_type=F32),
+            lax.dot_general(loadings, expression, (((0,), (1,)), ((), ())), preferred_element_type=F32),
             lax.dot_general(loadings, loadings, TN, preferred_element_type=F32),
         ],
         axis=1,
@@ -184,14 +199,14 @@
         piece = mine[c * width : c * width + width]
         own = jnp.concatenate([piece] + [cycle(piece, "zl", by) for by in (1, 2, 3)])
         ahead, behind = cycle(own, "y", 1), cycle(own, "y", -1)
+        if c < CHUNKS - 1:
+            far = cycle(ahead, "y", 1)
+            groups.append((c * width, [(0, 4), (4, 8), (12, 16), (8, 12)], [own, ahead, behind, far]))
+            continue
         low, high = ahead[: 2 * width], behind[2 * width :]
         low, high = cycle(low, "y", 1), cycle(high, "y", -1)
-        near_slots, far_slots = [(0, 4), (4, 8), (12, 16)], [(8, 10), (10, 12)]
-        if c < CHUNKS - 1:
-            groups.append((c * width, near_slots + far_slots, [own, ahead, behind, low, high]))
-        else:
-            groups.append((c * width, near_slots, [own, ahead, behind]))
-            groups.append((c * width, far_slots, [low, high]))
+        groups.append((c * width, [(0, 4), (4, 8), (12, 16)], [own, ahead, behind]))
+        groups.append((c * width, [(8, 10), (10, 12)], [low, high]))
     scores = []
     for _, _, pieces in groups:
         scores.append([])
@@ -199,11 +214,11 @@
             scores[-1].append(jnp.dot(rows, dosage, preferred_element_type=F32))
 
     two = jnp.stack([factors, cycle(factors, "zh", 1)])
-    near = jnp.concatenate([two] + [cycle(two, "x", by) for by in (1, 2, 3)])
-    other = cycle(near, "core", 1)
+    four = jnp.concatenate([two, cycle(two, "core", 1)])
+    gathered = [four] + [cycle(four, "x", by) for by in (1, 2, 3)]
     back = jnp.arange(16)
-    from_core = (at["core"] - back // 8) % 2
-    from_x = (at["x"] - back // 2 % 4) % 4
+    from_core = (at["core"] - back // 2 % 2) % 2
+    from_x = (at["x"] - back // 4) % 4
     from_zh = (at["zh"] - back % 2) % 2
     order = (from_zh * 8 + from_x * 2 + from_core).astype(jnp.int32)
     fac, inverse, proj = pl.pallas_call(
@@ -215,8 +230,7 @@
         ),
         in_specs=[
             pl.BlockSpec(memory_space=pltpu.SMEM),
-            pl.BlockSpec(memory_space=pltpu.VMEM),
-            pl.BlockSpec(memory_space=pltpu.VMEM),
+            *[pl.BlockSpec(memory_space=pltpu.VMEM)] * 4,
             pl.BlockSpec(memory_space=pl.ANY),
         ],
         scratch_shapes=[
@@ -227,7 +241,7 @@
         cost_estimate=pl.CostEstimate(flops=9_000_000_000, bytes_accessed=10_000_000, transcendentals=0),
         compiler_params=pltpu.CompilerParams(vmem_limit_bytes=24 << 20),
         name="hess",
-    )(order, near, other, dosage)
+    )(order, *gathered, dosage)
 
     back_z = (at["zl"] - jnp.arange(4)) % 4
     back_y = (at["y"] - jnp.arange(4)) % 4

time: 198 us -> 209 us (1.056)
  the two profiles are of different devices: /device:TPU:64 before, /device:TPU:32 now
where the time goes in v4:
time: 209 us; the launch traced here: 208 us
  waiting for transfers between devices  102 us (49%)
  starting transfers between devices  46.7 us (22%)
  Pallas kernels  34.9 us (17%)
  matrix products  13.9 us (7%)
  local copies, waits for them, and re-layouts  7.38 us (4%)
  other arithmetic  2.7 us (1%)
    ppermute x18, waiting for transfers between devices, cycle(): lax.ppermute(array, axis, [(i, (i + by) % size) for i in range(size)])  88.4 us
    ppermute x18, starting transfers between devices, cycle(): lax.ppermute(array, axis, [(i, (i + by) % size) for i in range(size)])  24.6 us
    pallas_call x3, Pallas kernels, finish(): pl.pallas_call(functools.partial(finish_kernel, float(samples) ** (-0.5),...  15.9 us
    dot_general x9, matrix products, body(): scores[-1].append(jnp.dot(rows, dosage, preferred_element_type=F32))  12.3 us
    pallas_call x1, Pallas kernels, body(): pl.pallas_call(hess_kernel, out_shape=(jax.ShapeDtypeStruct((k, all_sampl...  10.1 us
    pallas_call x1, Pallas kernels, body(): pl.pallas_call(factor_kernel, out_shape=jax.ShapeDtypeStruct((k, samples)...  8.94 us
    all_to_all x1, starting transfers between devices, body(): lax.all_to_all(both.reshape(n_cols, k // n_cols, samples + k), COLS, 0, 0...  8.65 us
    all_to_all x1, starting transfers between devices, body(): lax.all_to_all(flipped.reshape(n_samp, panel, samples), SAMP, 0, 0, tiled...  8.33 us
  transfers between devices with their start and end apart: 21, of which 13 were waited for; matrix products, arithmetic and copies ran while one was open for 7% of the time, Pallas kernels for 9%

profile of v4, /device:TPU:32, one launch (start us, length us, event | category | flops | bytes accessed | tf_op | source)
XLA Modules:
  0.0 208.1 jit_solution(16873789786050064234)
XLA Ops:
  0.0 0.9 copy-done
  1.0 0.3 fusion.17
  1.2 1.4 fusion.16
  2.6 0.7 maximum_bitcast_fusion
  3.3 8.7 %all-to-all-start.1 = ((f32[16,8,384]{2,1,0:T(8,128)}), f32[16,8,384]{2,1,0:T(8,128)S(1)}, u32[]{:S(2)}, u32[]{:S(2)}) async-start(f32[16,8,384]{2,1,0:T(8,128)} %maximum_bitcast_fusion), calls=%async_computation.1 | async-start | bytes 393216 | tf_op jit(solution)/shard_map/all_to_all | solution.py:185
  11.9 2.0 copy.8
  14.0 5.9 %all-to-all-done.1 = f32[16,8,384]{2,1,0:T(8,128)S(1)} async-done(((f32[16,8,384]{2,1,0:T(8,128)}), f32[16,8,384]{2,1,0:T(8,128)S(1)}, u32[]{:S(2)}, u32[]{:S(2)}) %all-to-all-start.1) | async-done | bytes 196640 | tf_op jit(solution)/shard_map/all_to_all | solution.py:185
  20.0 0.7 broadcast_in_dim.2
  20.7 5.1 %all-to-all-start.2 = ((f32[16,8,384]{2,1,0:T(8,128)}), f32[16,8,384]{2,1,0:T(8,128)S(1)}, u32[]{:S(2)}, u32[]{:S(2)}) async-start(f32[16,8,384]{2,1,0:T(8,128)} %broadcast_in_dim.2), calls=%async_computation.2 | async-start | bytes 393216 | tf_op jit(solution)/shard_map/all_to_all | solution.py:187
  25.8 0.1 broadcast_add_fusion
  25.9 7.8 %all-to-all-done.2 = f32[16,8,384]{2,1,0:T(8,128)S(1)} async-done(((f32[16,8,384]{2,1,0:T(8,128)}), f32[16,8,384]{2,1,0:T(8,128)S(1)}, u32[]{:S(2)}, u32[]{:S(2)}) %all-to-all-start.2) | async-done | bytes 196640 | tf_op jit(solution)/shard_map/all_to_all | solution.py:187
  33.6 8.3 %all-to-all-start = ((bf16[16,64,256]{2,1,0:T(8,128)(2,1)}), bf16[16,64,256]{2,1,0:T(8,128)(2,1)S(1)}, u32[]{:S(2)}, u32[]{:S(2)}) async-start(bf16[16,64,256]{2,1,0:T(8,128)(2,1)} %bitcast.2), calls=%async_computation | async-start | bytes 1048576 | tf_op jit(solution)/shard_map/all_to_all | solution.py:175
  42.0 8.9 %factor.1 = bf16[128,256]{1,0:T(8,128)(2,1)} custom-call(f32[128,384]{1,0:T(8,128)} %bitcast.58), custom_call_target="tpu_custom_call" | custom-call | flops 7000000000 | bytes 400000 | tf_op jit(solution)/shard_map/factor/pallas_call | solution.py:188
  50.9 5.8 %collective-permute-start.7 = (bf16[128,256]{1,0:T(8,128)(2,1)}, bf16[128,256]{1,0:T(8,128)(2,1)S(1)}, u32[]{:S(2)}, u32[]{:S(2)}) collective-permute-start(bf16[128,256]{1,0:T(8,128)(2,1)} %factor.1), channel_id=1, source_target_pairs={{0,128},{128,0},{1,129},{129,1},{2,130},{130,2},{3,131},{131,3},{4... | collective-permute-start | bytes 196616 | tf_op jit(solution)/shard_map/ppermute | solution.py:24
  56.7 0.1 pad_add_fusion.places
  56.8 6.2 %collective-permute-done.7 = bf16[128,256]{1,0:T(8,128)(2,1)S(1)} collective-permute-done((bf16[128,256]{1,0:T(8,128)(2,1)}, bf16[128,256]{1,0:T(8,128)(2,1)S(1)}, u32[]{:S(2)}, u32[]{:S(2)}) %collective-permute-start.7) | collective-permute-done | bytes 65568 | tf_op jit(solution)/shard_map/ppermute | solution.py:24
  63.0 0.9 pad_maximum_fusion.1
  63.9 0.1 collective-permute-start.8
  64.0 0.1 pad_add_fusion.1.places
  64.1 1.2 collective-permute-done.8
  65.3 0.9 pad_maximum_fusion.refs_0_
  66.2 3.0 %collective-permute-start.10 = (bf16[4,128,256]{2,1,0:T(8,128)(2,1)S(1)}, bf16[4,128,256]{2,1,0:T(8,128)(2,1)S(1)}, u32[]{:S(2)}, u32[]{:S(2)}) collective-permute-start(bf16[4,128,256]{2,1,0:T(8,128)(2,1)S(1)} %pad_maximum_fusion.refs_0_), channel_id=1, source_target_pairs={{0,64},{32,96},{64,0},{96,32},{1,65},{33,97},{65,1},{97,33},{2,66}... | collective-permute-start | bytes 786440 | tf_op jit(solution)/shard_map/ppermute | solution.py:24
  69.2 1.2 collective-permute-start.11
  70.4 0.9 collective-permute-start.9
  71.3 0.0 all-to-all-done
  71.4 1.0 collective-permute-start.12
  72.3 0.2 collective-permute-start.13
  72.6 4.4 %collective-permute-done.10.refs_2_ = bf16[4,128,256]{2,1,0:T(8,128)(2,1)S(1)} collective-permute-done((bf16[4,128,256]{2,1,0:T(8,128)(2,1)S(1)}, bf16[4,128,256]{2,1,0:T(8,128)(2,1)S(1)}, u32[]{:S(2)}, u32[]{:S(2)}) %collective-permute-start.10) | collective-permute-done | bytes 262176 | tf_op jit(solution)/shard_map/ppermute | solution.py:24
  77.0 4.8 %collective-permute-done.11.refs_3_ = bf16[4,128,256]{2,1,0:T(8,128)(2,1)S(1)} collective-permute-done((bf16[4,128,256]{2,1,0:T(8,128)(2,1)S(1)}, bf16[4,128,256]{2,1,0:T(8,128)(2,1)S(1)}, u32[]{:S(2)}, u32[]{:S(2)}) %collective-permute-start.11) | collective-permute-done | bytes 262176 | tf_op jit(solution)/shard_map/ppermute | solution.py:24
  81.8 0.9 collective-permute-start
  82.7 0.2 collective-permute-start.1
  82.9 3.4 %copy-done.1 = bf16[4096,1024]{1,0:T(8,128)(2,1)S(1)} copy-done((bf16[4096,1024]{1,0:T(8,128)(2,1)S(1)}, bf16[4096,1024]{1,0:T(8,128)(2,1)}, u32[]{:S(2)}) %copy-start.1) | copy-done | bytes 8388632
  86.3 10.1 %hess.1 = (bf16[128,4096]{1,0:T(8,128)(2,1)S(1)}, f32[128,128]{1,0:T(8,128)S(1)}, bf16[256,1024]{1,0:T(8,128)(2,1)S(1)}) custom-call(s32[16]{0:T(128)S(1)} %fusion.places, bf16[4,128,256]{2,1,0:T(8,128)(2,1)S(1)} %pad_maximum_fusion.refs_0_, bf16[4,128,256]{2,1,0:T(8,128)(2,1)S(1)} %collective-permute-done.9.refs_1_, ...), custom_call_target="tpu_custom_call" | custom-call | flops 8999999488 | bytes 10000000 | tf_op jit(solution)/shard_map/hess/pallas_call | solution.py:224
  96.4 0.0 collective-permute-done.12
  96.4 1.3 collective-permute-start.2
  97.7 9.4 %collective-permute-done.13 = bf16[32,4096]{1,0:T(8,128)(2,1)S(1)} collective-permute-done((bf16[32,4096]{1,0:T(8,128)(2,1)S(1)}, bf16[32,4096]{1,0:T(8,128)(2,1)S(1)}, u32[]{:S(2)}, u32[]{:S(2)}) %collective-permute-start.13) | collective-permute-done | bytes 262176 | tf_op jit(solution)/shard_map/ppermute | solution.py:24
  107.2 0.0 collective-permute-done.14
  107.2 0.6 collective-permute-start.15
  107.8 2.7 %collective-permute-start.16 = (bf16[128,4096]{1,0:T(8,128)(2,1)S(1)}, bf16[128,4096]{1,0:T(8,128)(2,1)S(1)}, u32[]{:S(2)}, u32[]{:S(2)}) collective-permute-start(bf16[128,4096]{1,0:T(8,128)(2,1)S(1)} %constant_dynamic-update-slice_fusion.4.refs_0_), channel_id=1, source_target_pairs={{0,3},{1,0},{2,1},{3,2},{4,7},{5,4},{6,5},{7,6},{8,11},{9,8},{10,9... | collective-permute-start | bytes 3145736 | tf_op jit(solution)/shard_map/ppermute | solution.py:24
  110.5 2.2 %collective-permute-done = bf16[32,4096]{1,0:T(8,128)(2,1)S(1)} collective-permute-done((bf16[32,4096]{1,0:T(8,128)(2,1)S(1)}, bf16[32,4096]{1,0:T(8,128)(2,1)S(1)}, u32[]{:S(2)}, u32[]{:S(2)}) %collective-permute-start) | collective-permute-done | bytes 262176 | tf_op jit(solution)/shard_map/ppermute | solution.py:24
  112.8 3.9 %collective-permute-done.1 = bf16[32,4096]{1,0:T(8,128)(2,1)S(1)} collective-permute-done((bf16[32,4096]{1,0:T(8,128)(2,1)S(1)}, bf16[32,4096]{1,0:T(8,128)(2,1)S(1)}, u32[]{:S(2)}, u32[]{:S(2)}) %collective-permute-start.1) | collective-permute-done | bytes 262176 | tf_op jit(solution)/shard_map/ppermute | solution.py:24
  116.7 0.6 collective-permute-done.2
  117.4 0.6 collective-permute-start.3
  118.0 2.7 %collective-permute-start.5 = (bf16[128,4096]{1,0:T(8,128)(2,1)S(1)}, bf16[128,4096]{1,0:T(8,128)(2,1)S(1)}, u32[]{:S(2)}, u32[]{:S(2)}) collective-permute-start(bf16[128,4096]{1,0:T(8,128)(2,1)S(1)} %constant_dynamic-update-slice_fusion.refs_0_), channel_id=1, source_target_pairs={{0,3},{1,0},{2,1},{3,2},{4,7},{5,4},{6,5},{7,6},{8,11},{9,8},{10,9... | collective-permute-start | bytes 3145736 | tf_op jit(solution)/shard_map/ppermute | solution.py:24
  120.7 1.3 fusion.21.refs_4_
  122.0 1.3 fusion.18.refs_3_
  123.3 31.7 %collective-permute-done.3.refs_1_ = bf16[128,4096]{1,0:T(8,128)(2,1)S(1)} collective-permute-done((bf16[128,4096]{1,0:T(8,128)(2,1)S(1)}, bf16[128,4096]{1,0:T(8,128)(2,1)S(1)}, u32[]{:S(2)}, u32[]{:S(2)}) %collective-permute-start.3) | collective-permute-done | bytes 1048608 | tf_op jit(solution)/shard_map/ppermute | solution.py:24
  155.0 0.1 collective-permute-start.4
  155.2 3.3 %collective-permute-start.6 = (bf16[64,4096]{1,0:T(8,128)(2,1)S(1)}, bf16[64,4096]{1,0:T(8,128)(2,1)S(1)}, u32[]{:S(2)}, u32[]{:S(2)}) collective-permute-start(bf16[64,4096]{1,0:T(8,128)(2,1)S(1)} %slice.59), channel_id=1, source_target_pairs={{0,3},{1,0},{2,1},{3,2},{4,7},{5,4},{6,5},{7,6},{8,11},{9,8},{10,9... | collective-permute-start | bytes 1572872 | tf_op jit(solution)/shard_map/ppermute | solution.py:24
  158.5 0.0 collective-permute-done.15.refs_1_
  158.5 0.0 collective-permute-start.17
  158.5 1.3 fusion.22.refs_5_
  159.8 1.3 fusion.19.refs_4_
  161.1 1.3 fusion.20.refs_5_
  162.4 0.0 collective-permute-done.16.refs_2_
  162.4 1.3 fusion.23.refs_6_
  163.7 7.4 %collective-permute-done.4.refs_0_ = bf16[64,4096]{1,0:T(8,128)(2,1)S(1)} collective-permute-done((bf16[64,4096]{1,0:T(8,128)(2,1)S(1)}, bf16[64,4096]{1,0:T(8,128)(2,1)S(1)}, u32[]{:S(2)}, u32[]{:S(2)}) %collective-permute-start.4) | collective-permute-done | bytes 524320 | tf_op jit(solution)/shard_map/ppermute | solution.py:24
  171.1 1.6 fusion.14.refs_2_
  172.7 1.6 fusion.15.refs_3_
  174.3 16.5 %collective-permute-done.17.refs_3_ = bf16[128,4096]{1,0:T(8,128)(2,1)S(1)} collective-permute-done((bf16[128,4096]{1,0:T(8,128)(2,1)S(1)}, bf16[128,4096]{1,0:T(8,128)(2,1)S(1)}, u32[]{:S(2)}, u32[]{:S(2)}) %collective-permute-start.17) | collective-permute-done | bytes 1048608 | tf_op jit(solution)/shard_map/ppermute | solution.py:24
  190.7 1.3 fusion.24.refs_7_
  192.1 6.9 %shard_map.37.refs_9_ = bf16[16,1,64,1024]{3,2,1,0:T(8,128)(2,1)} custom-call(s32[16]{0:T(128)S(1)} %pad_add_fusion.1.places, bf16[128,4096]{1,0:T(8,128)(2,1)S(1)} %constant_dynamic-update-slice_fusion.4.refs_0_, bf16[128,4096]{1,0:T(8,128)(2,1)S(1)} %collective-permute-done.15.refs_1_, bf16[128,4096]{1,0:T(8,128)(2,1)S(1)} %collective-permute-done.16.refs_2_, ...), custom_call_target="tpu_custom_call" | custom-call | flops 1073741824 | bytes 8388608 | tf_op jit(solution)/shard_map/pallas_call | solution.py:144
  199.0 5.3 %shard_map.38.refs_7_ = bf16[16,1,64,1024]{3,2,1,0:T(8,128)(2,1)} custom-call(s32[12]{0:T(128)S(1)} %pad_add_fusion.places, bf16[128,4096]{1,0:T(8,128)(2,1)S(1)} %constant_dynamic-update-slice_fusion.refs_0_, bf16[128,4096]{1,0:T(8,128)(2,1)S(1)} %collective-permute-done.3.refs_1_, ...), custom_call_target="tpu_custom_call", output_to_operand_aliasing={{}: (10, {})} | custom-call | flops 805306368 | bytes 6291456 | tf_op jit(solution)/shard_map/pallas_call | solution.py:144
  204.3 3.7 %shard_map.39 = bf16[16,1,64,1024]{3,2,1,0:T(8,128)(2,1)} custom-call(s32[4]{0:T(128)S(1)} %get-tuple-element.16.places, bf16[64,4096]{1,0:T(8,128)(2,1)S(1)} %collective-permute-done.4.refs_0_, bf16[64,4096]{1,0:T(8,128)(2,1)S(1)} %collective-permute-done.6.refs_1_, f32[64,1024]{1,0:T(8,128)S(1)} %fusion.14.refs_2_, ...), custom_call_target="tpu_custom_call", output_to_operand_aliasing={{}: (8, {})} | custom-call | flops 268435456 | bytes 2097152 | tf_op jit(solution)/shard_map/pallas_call | solution.py:144
  (25 shorter events, 0.4 us)
Async XLA Ops:
  0.0 1.0 copy-start
  3.3 16.6 %all-to-all-start.1 = ((f32[16,8,384]{2,1,0:T(8,128)}), f32[16,8,384]{2,1,0:T(8,128)S(1)}, u32[]{:S(2)}, u32[]{:S(2)}) async-start(f32[16,8,384]{2,1,0:T(8,128)} %maximum_bitcast_fusion), calls=%async_computation.1 | async-start | bytes 393216 | tf_op jit(solution)/shard_map/all_to_all | solution.py:185
  20.7 13.0 %all-to-all-start.2 = ((f32[16,8,384]{2,1,0:T(8,128)}), f32[16,8,384]{2,1,0:T(8,128)S(1)}, u32[]{:S(2)}, u32[]{:S(2)}) async-start(f32[16,8,384]{2,1,0:T(8,128)} %broadcast_in_dim.2), calls=%async_computation.2 | async-start | bytes 393216 | tf_op jit(solution)/shard_map/all_to_all | solution.py:187
  33.6 8.3 %copy-start.2 = (f32[16,8,384]{2,1,0:T(8,128)}, f32[16,8,384]{2,1,0:T(8,128)S(1)}, u32[]{:S(2)}) copy-start(f32[16,8,384]{2,1,0:T(8,128)S(1)} %all-to-all-done.2) | copy-start | bytes 589828
  33.6 37.6 %all-to-all-start = ((bf16[16,64,256]{2,1,0:T(8,128)(2,1)}), bf16[16,64,256]{2,1,0:T(8,128)(2,1)S(1)}, u32[]{:S(2)}, u32[]{:S(2)}) async-start(bf16[16,64,256]{2,1,0:T(8,128)(2,1)} %bitcast.2), calls=%async_computation | async-start | bytes 1048576 | tf_op jit(solution)/shard_map/all_to_all | solution.py:175
  50.9 12.1 %collective-permute-start.7 = (bf16[128,256]{1,0:T(8,128)(2,1)}, bf16[128,256]{1,0:T(8,128)(2,1)S(1)}, u32[]{:S(2)}, u32[]{:S(2)}) collective-permute-start(bf16[128,256]{1,0:T(8,128)(2,1)} %factor.1), channel_id=1, source_target_pairs={{0,128},{128,0},{1,129},{129,1},{2,130},{130,2},{3,131},{131,3},{4... | collective-permute-start | bytes 196616 | tf_op jit(solution)/shard_map/ppermute | solution.py:24
  63.9 1.4 collective-permute-start.8
  66.2 10.8 %collective-permute-start.10 = (bf16[4,128,256]{2,1,0:T(8,128)(2,1)S(1)}, bf16[4,128,256]{2,1,0:T(8,128)(2,1)S(1)}, u32[]{:S(2)}, u32[]{:S(2)}) collective-permute-start(bf16[4,128,256]{2,1,0:T(8,128)(2,1)S(1)} %pad_maximum_fusion.refs_0_), channel_id=1, source_target_pairs={{0,64},{32,96},{64,0},{96,32},{1,65},{33,97},{65,1},{97,33},{2,66}... | collective-permute-start | bytes 786440 | tf_op jit(solution)/shard_map/ppermute | solution.py:24
  69.2 12.6 %collective-permute-start.11 = (bf16[4,128,256]{2,1,0:T(8,128)(2,1)S(1)}, bf16[4,128,256]{2,1,0:T(8,128)(2,1)S(1)}, u32[]{:S(2)}, u32[]{:S(2)}) collective-permute-start(bf16[4,128,256]{2,1,0:T(8,128)(2,1)S(1)} %pad_maximum_fusion.refs_0_), channel_id=1, source_target_pairs={{0,96},{32,0},{64,32},{96,64},{1,97},{33,1},{65,33},{97,65},{2,98}... | collective-permute-start | bytes 786440 | tf_op jit(solution)/shard_map/ppermute | solution.py:24
  70.4 12.3 %collective-permute-start.9 = (bf16[4,128,256]{2,1,0:T(8,128)(2,1)S(1)}, bf16[4,128,256]{2,1,0:T(8,128)(2,1)S(1)}, u32[]{:S(2)}, u32[]{:S(2)}) collective-permute-start(bf16[4,128,256]{2,1,0:T(8,128)(2,1)S(1)} %pad_maximum_fusion.refs_0_), channel_id=1, source_target_pairs={{0,32},{32,64},{64,96},{96,0},{1,33},{33,65},{65,97},{97,1},{2,34}... | collective-permute-start | bytes 786440 | tf_op jit(solution)/shard_map/ppermute | solution.py:24
  71.4 25.0 %collective-permute-start.12 = (bf16[32,4096]{1,0:T(8,128)(2,1)S(1)}, bf16[32,4096]{1,0:T(8,128)(2,1)S(1)}, u32[]{:S(2)}, u32[]{:S(2)}) collective-permute-start(bf16[32,4096]{1,0:T(8,128)(2,1)S(1)} %bitcast.51), channel_id=1, source_target_pairs={{0,4},{4,8},{8,12},{12,0},{1,5},{5,9},{9,13},{13,1},{2,6},{6,10},{... | collective-permute-start | bytes 786440 | tf_op jit(solution)/shard_map/ppermute | solution.py:24
  72.3 34.8 %collective-permute-start.13 = (bf16[32,4096]{1,0:T(8,128)(2,1)S(1)}, bf16[32,4096]{1,0:T(8,128)(2,1)S(1)}, u32[]{:S(2)}, u32[]{:S(2)}) collective-permute-start(bf16[32,4096]{1,0:T(8,128)(2,1)S(1)} %bitcast.52), channel_id=1, source_target_pairs={{0,8},{4,12},{8,0},{12,4},{1,9},{5,13},{9,1},{13,5},{2,10},{6,14},... | collective-permute-start | bytes 786440 | tf_op jit(solution)/shard_map/ppermute | solution.py:24
  77.0 30.2 %collective-permute-start.14 = (bf16[32,4096]{1,0:T(8,128)(2,1)S(1)}, bf16[32,4096]{1,0:T(8,128)(2,1)S(1)}, u32[]{:S(2)}, u32[]{:S(2)}) collective-permute-start(bf16[32,4096]{1,0:T(8,128)(2,1)S(1)} %bitcast.53), channel_id=1, source_target_pairs={{0,12},{4,0},{8,4},{12,8},{1,13},{5,1},{9,5},{13,9},{2,14},{6,2},{... | collective-permute-start | bytes 786440 | tf_op jit(solution)/shard_map/ppermute | solution.py:24
  81.8 31.0 %collective-permute-start = (bf16[32,4096]{1,0:T(8,128)(2,1)S(1)}, bf16[32,4096]{1,0:T(8,128)(2,1)S(1)}, u32[]{:S(2)}, u32[]{:S(2)}) collective-permute-start(bf16[32,4096]{1,0:T(8,128)(2,1)S(1)} %bitcast.47), channel_id=1, source_target_pairs={{0,4},{4,8},{8,12},{12,0},{1,5},{5,9},{9,13},{13,1},{2,6},{6,10},{... | collective-permute-start | bytes 786440 | tf_op jit(solution)/shard_map/ppermute | solution.py:24
  82.7 34.0 %collective-permute-start.1 = (bf16[32,4096]{1,0:T(8,128)(2,1)S(1)}, bf16[32,4096]{1,0:T(8,128)(2,1)S(1)}, u32[]{:S(2)}, u32[]{:S(2)}) collective-permute-start(bf16[32,4096]{1,0:T(8,128)(2,1)S(1)} %bitcast.48), channel_id=1, source_target_pairs={{0,8},{4,12},{8,0},{12,4},{1,9},{5,13},{9,1},{13,5},{2,10},{6,14},... | collective-permute-start | bytes 786440 | tf_op jit(solution)/shard_map/ppermute | solution.py:24
  82.9 3.4 %copy-start.1 = (bf16[4096,1024]{1,0:T(8,128)(2,1)S(1)}, bf16[4096,1024]{1,0:T(8,128)(2,1)}, u32[]{:S(2)}) copy-start(bf16[4096,1024]{1,0:T(8,128)(2,1)} %refs_4_.1) | copy-start | bytes 25165828
  96.4 21.0 %collective-permute-start.2 = (bf16[32,4096]{1,0:T(8,128)(2,1)S(1)}, bf16[32,4096]{1,0:T(8,128)(2,1)S(1)}, u32[]{:S(2)}, u32[]{:S(2)}) collective-permute-start(bf16[32,4096]{1,0:T(8,128)(2,1)S(1)} %bitcast.49), channel_id=1, source_target_pairs={{0,12},{4,0},{8,4},{12,8},{1,13},{5,1},{9,5},{13,9},{2,14},{6,2},{... | collective-permute-start | bytes 786440 | tf_op jit(solution)/shard_map/ppermute | solution.py:24
  107.2 51.3 %collective-permute-start.15 = (bf16[128,4096]{1,0:T(8,128)(2,1)S(1)}, bf16[128,4096]{1,0:T(8,128)(2,1)S(1)}, u32[]{:S(2)}, u32[]{:S(2)}) collective-permute-start(bf16[128,4096]{1,0:T(8,128)(2,1)S(1)} %constant_dynamic-update-slice_fusion.4.refs_0_), channel_id=1, source_target_pairs={{0,1},{1,2},{2,3},{3,0},{4,5},{5,6},{6,7},{7,4},{8,9},{9,10},{10,1... | collective-permute-start | bytes 3145736 | tf_op jit(solution)/shard_map/ppermute | solution.py:24
  107.8 54.6 %collective-permute-start.16 = (bf16[128,4096]{1,0:T(8,128)(2,1)S(1)}, bf16[128,4096]{1,0:T(8,128)(2,1)S(1)}, u32[]{:S(2)}, u32[]{:S(2)}) collective-permute-start(bf16[128,4096]{1,0:T(8,128)(2,1)S(1)} %constant_dynamic-update-slice_fusion.4.refs_0_), channel_id=1, source_target_pairs={{0,3},{1,0},{2,1},{3,2},{4,7},{5,4},{6,5},{7,6},{8,11},{9,8},{10,9... | collective-permute-start | bytes 3145736 | tf_op jit(solution)/shard_map/ppermute | solution.py:24
  117.4 37.6 %collective-permute-start.3 = (bf16[128,4096]{1,0:T(8,128)(2,1)S(1)}, bf16[128,4096]{1,0:T(8,128)(2,1)S(1)}, u32[]{:S(2)}, u32[]{:S(2)}) collective-permute-start(bf16[128,4096]{1,0:T(8,128)(2,1)S(1)} %constant_dynamic-update-slice_fusion.refs_0_), channel_id=1, source_target_pairs={{0,1},{1,2},{2,3},{3,0},{4,5},{5,6},{6,7},{7,4},{8,9},{9,10},{10,1... | collective-permute-start | bytes 3145736 | tf_op jit(solution)/shard_map/ppermute | solution.py:24
  118.0 37.1 %collective-permute-start.5 = (bf16[128,4096]{1,0:T(8,128)(2,1)S(1)}, bf16[128,4096]{1,0:T(8,128)(2,1)S(1)}, u32[]{:S(2)}, u32[]{:S(2)}) collective-permute-start(bf16[128,4096]{1,0:T(8,128)(2,1)S(1)} %constant_dynamic-update-slice_fusion.refs_0_), channel_id=1, source_target_pairs={{0,3},{1,0},{2,1},{3,2},{4,7},{5,4},{6,5},{7,6},{8,11},{9,8},{10,9... | collective-permute-start | bytes 3145736 | tf_op jit(solution)/shard_map/ppermute | solution.py:24
  155.0 16.1 %collective-permute-start.4 = (bf16[64,4096]{1,0:T(8,128)(2,1)S(1)}, bf16[64,4096]{1,0:T(8,128)(2,1)S(1)}, u32[]{:S(2)}, u32[]{:S(2)}) collective-permute-start(bf16[64,4096]{1,0:T(8,128)(2,1)S(1)} %slice.58), channel_id=1, source_target_pairs={{0,1},{1,2},{2,3},{3,0},{4,5},{5,6},{6,7},{7,4},{8,9},{9,10},{10,1... | collective-permute-start | bytes 1572872 | tf_op jit(solution)/shard_map/ppermute | solution.py:24
  155.2 17.5 %collective-permute-start.6 = (bf16[64,4096]{1,0:T(8,128)(2,1)S(1)}, bf16[64,4096]{1,0:T(8,128)(2,1)S(1)}, u32[]{:S(2)}, u32[]{:S(2)}) collective-permute-start(bf16[64,4096]{1,0:T(8,128)(2,1)S(1)} %slice.59), channel_id=1, source_target_pairs={{0,3},{1,0},{2,1},{3,2},{4,7},{5,4},{6,5},{7,6},{8,11},{9,8},{10,9... | collective-permute-start | bytes 1572872 | tf_op jit(solution)/shard_map/ppermute | solution.py:24
  158.5 32.3 %collective-permute-start.17 = (bf16[128,4096]{1,0:T(8,128)(2,1)S(1)}, bf16[128,4096]{1,0:T(8,128)(2,1)S(1)}, u32[]{:S(2)}, u32[]{:S(2)}) collective-permute-start(bf16[128,4096]{1,0:T(8,128)(2,1)S(1)} %collective-permute-done.15.refs_1_), channel_id=1, source_target_pairs={{0,1},{1,2},{2,3},{3,0},{4,5},{5,6},{6,7},{7,4},{8,9},{9,10},{10,1... | collective-permute-start | bytes 3145736 | tf_op jit(solution)/shard_map/ppermute | solution.py:24

commit v5 on v1

--- a/solution.py
+++ b/solution.py
@@ -80,18 +80,16 @@
     out_ref[...] = found.astype(BF16)
 
 
-def hess_kernel(places, near, other, dos_hbm, fac, inverse, proj, mat, dos, sem):
+def hess_kernel(places, *refs):
+    parts, (dos, fac, inverse, proj, mat) = refs[:-5], refs[-5:]
     k = mat.shape[0]
-    width = near.shape[2]
-    fetch = pltpu.make_async_copy(dos_hbm, dos, sem)
-    fetch.start()
-    for i in range(8):
-        fac[:, pl.ds(pl.multiple_of(places[i] * width, width), width)] = near[i]
-        fac[:, pl.ds(pl.multiple_of(places[8 + i] * width, width), width)] = other[i]
+    each, width = parts[0].shape[0], parts[0].shape[2]
+    for i, part in enumerate(parts):
+        for j in range(each):
+            fac[:, pl.ds(pl.multiple_of(places[each * i + j] * width, width), width)] = part[j]
     mat[...] = lax.dot_general(fac[...], fac[...], NT, preferred_element_type=F32) + ridge_sample * eye(k)
     sweep(mat)
     inverse[...] = -mat[...]
-    fetch.wait()
     total = jnp.dot(fac[...], dos[...], preferred_element_type=F32)
     high = total.astype(BF16)
     proj[:k, :] = high
@@ -162,7 +160,7 @@
 
     both = jnp.concatenate(
         [
-            lax.dot_general(loadings, flipped, TN, preferred_element_type=F32),
+            lax.dot_general(loadings, expression, (((0,), (1,)), ((), ())), preferred_element_type=F32),
             lax.dot_general(loadings, loadings, TN, preferred_element_type=F32),
         ],
         axis=1,
@@ -175,6 +173,7 @@
         out_shape=jax.ShapeDtypeStruct((k, samples), BF16),
         scratch_shapes=[pltpu.VMEM((k, k), F32)],
         cost_estimate=pl.CostEstimate(flops=7_000_000_000, bytes_accessed=400_000, transcendentals=0),
+        compiler_params=pltpu.CompilerParams(vmem_limit_bytes=8 << 20),
         name="factor",
     )(both.reshape(k, samples + k))
 
@@ -199,11 +198,11 @@
             scores[-1].append(jnp.dot(rows, dosage, preferred_element_type=F32))
 
     two = jnp.stack([factors, cycle(factors, "zh", 1)])
-    near = jnp.concatenate([two] + [cycle(two, "x", by) for by in (1, 2, 3)])
-    other = cycle(near, "core", 1)
+    four = jnp.concatenate([two, cycle(two, "core", 1)])
+    gathered = [four] + [cycle(four, "x", by) for by in (1, 2, 3)]
     back = jnp.arange(16)
-    from_core = (at["core"] - back // 8) % 2
-    from_x = (at["x"] - back // 2 % 4) % 4
+    from_core = (at["core"] - back // 2 % 2) % 2
+    from_x = (at["x"] - back // 4) % 4
     from_zh = (at["zh"] - back % 2) % 2
     order = (from_zh * 8 + from_x * 2 + from_core).astype(jnp.int32)
     fac, inverse, proj = pl.pallas_call(
@@ -215,19 +214,15 @@
         ),
         in_specs=[
             pl.BlockSpec(memory_space=pltpu.SMEM),
-            pl.BlockSpec(memory_space=pltpu.VMEM),
-            pl.BlockSpec(memory_space=pltpu.VMEM),
-            pl.BlockSpec(memory_space=pl.ANY),
+            *[pl.BlockSpec(memory_space=pltpu.VMEM)] * 5,
         ],
         scratch_shapes=[
             pltpu.VMEM((k, k), F32),
-            pltpu.VMEM(dosage.shape, BF16),
-            pltpu.SemaphoreType.DMA,
         ],
         cost_estimate=pl.CostEstimate(flops=9_000_000_000, bytes_accessed=10_000_000, transcendentals=0),
         compiler_params=pltpu.CompilerParams(vmem_limit_bytes=24 << 20),
         name="hess",
-    )(order, near, other, dosage)
+    )(order, *gathered, dosage)
 
     back_z = (at["zl"] - jnp.arange(4)) % 4
     back_y = (at["y"] - jnp.arange(4)) % 4

time: 198 us -> 191 us (0.965)
  the two profiles are of different devices: /device:TPU:64 before, /device:TPU:32 now
where the time goes in v5:
time: 191 us
  waiting for transfers between devices  87 us (46%)
  starting transfers between devices  52.1 us (27%)
  Pallas kernels  27.1 us (14%)
  matrix products  15.5 us (8%)
  local copies, waits for them, and re-layouts  7.45 us (4%)
    ppermute x19, waiting for transfers between devices, cycle(): lax.ppermute(array, axis, [(i, (i + by) % size) for i in range(size)])  73.3 us
    ppermute x19, starting transfers between devices, cycle(): lax.ppermute(array, axis, [(i, (i + by) % size) for i in range(size)])  30 us
    dot_general x10, matrix products, body(): scores[-1].append(jnp.dot(rows, dosage, preferred_element_type=F32))  13.8 us
    pallas_call x3, Pallas kernels, finish(): pl.pallas_call(functools.partial(finish_kernel, float(samples) ** (-0.5),...  10.2 us
    pallas_call x1, Pallas kernels, body(): pl.pallas_call(hess_kernel, out_shape=(jax.ShapeDtypeStruct((k, all_sampl...  9.53 us
    all_to_all x1, starting transfers between devices, body(): lax.all_to_all(both.reshape(n_cols, k // n_cols, samples + k), COLS, 0, 0...  8.65 us
    all_to_all x1, starting transfers between devices, body(): lax.all_to_all(flipped.reshape(n_samp, panel, samples), SAMP, 0, 0, tiled...  8.34 us
    all_to_all x1, waiting for transfers between devices, body(): lax.all_to_all(jnp.broadcast_to(both[None], (n_cols,) + both.shape), COLS...  7.77 us
  transfers between devices with their start and end apart: 22, of which 15 were waited for; matrix products, arithmetic and copies ran while one was open for 8% of the time, Pallas kernels for 9%

profile of v5, /device:TPU:32, one launch (start us, length us, event | category | flops | bytes accessed | tf_op | source)
XLA Modules:
  0.0 190.6 jit_solution(8324804851922125048)
XLA Ops:
  0.0 0.9 copy-done
  1.0 0.3 fusion.17
  1.2 1.4 fusion.16
  2.6 0.7 maximum_bitcast_fusion
  3.3 8.7 %all-to-all-start.1 = ((f32[16,8,384]{2,1,0:T(8,128)}), f32[16,8,384]{2,1,0:T(8,128)S(1)}, u32[]{:S(2)}, u32[]{:S(2)}) async-start(f32[16,8,384]{2,1,0:T(8,128)} %maximum_bitcast_fusion), calls=%async_computation.1 | async-start | bytes 393216 | tf_op jit(solution)/shard_map/all_to_all | solution.py:168
  11.9 2.0 %copy.8 = bf16[256,1024]{0,1:T(8,128)(2,1)} copy(bf16[256,1024]{1,0:T(8,128)(2,1)} %param.3) | data formatting | bytes 1048576 | tf_op args[0]
  14.0 5.9 %all-to-all-done.1 = f32[16,8,384]{2,1,0:T(8,128)S(1)} async-done(((f32[16,8,384]{2,1,0:T(8,128)}), f32[16,8,384]{2,1,0:T(8,128)S(1)}, u32[]{:S(2)}, u32[]{:S(2)}) %all-to-all-start.1) | async-done | bytes 196640 | tf_op jit(solution)/shard_map/all_to_all | solution.py:168
  20.0 0.7 broadcast_in_dim.2
  20.7 5.1 %all-to-all-start.2 = ((f32[16,8,384]{2,1,0:T(8,128)}), f32[16,8,384]{2,1,0:T(8,128)S(1)}, u32[]{:S(2)}, u32[]{:S(2)}) async-start(f32[16,8,384]{2,1,0:T(8,128)} %broadcast_in_dim.2), calls=%async_computation.2 | async-start | bytes 393216 | tf_op jit(solution)/shard_map/all_to_all | solution.py:170
  25.8 0.1 broadcast_add_fusion
  25.9 7.8 %all-to-all-done.2 = f32[16,8,384]{2,1,0:T(8,128)S(1)} async-done(((f32[16,8,384]{2,1,0:T(8,128)}), f32[16,8,384]{2,1,0:T(8,128)S(1)}, u32[]{:S(2)}, u32[]{:S(2)}) %all-to-all-start.2) | async-done | bytes 196640 | tf_op jit(solution)/shard_map/all_to_all | solution.py:170
  33.6 8.3 %all-to-all-start = ((bf16[16,64,256]{2,1,0:T(8,128)(2,1)}), bf16[16,64,256]{2,1,0:T(8,128)(2,1)S(1)}, u32[]{:S(2)}, u32[]{:S(2)}) async-start(bf16[16,64,256]{2,1,0:T(8,128)(2,1)} %bitcast.2), calls=%async_computation | async-start | bytes 1048576 | tf_op jit(solution)/shard_map/all_to_all | solution.py:158
  42.0 7.4 %factor.1 = bf16[128,256]{1,0:T(8,128)(2,1)S(1)} custom-call(f32[128,384]{1,0:T(8,128)S(1)} %bitcast.49), custom_call_target="tpu_custom_call" | custom-call | flops 7000000000 | bytes 400000 | tf_op jit(solution)/shard_map/factor/pallas_call | solution.py:171
  49.4 5.9 %collective-permute-start.7 = (bf16[128,256]{1,0:T(8,128)(2,1)S(1)}, bf16[128,256]{1,0:T(8,128)(2,1)S(1)}, u32[]{:S(2)}, u32[]{:S(2)}) collective-permute-start(bf16[128,256]{1,0:T(8,128)(2,1)S(1)} %factor.1), channel_id=1, source_target_pairs={{0,128},{128,0},{1,129},{129,1},{2,130},{130,2},{3,131},{131,3},{4... | collective-permute-start | bytes 196616 | tf_op jit(solution)/shard_map/ppermute | solution.py:24
  55.3 0.1 pad_add_fusion.places
  55.4 7.7 %collective-permute-done.7 = bf16[128,256]{1,0:T(8,128)(2,1)S(1)} collective-permute-done((bf16[128,256]{1,0:T(8,128)(2,1)S(1)}, bf16[128,256]{1,0:T(8,128)(2,1)S(1)}, u32[]{:S(2)}, u32[]{:S(2)}) %collective-permute-start.7) | collective-permute-done | bytes 65568 | tf_op jit(solution)/shard_map/ppermute | solution.py:24
  63.0 0.1 collective-permute-start.8
  63.1 0.1 pad_add_fusion.1.places
  63.2 1.2 collective-permute-done.8
  64.5 3.0 %collective-permute-start.10 = (bf16[4,128,256]{2,1,0:T(8,128)(2,1)S(1)}, bf16[4,128,256]{2,1,0:T(8,128)(2,1)S(1)}, u32[]{:S(2)}, u32[]{:S(2)}) collective-permute-start(bf16[4,128,256]{2,1,0:T(8,128)(2,1)S(1)} %pad_maximum_fusion.refs_0_), channel_id=1, source_target_pairs={{0,64},{32,96},{64,0},{96,32},{1,65},{33,97},{65,1},{97,33},{2,66}... | collective-permute-start | bytes 786440 | tf_op jit(solution)/shard_map/ppermute | solution.py:24
  67.5 1.2 collective-permute-start.11
  68.7 0.9 collective-permute-start.9
  69.5 0.0 all-to-all-done
  69.6 0.9 collective-permute-start.12
  70.5 1.7 collective-permute-start.13
  72.2 3.1 %collective-permute-done.10.refs_2_ = bf16[4,128,256]{2,1,0:T(8,128)(2,1)S(1)} collective-permute-done((bf16[4,128,256]{2,1,0:T(8,128)(2,1)S(1)}, bf16[4,128,256]{2,1,0:T(8,128)(2,1)S(1)}, u32[]{:S(2)}, u32[]{:S(2)}) %collective-permute-start.10) | collective-permute-done | bytes 262176 | tf_op jit(solution)/shard_map/ppermute | solution.py:24
  75.3 0.0 collective-permute-start.14
  75.3 4.8 %collective-permute-done.11.refs_3_ = bf16[4,128,256]{2,1,0:T(8,128)(2,1)S(1)} collective-permute-done((bf16[4,128,256]{2,1,0:T(8,128)(2,1)S(1)}, bf16[4,128,256]{2,1,0:T(8,128)(2,1)S(1)}, u32[]{:S(2)}, u32[]{:S(2)}) %collective-permute-start.11) | collective-permute-done | bytes 262176 | tf_op jit(solution)/shard_map/ppermute | solution.py:24
  80.0 0.8 collective-permute-start
  80.9 1.7 collective-permute-start.1
  82.5 3.4 %copy-done.1 = bf16[4096,1024]{1,0:T(8,128)(2,1)S(1)} copy-done((bf16[4096,1024]{1,0:T(8,128)(2,1)S(1)}, bf16[4096,1024]{1,0:T(8,128)(2,1)}, u32[]{:S(2)}) %copy-start.1) | copy-done | bytes 8388632
  85.9 9.5 %hess.1 = (bf16[128,4096]{1,0:T(8,128)(2,1)S(1)}, f32[128,128]{1,0:T(8,128)S(1)}, bf16[256,1024]{1,0:T(8,128)(2,1)S(1)}) custom-call(s32[16]{0:T(128)S(1)} %fusion.places, bf16[4,128,256]{2,1,0:T(8,128)(2,1)S(1)} %pad_maximum_fusion.refs_0_, bf16[4,128,256]{2,1,0:T(8,128)(2,1)S(1)} %collective-permute-done.9.refs_1_, ...), custom_call_target="tpu_custom_call" | custom-call | flops 8999999488 | bytes 10000000 | tf_op jit(solution)/shard_map/hess/pallas_call | solution.py:208
  95.5 0.3 collective-permute-start.2
  95.8 9.5 %collective-permute-done.13 = bf16[32,4096]{1,0:T(8,128)(2,1)S(1)} collective-permute-done((bf16[32,4096]{1,0:T(8,128)(2,1)S(1)}, bf16[32,4096]{1,0:T(8,128)(2,1)S(1)}, u32[]{:S(2)}, u32[]{:S(2)}) %collective-permute-start.13) | collective-permute-done | bytes 262176 | tf_op jit(solution)/shard_map/ppermute | solution.py:24
  105.4 0.5 collective-permute-done.14
  105.9 0.6 collective-permute-start.15
  106.5 2.7 %collective-permute-start.16 = (bf16[128,4096]{1,0:T(8,128)(2,1)S(1)}, bf16[128,4096]{1,0:T(8,128)(2,1)S(1)}, u32[]{:S(2)}, u32[]{:S(2)}) collective-permute-start(bf16[128,4096]{1,0:T(8,128)(2,1)S(1)} %constant_dynamic-update-slice_fusion.4.refs_0_), channel_id=1, source_target_pairs={{0,3},{1,0},{2,1},{3,2},{4,7},{5,4},{6,5},{7,6},{8,11},{9,8},{10,9... | collective-permute-start | bytes 3145736 | tf_op jit(solution)/shard_map/ppermute | solution.py:24
  109.2 1.8 collective-permute-done
  111.0 3.9 %collective-permute-done.1 = bf16[32,4096]{1,0:T(8,128)(2,1)S(1)} collective-permute-done((bf16[32,4096]{1,0:T(8,128)(2,1)S(1)}, bf16[32,4096]{1,0:T(8,128)(2,1)S(1)}, u32[]{:S(2)}, u32[]{:S(2)}) %collective-permute-start.1) | collective-permute-done | bytes 262176 | tf_op jit(solution)/shard_map/ppermute | solution.py:24
  114.9 2.0 %collective-permute-done.2 = bf16[32,4096]{1,0:T(8,128)(2,1)S(1)} collective-permute-done((bf16[32,4096]{1,0:T(8,128)(2,1)S(1)}, bf16[32,4096]{1,0:T(8,128)(2,1)S(1)}, u32[]{:S(2)}, u32[]{:S(2)}) %collective-permute-start.2) | collective-permute-done | bytes 262176 | tf_op jit(solution)/shard_map/ppermute | solution.py:24
  117.0 0.6 collective-permute-start.3
  117.7 2.7 %collective-permute-start.5 = (bf16[128,4096]{1,0:T(8,128)(2,1)S(1)}, bf16[128,4096]{1,0:T(8,128)(2,1)S(1)}, u32[]{:S(2)}, u32[]{:S(2)}) collective-permute-start(bf16[128,4096]{1,0:T(8,128)(2,1)S(1)} %constant_dynamic-update-slice_fusion.refs_0_), channel_id=1, source_target_pairs={{0,3},{1,0},{2,1},{3,2},{4,7},{5,4},{6,5},{7,6},{8,11},{9,8},{10,9... | collective-permute-start | bytes 3145736 | tf_op jit(solution)/shard_map/ppermute | solution.py:24
  120.3 1.3 fusion.21.refs_5_
  121.6 1.3 fusion.18.refs_3_
  122.9 10.3 %collective-permute-done.15.refs_1_ = bf16[128,4096]{1,0:T(8,128)(2,1)S(1)} collective-permute-done((bf16[128,4096]{1,0:T(8,128)(2,1)S(1)}, bf16[128,4096]{1,0:T(8,128)(2,1)S(1)}, u32[]{:S(2)}, u32[]{:S(2)}) %collective-permute-start.15) | collective-permute-done | bytes 1048608 | tf_op jit(solution)/shard_map/ppermute | solution.py:24
  133.2 0.1 collective-permute-start.17
  133.3 0.0 collective-permute-done.16.refs_2_
  133.4 3.3 %collective-permute-start.18 = (bf16[64,4096]{1,0:T(8,128)(2,1)S(1)}, bf16[64,4096]{1,0:T(8,128)(2,1)S(1)}, u32[]{:S(2)}, u32[]{:S(2)}) collective-permute-start(bf16[64,4096]{1,0:T(8,128)(2,1)S(1)} %slice.71), channel_id=1, source_target_pairs={{0,3},{1,0},{2,1},{3,2},{4,7},{5,4},{6,5},{7,6},{8,11},{9,8},{10,9... | collective-permute-start | bytes 1572872 | tf_op jit(solution)/shard_map/ppermute | solution.py:24
  136.7 19.0 %collective-permute-done.3.refs_1_ = bf16[128,4096]{1,0:T(8,128)(2,1)S(1)} collective-permute-done((bf16[128,4096]{1,0:T(8,128)(2,1)S(1)}, bf16[128,4096]{1,0:T(8,128)(2,1)S(1)}, u32[]{:S(2)}, u32[]{:S(2)}) %collective-permute-start.3) | collective-permute-done | bytes 1048608 | tf_op jit(solution)/shard_map/ppermute | solution.py:24
  155.7 0.1 collective-permute-start.4
  155.8 3.5 %collective-permute-start.6 = (bf16[64,4096]{1,0:T(8,128)(2,1)S(1)}, bf16[64,4096]{1,0:T(8,128)(2,1)S(1)}, u32[]{:S(2)}, u32[]{:S(2)}) collective-permute-start(bf16[64,4096]{1,0:T(8,128)(2,1)S(1)} %slice.68), channel_id=1, source_target_pairs={{0,3},{1,0},{2,1},{3,2},{4,7},{5,4},{6,5},{7,6},{8,11},{9,8},{10,9... | collective-permute-start | bytes 1572872 | tf_op jit(solution)/shard_map/ppermute | solution.py:24
  159.4 1.3 fusion.22.refs_6_
  160.6 1.3 fusion.23.refs_7_
  161.9 1.3 fusion.19.refs_4_
  163.1 1.3 fusion.20.refs_5_
  164.4 2.5 %collective-permute-done.17.refs_3_ = bf16[64,4096]{1,0:T(8,128)(2,1)S(1)} collective-permute-done((bf16[64,4096]{1,0:T(8,128)(2,1)S(1)}, bf16[64,4096]{1,0:T(8,128)(2,1)S(1)}, u32[]{:S(2)}, u32[]{:S(2)}) %collective-permute-start.17) | collective-permute-done | bytes 524320 | tf_op jit(solution)/shard_map/ppermute | solution.py:24
  166.9 1.6 fusion.24.refs_8_
  168.5 1.6 fusion.25.refs_9_
  170.1 7.0 %collective-permute-done.4.refs_0_ = bf16[64,4096]{1,0:T(8,128)(2,1)S(1)} collective-permute-done((bf16[64,4096]{1,0:T(8,128)(2,1)S(1)}, bf16[64,4096]{1,0:T(8,128)(2,1)S(1)}, u32[]{:S(2)}, u32[]{:S(2)}) %collective-permute-start.4) | collective-permute-done | bytes 524320 | tf_op jit(solution)/shard_map/ppermute | solution.py:24
  177.1 1.6 fusion.14.refs_2_
  178.7 1.6 fusion.15.refs_3_
  180.3 4.2 %shard_map.37.refs_9_ = bf16[16,1,64,1024]{3,2,1,0:T(8,128)(2,1)} custom-call(s32[16]{0:T(128)S(1)} %pad_add_fusion.1.places, bf16[128,4096]{1,0:T(8,128)(2,1)S(1)} %constant_dynamic-update-slice_fusion.4.refs_0_, bf16[128,4096]{1,0:T(8,128)(2,1)S(1)} %collective-permute-done.15.refs_1_, bf16[128,4096]{1,0:T(8,128)(2,1)S(1)} %collective-permute-done.16.refs_2_, ...), custom_call_target="tpu_custom_call" | custom-call | flops 1073741824 | bytes 8388608 | tf_op jit(solution)/shard_map/pallas_call | solution.py:133
  184.5 3.4 %shard_map.38.refs_7_ = bf16[16,1,64,1024]{3,2,1,0:T(8,128)(2,1)} custom-call(s32[12]{0:T(128)S(1)} %pad_add_fusion.places, bf16[128,4096]{1,0:T(8,128)(2,1)S(1)} %constant_dynamic-update-slice_fusion.refs_0_, bf16[128,4096]{1,0:T(8,128)(2,1)S(1)} %collective-permute-done.3.refs_1_, ...), custom_call_target="tpu_custom_call", output_to_operand_aliasing={{}: (10, {})} | custom-call | flops 805306368 | bytes 6291456 | tf_op jit(solution)/shard_map/pallas_call | solution.py:133
  187.9 2.6 %shard_map.39 = bf16[16,1,64,1024]{3,2,1,0:T(8,128)(2,1)} custom-call(s32[4]{0:T(128)S(1)} %get-tuple-element.16.places, bf16[64,4096]{1,0:T(8,128)(2,1)S(1)} %collective-permute-done.4.refs_0_, bf16[64,4096]{1,0:T(8,128)(2,1)S(1)} %collective-permute-done.6.refs_1_, f32[64,1024]{1,0:T(8,128)S(1)} %fusion.14.refs_2_, ...), custom_call_target="tpu_custom_call", output_to_operand_aliasing={{}: (8, {})} | custom-call | flops 268435456 | bytes 2097152 | tf_op jit(solution)/shard_map/pallas_call | solution.py:133
  (28 shorter events, 0.5 us)
Async XLA Ops:
  0.0 1.0 copy-start
  3.3 16.6 %all-to-all-start.1 = ((f32[16,8,384]{2,1,0:T(8,128)}), f32[16,8,384]{2,1,0:T(8,128)S(1)}, u32[]{:S(2)}, u32[]{:S(2)}) async-start(f32[16,8,384]{2,1,0:T(8,128)} %maximum_bitcast_fusion), calls=%async_computation.1 | async-start | bytes 393216 | tf_op jit(solution)/shard_map/all_to_all | solution.py:168
  20.7 13.0 %all-to-all-start.2 = ((f32[16,8,384]{2,1,0:T(8,128)}), f32[16,8,384]{2,1,0:T(8,128)S(1)}, u32[]{:S(2)}, u32[]{:S(2)}) async-start(f32[16,8,384]{2,1,0:T(8,128)} %broadcast_in_dim.2), calls=%async_computation.2 | async-start | bytes 393216 | tf_op jit(solution)/shard_map/all_to_all | solution.py:170
  33.6 35.9 %all-to-all-start = ((bf16[16,64,256]{2,1,0:T(8,128)(2,1)}), bf16[16,64,256]{2,1,0:T(8,128)(2,1)S(1)}, u32[]{:S(2)}, u32[]{:S(2)}) async-start(bf16[16,64,256]{2,1,0:T(8,128)(2,1)} %bitcast.2), calls=%async_computation | async-start | bytes 1048576 | tf_op jit(solution)/shard_map/all_to_all | solution.py:158
  49.4 13.7 %collective-permute-start.7 = (bf16[128,256]{1,0:T(8,128)(2,1)S(1)}, bf16[128,256]{1,0:T(8,128)(2,1)S(1)}, u32[]{:S(2)}, u32[]{:S(2)}) collective-permute-start(bf16[128,256]{1,0:T(8,128)(2,1)S(1)} %factor.1), channel_id=1, source_target_pairs={{0,128},{128,0},{1,129},{129,1},{2,130},{130,2},{3,131},{131,3},{4... | collective-permute-start | bytes 196616 | tf_op jit(solution)/shard_map/ppermute | solution.py:24
  63.0 1.4 collective-permute-start.8
  64.5 10.8 %collective-permute-start.10 = (bf16[4,128,256]{2,1,0:T(8,128)(2,1)S(1)}, bf16[4,128,256]{2,1,0:T(8,128)(2,1)S(1)}, u32[]{:S(2)}, u32[]{:S(2)}) collective-permute-start(bf16[4,128,256]{2,1,0:T(8,128)(2,1)S(1)} %pad_maximum_fusion.refs_0_), channel_id=1, source_target_pairs={{0,64},{32,96},{64,0},{96,32},{1,65},{33,97},{65,1},{97,33},{2,66}... | collective-permute-start | bytes 786440 | tf_op jit(solution)/shard_map/ppermute | solution.py:24
  67.5 12.6 %collective-permute-start.11 = (bf16[4,128,256]{2,1,0:T(8,128)(2,1)S(1)}, bf16[4,128,256]{2,1,0:T(8,128)(2,1)S(1)}, u32[]{:S(2)}, u32[]{:S(2)}) collective-permute-start(bf16[4,128,256]{2,1,0:T(8,128)(2,1)S(1)} %pad_maximum_fusion.refs_0_), channel_id=1, source_target_pairs={{0,96},{32,0},{64,32},{96,64},{1,97},{33,1},{65,33},{97,65},{2,98}... | collective-permute-start | bytes 786440 | tf_op jit(solution)/shard_map/ppermute | solution.py:24
  68.7 12.2 %collective-permute-start.9 = (bf16[4,128,256]{2,1,0:T(8,128)(2,1)S(1)}, bf16[4,128,256]{2,1,0:T(8,128)(2,1)S(1)}, u32[]{:S(2)}, u32[]{:S(2)}) collective-permute-start(bf16[4,128,256]{2,1,0:T(8,128)(2,1)S(1)} %pad_maximum_fusion.refs_0_), channel_id=1, source_target_pairs={{0,32},{32,64},{64,96},{96,0},{1,33},{33,65},{65,97},{97,1},{2,34}... | collective-permute-start | bytes 786440 | tf_op jit(solution)/shard_map/ppermute | solution.py:24
  69.6 25.8 %collective-permute-start.12 = (bf16[32,4096]{1,0:T(8,128)(2,1)S(1)}, bf16[32,4096]{1,0:T(8,128)(2,1)S(1)}, u32[]{:S(2)}, u32[]{:S(2)}) collective-permute-start(bf16[32,4096]{1,0:T(8,128)(2,1)S(1)} %bitcast.56), channel_id=1, source_target_pairs={{0,4},{4,8},{8,12},{12,0},{1,5},{5,9},{9,13},{13,1},{2,6},{6,10},{... | collective-permute-start | bytes 786440 | tf_op jit(solution)/shard_map/ppermute | solution.py:24
  70.5 34.8 %collective-permute-start.13 = (bf16[32,4096]{1,0:T(8,128)(2,1)S(1)}, bf16[32,4096]{1,0:T(8,128)(2,1)S(1)}, u32[]{:S(2)}, u32[]{:S(2)}) collective-permute-start(bf16[32,4096]{1,0:T(8,128)(2,1)S(1)} %bitcast.57), channel_id=1, source_target_pairs={{0,8},{4,12},{8,0},{12,4},{1,9},{5,13},{9,1},{13,5},{2,10},{6,14},... | collective-permute-start | bytes 786440 | tf_op jit(solution)/shard_map/ppermute | solution.py:24
  75.3 30.6 %collective-permute-start.14 = (bf16[32,4096]{1,0:T(8,128)(2,1)S(1)}, bf16[32,4096]{1,0:T(8,128)(2,1)S(1)}, u32[]{:S(2)}, u32[]{:S(2)}) collective-permute-start(bf16[32,4096]{1,0:T(8,128)(2,1)S(1)} %bitcast.58), channel_id=1, source_target_pairs={{0,12},{4,0},{8,4},{12,8},{1,13},{5,1},{9,5},{13,9},{2,14},{6,2},{... | collective-permute-start | bytes 786440 | tf_op jit(solution)/shard_map/ppermute | solution.py:24
  80.0 30.9 %collective-permute-start = (bf16[32,4096]{1,0:T(8,128)(2,1)S(1)}, bf16[32,4096]{1,0:T(8,128)(2,1)S(1)}, u32[]{:S(2)}, u32[]{:S(2)}) collective-permute-start(bf16[32,4096]{1,0:T(8,128)(2,1)S(1)} %bitcast.52), channel_id=1, source_target_pairs={{0,4},{4,8},{8,12},{12,0},{1,5},{5,9},{9,13},{13,1},{2,6},{6,10},{... | collective-permute-start | bytes 786440 | tf_op jit(solution)/shard_map/ppermute | solution.py:24
  80.9 34.0 %collective-permute-start.1 = (bf16[32,4096]{1,0:T(8,128)(2,1)S(1)}, bf16[32,4096]{1,0:T(8,128)(2,1)S(1)}, u32[]{:S(2)}, u32[]{:S(2)}) collective-permute-start(bf16[32,4096]{1,0:T(8,128)(2,1)S(1)} %bitcast.53), channel_id=1, source_target_pairs={{0,8},{4,12},{8,0},{12,4},{1,9},{5,13},{9,1},{13,5},{2,10},{6,14},... | collective-permute-start | bytes 786440 | tf_op jit(solution)/shard_map/ppermute | solution.py:24
  82.5 3.4 %copy-start.1 = (bf16[4096,1024]{1,0:T(8,128)(2,1)S(1)}, bf16[4096,1024]{1,0:T(8,128)(2,1)}, u32[]{:S(2)}) copy-start(bf16[4096,1024]{1,0:T(8,128)(2,1)} %refs_4_.1) | copy-start | bytes 25165828
  95.5 21.5 %collective-permute-start.2 = (bf16[32,4096]{1,0:T(8,128)(2,1)S(1)}, bf16[32,4096]{1,0:T(8,128)(2,1)S(1)}, u32[]{:S(2)}, u32[]{:S(2)}) collective-permute-start(bf16[32,4096]{1,0:T(8,128)(2,1)S(1)} %bitcast.54), channel_id=1, source_target_pairs={{0,12},{4,0},{8,4},{12,8},{1,13},{5,1},{9,5},{13,9},{2,14},{6,2},{... | collective-permute-start | bytes 786440 | tf_op jit(solution)/shard_map/ppermute | solution.py:24
  105.9 27.3 %collective-permute-start.15 = (bf16[128,4096]{1,0:T(8,128)(2,1)S(1)}, bf16[128,4096]{1,0:T(8,128)(2,1)S(1)}, u32[]{:S(2)}, u32[]{:S(2)}) collective-permute-start(bf16[128,4096]{1,0:T(8,128)(2,1)S(1)} %constant_dynamic-update-slice_fusion.4.refs_0_), channel_id=1, source_target_pairs={{0,1},{1,2},{2,3},{3,0},{4,5},{5,6},{6,7},{7,4},{8,9},{9,10},{10,1... | collective-permute-start | bytes 3145736 | tf_op jit(solution)/shard_map/ppermute | solution.py:24
  106.5 26.8 %collective-permute-start.16 = (bf16[128,4096]{1,0:T(8,128)(2,1)S(1)}, bf16[128,4096]{1,0:T(8,128)(2,1)S(1)}, u32[]{:S(2)}, u32[]{:S(2)}) collective-permute-start(bf16[128,4096]{1,0:T(8,128)(2,1)S(1)} %constant_dynamic-update-slice_fusion.4.refs_0_), channel_id=1, source_target_pairs={{0,3},{1,0},{2,1},{3,2},{4,7},{5,4},{6,5},{7,6},{8,11},{9,8},{10,9... | collective-permute-start | bytes 3145736 | tf_op jit(solution)/shard_map/ppermute | solution.py:24
  117.0 38.6 %collective-permute-start.3 = (bf16[128,4096]{1,0:T(8,128)(2,1)S(1)}, bf16[128,4096]{1,0:T(8,128)(2,1)S(1)}, u32[]{:S(2)}, u32[]{:S(2)}) collective-permute-start(bf16[128,4096]{1,0:T(8,128)(2,1)S(1)} %constant_dynamic-update-slice_fusion.refs_0_), channel_id=1, source_target_pairs={{0,1},{1,2},{2,3},{3,0},{4,5},{5,6},{6,7},{7,4},{8,9},{9,10},{10,1... | collective-permute-start | bytes 3145736 | tf_op jit(solution)/shard_map/ppermute | solution.py:24
  117.7 38.1 %collective-permute-start.5 = (bf16[128,4096]{1,0:T(8,128)(2,1)S(1)}, bf16[128,4096]{1,0:T(8,128)(2,1)S(1)}, u32[]{:S(2)}, u32[]{:S(2)}) collective-permute-start(bf16[128,4096]{1,0:T(8,128)(2,1)S(1)} %constant_dynamic-update-slice_fusion.refs_0_), channel_id=1, source_target_pairs={{0,3},{1,0},{2,1},{3,2},{4,7},{5,4},{6,5},{7,6},{8,11},{9,8},{10,9... | collective-permute-start | bytes 3145736 | tf_op jit(solution)/shard_map/ppermute | solution.py:24
  133.2 33.7 %collective-permute-start.17 = (bf16[64,4096]{1,0:T(8,128)(2,1)S(1)}, bf16[64,4096]{1,0:T(8,128)(2,1)S(1)}, u32[]{:S(2)}, u32[]{:S(2)}) collective-permute-start(bf16[64,4096]{1,0:T(8,128)(2,1)S(1)} %slice.70), channel_id=1, source_target_pairs={{0,1},{1,2},{2,3},{3,0},{4,5},{5,6},{6,7},{7,4},{8,9},{9,10},{10,1... | collective-permute-start | bytes 1572872 | tf_op jit(solution)/shard_map/ppermute | solution.py:24
  133.4 35.1 %collective-permute-start.18 = (bf16[64,4096]{1,0:T(8,128)(2,1)S(1)}, bf16[64,4096]{1,0:T(8,128)(2,1)S(1)}, u32[]{:S(2)}, u32[]{:S(2)}) collective-permute-start(bf16[64,4096]{1,0:T(8,128)(2,1)S(1)} %slice.71), channel_id=1, source_target_pairs={{0,3},{1,0},{2,1},{3,2},{4,7},{5,4},{6,5},{7,6},{8,11},{9,8},{10,9... | collective-permute-start | bytes 1572872 | tf_op jit(solution)/shard_map/ppermute | solution.py:24
  155.7 21.4 %collective-permute-start.4 = (bf16[64,4096]{1,0:T(8,128)(2,1)S(1)}, bf16[64,4096]{1,0:T(8,128)(2,1)S(1)}, u32[]{:S(2)}, u32[]{:S(2)}) collective-permute-start(bf16[64,4096]{1,0:T(8,128)(2,1)S(1)} %slice.67), channel_id=1, source_target_pairs={{0,1},{1,2},{2,3},{3,0},{4,5},{5,6},{6,7},{7,4},{8,9},{9,10},{10,1... | collective-permute-start | bytes 1572872 | tf_op jit(solution)/shard_map/ppermute | solution.py:24
  155.8 22.8 %collective-permute-start.6 = (bf16[64,4096]{1,0:T(8,128)(2,1)S(1)}, bf16[64,4096]{1,0:T(8,128)(2,1)S(1)}, u32[]{:S(2)}, u32[]{:S(2)}) collective-permute-start(bf16[64,4096]{1,0:T(8,128)(2,1)S(1)} %slice.68), channel_id=1, source_target_pairs={{0,3},{1,0},{2,1},{3,2},{4,7},{5,4},{6,5},{7,6},{8,11},{9,8},{10,9... | collective-permute-start | bytes 1572872 | tf_op jit(solution)/shard_map/ppermute | solution.py:24
